TPU v7x, 256 devices: a whole 4x4x8 slice. The times are simulated.
256 devices in a mesh: seq: 64 (over y_lo, x, z), head: 4 (over y_hi, core).
Axes of the slice: x: 4, y: 4 (y_hi: 2, y_lo: 2; y = y_hi * 2 + y_lo), z: 8, core: 2. Of those that a mesh axis runs over, the one named last changes fastest.
Arguments:
- linear_query_rows: bfloat16 [8192, 64, 128], P('seq', 'head'), may hold values from -6 to 6
- lin_keys: bfloat16 [8192, 64, 128], P('seq', 'head'), may hold values from -0.5 to 0.5
- linear_value_rows: bfloat16 [8192, 64, 128], P('seq', 'head'), may hold values from -6 to 6
- log_decay: float32 [64, 8192], P('head', 'seq'), may hold values from -1 to 0, as said below
- norm_gain: bfloat16 [64, 128], P('head'), may hold values from 0.5 to 1.5
- soft_queries: bfloat16 [8192, 64, 128], P('seq', 'head'), may hold values from -200 to 200
- soft_keys: bfloat16 [8192, 8, 128], P('seq', 'head'), may hold values from -5 to 5
- soft_values: bfloat16 [8192, 8, 128], P('seq', 'head'), may hold values from -6 to 6
- window_start: int32 [64], P('seq'), may hold values from 0 to 62, as said below
Outputs:
- lin_out: bfloat16 [8192, 64, 128], P('seq', 'head')
- soft_out: bfloat16 [8192, 64, 128], P('seq', 'head')
Inputs may be any that keep to these rules, and one draw needn't show every extreme that they name: window_start[b] lies between b - 3 and b and is never negative; the last block's entry is 60 and the next-to-last block's entry is 62. `log_decay`: decay logarithms are negative.
All inputs are finite; a program needn't handle non-finite values.
Results may differ from a plain program's by a relative error of at most 0.013.
Values may be sent and summed in bfloat16 or wider, within the bound.
A program may use at most 192 MiB of HBM per device.

v0:
```python
import jax
import jax.numpy as jnp
from jax import lax
from jax.sharding import PartitionSpec as P

DH = 128
HEADS = 64
REACH = 3


def prefix(shard, axis, combine, identity):
    length, here = (lax.axis_size(axis), lax.axis_index(axis))
    everything = jax.tree.map(lambda part: lax.all_gather(part, axis), shard)
    start = jax.tree.map(
        lambda part, zero: jnp.broadcast_to(jnp.asarray(zero, part.dtype), part.shape),
        shard,
        identity,
    )

    def hop(k, before):
        reached = k < here
        new = combine(before, jax.tree.map(lambda part: part[k], everything))
        return jax.tree.map(lambda a, b: jnp.where(reached, a, b), new, before)

    return lax.fori_loop(0, length, hop, start)


def from_behind(value, axis, steps):
    count = lax.axis_size(axis)
    first, last = (max(0, -steps), min(count, count - steps))
    return lax.ppermute(value, axis, [(source, source + steps) for source in range(first, last)])


def combine_states(earlier, later):
    return (earlier[0] * later[0], later[0][:, None, None] * earlier[1] + later[1])


def split_parts(matrix):
    upper = matrix.astype(jnp.bfloat16)
    lower = (matrix - upper.astype(jnp.float32)).astype(jnp.bfloat16)
    return (upper, lower)


def attend(carried_over_state, query_rows, key_rows, value_rows, visible, score_scale):
    running_max, running_sum, accumulated = carried_over_state
    attention_logits = (
        jnp.einsum("cphm,npm->phcn", query_rows, key_rows, preferred_element_type=jnp.float32)
        * score_scale
    )
    masked = jnp.where(visible, attention_logits, -jnp.inf)
    new_max = jnp.maximum(running_max, jnp.max(masked, axis=-1))
    power_exponent = jnp.exp(masked - new_max[..., None])
    fading = jnp.exp(running_max - new_max)
    new_sum = running_sum * fading + jnp.sum(power_exponent, axis=-1)
    product = jnp.einsum(
        "qyjl,lqu->qyju",
        power_exponent.astype(jnp.bfloat16),
        value_rows,
        preferred_element_type=jnp.float32,
    )
    return (new_max, new_sum, accumulated * fading[..., None] + product)


def body(
    linear_query_rows,
    lin_keys,
    linear_value_rows,
    log_decay,
    norm_gain,
    soft_queries,
    soft_keys,
    soft_values,
    window_start,
):
    row_count, heads_here, head_width = linear_query_rows.shape
    cumulated = jnp.cumsum(log_decay, axis=1)
    token_locations = jnp.arange(row_count, dtype=jnp.int32)
    lower_mask = token_locations[:, None] >= token_locations[None, :]
    tail = jnp.exp(cumulated[:, -1:] - cumulated)
    key_product = lin_keys.astype(jnp.float32) * tail.T[:, :, None]
    key_product_upper, key_product_lower = split_parts(key_product)
    recurrent_state = jnp.einsum(
        "egz,egc->gzc", key_product_upper, linear_value_rows, preferred_element_type=jnp.float32
    )
    recurrent_state = recurrent_state + jnp.einsum(
        "egz,egc->gzc", key_product_lower, linear_value_rows, preferred_element_type=jnp.float32
    )
    falling = jnp.exp(cumulated[:, -1])
    identity = (jnp.ones_like(falling), jnp.zeros_like(recurrent_state))
    preceding_state = prefix((falling, recurrent_state), "seq", combine_states, identity)[1]
    lin_scores = jnp.einsum(
        "thd,shd->hts", linear_query_rows, lin_keys, preferred_element_type=jnp.float32
    )
    gap = jnp.where(lower_mask[None], cumulated[:, :, None] - cumulated[:, None, :], -jnp.inf)
    lin_weights = (lin_scores * jnp.exp(gap)).astype(jnp.bfloat16)
    local_part = jnp.einsum(
        "hts,shd->thd", lin_weights, linear_value_rows, preferred_element_type=jnp.float32
    )
    preceding_upper, preceding_lower = split_parts(preceding_state)
    carried_part = jnp.einsum(
        "nwg,wgq->nwq", linear_query_rows, preceding_upper, preferred_element_type=jnp.float32
    )
    carried_part = carried_part + jnp.einsum(
        "nwg,wgq->nwq", linear_query_rows, preceding_lower, preferred_element_type=jnp.float32
    )
    mixed = local_part + jnp.exp(cumulated).T[:, :, None] * carried_part
    squares = lax.psum(jnp.sum(mixed * mixed, axis=(1, 2)), "head")
    lin_out = (
        mixed
        * lax.rsqrt(squares / (HEADS * DH) + 1e-06)[:, None, None]
        * norm_gain.astype(jnp.float32)
    ).astype(jnp.bfloat16)
    kv_here = soft_keys.shape[1]
    group = heads_here // kv_here
    score_scale = float(head_width) ** (-0.5)
    query_rows = soft_queries.reshape(row_count, kv_here, group, head_width)
    block_index = lax.axis_index("seq")
    first_block = window_start[0]
    carried_over_state = (
        jnp.full((kv_here, group, row_count), -jnp.inf, jnp.float32),
        jnp.zeros((kv_here, group, row_count), jnp.float32),
        jnp.zeros((kv_here, group, row_count, head_width), jnp.float32),
    )
    carried_over_state = attend(
        carried_over_state, query_rows, soft_keys, soft_values, lower_mask, score_scale
    )
    current = (soft_keys, soft_values)
    for step_back in range(1, REACH + 1):
        current = from_behind((current[0], current[1]), "seq", 1)
        carried_over_state = attend(
            carried_over_state,
            query_rows,
            current[0],
            current[1],
            block_index - step_back >= first_block,
            score_scale,
        )
    final_output = carried_over_state[2] / carried_over_state[1][..., None]
    soft_out = (
        final_output.transpose(2, 0, 1, 3)
        .reshape(row_count, heads_here, head_width)
        .astype(jnp.bfloat16)
    )
    return (lin_out, soft_out)


def solution(mesh):
    placed = (
        P("seq", "head", None),
        P("seq", "head", None),
        P("seq", "head", None),
        P("head", "seq"),
        P("head", None),
        P("seq", "head", None),
        P("seq", "head", None),
        P("seq", "head", None),
        P("seq"),
    )
    return jax.shard_map(
        body,
        mesh=mesh,
        in_specs=placed,
        out_specs=(P("seq", "head", None), P("seq", "head", None)),
        check_vma=False,
    )
```

profile of v0, /device:TPU:60, one launch (start us, length us, event | category | flops | bytes accessed | tf_op | source)
XLA Modules:
  0.0 863.6 jit_solution(2371309144066334184)
XLA Ops:
  11.4 2.4 convolution_add_fusion.1
  14.7 3.8 collective-permute-start
  19.4 3.8 collective-permute-start.1
  24.5 3.2 convolution_bitcast_fusion.4
  30.8 125.1 %all-reduce = f32[1024]{0:T(1024)S(1)} all-reduce(f32[1024]{0:T(1024)S(1)} %dynamic-update-slice), channel_id=2, replica_groups=mesh['seq'=64,'head'=4] {'seq'}, use_global_device_ids=true, to_apply=%add | all-reduce | flops 1024 | bytes 8192
  156.6 5.2 collective-permute-start.2
  162.1 4.9 collective-permute-start.3
  167.0 5.5 collective-permute-start.4
  172.8 4.6 collective-permute-start.5
  178.4 1.8 fusion.5
  183.2 564.3 %all-gather.4.cloned.1.call-done = f32[1024,128,128]{2,1,0:T(8,128)} async-done(((f32[16,128,128]{2,1,0:T(8,128)}), f32[1024,128,128]{2,1,0:T(8,128)}) %all-gather.4.cloned.1.call-update) | async-done | bytes 67108880 | tf_op jit(solution)/shard_map/all_gather | solution.py:13
  747.5 95.9 %while.14 = (s32[]{:T(128)}, f32[16,128,128]{2,1,0:T(8,128)S(1)}, s32[]{:T(128)}, f32[64,16]{1,0:T(8,128)S(1)}, f32[64,16,128,128]{3,2,1,0:T(8,128)}, /*index=5*/s32[]{:T(128)}, s32[]{:T(128)}) while((s32[]{:T(128)}, f32[16,128,128]{2,1,0:T(8,128)S(1)}, s32[]{:T(128)}, f32[64,16]{1,0:T(8,128)S(1)}, f32[64,16,128,128]{3,2,1,0:T(8,128)}, ...), condition=%wide.region_2.3_spmd.clone, body=%wide.region_1.2_spmd.clone.sunk | while | flops 1048580 | bytes 3146025 | solution.py:25
  749.0 1.5 fusion.89
  750.5 1.5 fusion.89
  753.5 1.5 fusion.89
  755.0 1.5 fusion.89
  756.5 1.5 fusion.89
  758.0 1.5 fusion.89
  761.0 1.5 fusion.89
  762.5 1.5 fusion.89
  765.5 1.5 fusion.89
  767.0 1.5 fusion.89
  770.0 1.5 fusion.89
  771.5 1.5 fusion.89
  773.0 1.5 fusion.89
  774.5 1.5 fusion.89
  777.5 1.5 fusion.89
  779.0 1.5 fusion.89
  782.0 1.5 fusion.89
  843.4 1.6 fusion.55
  845.0 1.9 multiply_reduce_fusion
  846.9 8.3 psum.7
  (153 shorter events, 84.9 us)
Async XLA Ops:
  7.2 16.2 %copy-start = (bf16[128,16,128]{2,1,0:T(8,128)(2,1)S(1)}, bf16[128,16,128]{2,1,0:T(8,128)(2,1)}, u32[]{:S(2)}) copy-start(bf16[128,16,128]{2,1,0:T(8,128)(2,1)} %param.16) | copy-start | bytes 1572868
  7.2 740.3 %all-gather.4.cloned.1.call-start = ((), (), s32[]{:S(2)}) async-start(), calls=%async_computation | async-start | bytes 68157440 | tf_op jit(solution)/shard_map/all_gather | solution.py:13
  14.7 141.9 %collective-permute-start = (bf16[128,2,128]{2,0,1:T(8,128)(2,1)S(1)}, bf16[128,2,128]{2,0,1:T(8,128)(2,1)S(1)}, u32[]{:S(2)}, u32[]{:S(2)}) collective-permute-start(bf16[128,2,128]{2,0,1:T(8,128)(2,1)S(1)} %copy.78), channel_id=1, source_target_pairs={{0,4},{4,8},{8,12},{12,16},{16,20},{20,24},{24,28},{28,32},{32,36}... | collective-permute-start | bytes 196616 | tf_op jit(solution)/shard_map/ppermute | solution.py:31
  19.4 142.7 %collective-permute-start.1 = (bf16[128,2,128]{2,0,1:T(8,128)(2,1)S(1)}, bf16[128,2,128]{2,0,1:T(8,128)(2,1)S(1)}, u32[]{:S(2)}, u32[]{:S(2)}) collective-permute-start(bf16[128,2,128]{2,0,1:T(8,128)(2,1)S(1)} %copy.80), channel_id=1, source_target_pairs={{0,4},{4,8},{8,12},{12,16},{16,20},{20,24},{24,28},{28,32},{32,36}... | collective-permute-start | bytes 196616 | tf_op jit(solution)/shard_map/ppermute | solution.py:31
  156.6 10.4 %collective-permute-start.2 = (bf16[128,2,128]{2,0,1:T(8,128)(2,1)S(1)}, bf16[128,2,128]{2,0,1:T(8,128)(2,1)S(1)}, u32[]{:S(2)}, u32[]{:S(2)}) collective-permute-start(bf16[128,2,128]{2,0,1:T(8,128)(2,1)S(1)} %collective-permute-done), channel_id=1, source_target_pairs={{0,4},{4,8},{8,12},{12,16},{16,20},{20,24},{24,28},{28,32},{32,36}... | collective-permute-start | bytes 196616 | tf_op jit(solution)/shard_map/ppermute | solution.py:31
  162.1 10.7 %collective-permute-start.3 = (bf16[128,2,128]{2,0,1:T(8,128)(2,1)S(1)}, bf16[128,2,128]{2,0,1:T(8,128)(2,1)S(1)}, u32[]{:S(2)}, u32[]{:S(2)}) collective-permute-start(bf16[128,2,128]{2,0,1:T(8,128)(2,1)S(1)} %collective-permute-done.1), channel_id=1, source_target_pairs={{0,4},{4,8},{8,12},{12,16},{16,20},{20,24},{24,28},{28,32},{32,36}... | collective-permute-start | bytes 196616 | tf_op jit(solution)/shard_map/ppermute | solution.py:31
  167.0 10.4 %collective-permute-start.4 = (bf16[128,2,128]{2,0,1:T(8,128)(2,1)S(1)}, bf16[128,2,128]{2,0,1:T(8,128)(2,1)S(1)}, u32[]{:S(2)}, u32[]{:S(2)}) collective-permute-start(bf16[128,2,128]{2,0,1:T(8,128)(2,1)S(1)} %collective-permute-done.2), channel_id=1, source_target_pairs={{0,4},{4,8},{8,12},{12,16},{16,20},{20,24},{24,28},{28,32},{32,36}... | collective-permute-start | bytes 196616 | tf_op jit(solution)/shard_map/ppermute | solution.py:31
  172.8 8.7 %collective-permute-start.5 = (bf16[128,2,128]{2,0,1:T(8,128)(2,1)S(1)}, bf16[128,2,128]{2,0,1:T(8,128)(2,1)S(1)}, u32[]{:S(2)}, u32[]{:S(2)}) collective-permute-start(bf16[128,2,128]{2,0,1:T(8,128)(2,1)S(1)} %collective-permute-done.3), channel_id=1, source_target_pairs={{0,4},{4,8},{8,12},{12,16},{16,20},{20,24},{24,28},{28,32},{32,36}... | collective-permute-start | bytes 196616 | tf_op jit(solution)/shard_map/ppermute | solution.py:31
Sparse Core Ops, SparseCore 0:
  14.0 733.4 all-gather.3
where the time goes:
time: 873 us; the launch traced here: 864 us
  waiting for transfers between devices  564 us (65%)
  blocking collectives  133 us (15%)
  other arithmetic  97.6 us (11%)
  starting transfers between devices  27.8 us (3%)
  matrix products  16.2 us (2%)
  between operations  15.6 us (2%)
    all_gather x1, waiting for transfers between devices, prefix(): everything = jax.tree.map(lambda part: lax.all_gather(part, axis), shard)  564 us
    unnamed x1, blocking collectives  125 us
    select_n x64, other arithmetic, hop(): return jax.tree.map(lambda a, b: jnp.where(reached, a, b), new, before)  93.3 us
    ppermute x6, starting transfers between devices, from_behind(): lax.ppermute(value, axis, [(source, source + steps) for source in range(f...  27.8 us
  transfers between devices with their start and end apart: 7, of which 1 were waited for; matrix products, arithmetic and copies ran while one was open for 2% of the time, Pallas kernels for 0%

commit v1 on v0

--- a/solution.py
+++ b/solution.py
@@ -8,21 +8,19 @@
 REACH = 3
 
 
-def prefix(shard, axis, combine, identity):
+def exclusive_scan(element, axis, combine):
     length, here = (lax.axis_size(axis), lax.axis_index(axis))
-    everything = jax.tree.map(lambda part: lax.all_gather(part, axis), shard)
-    start = jax.tree.map(
-        lambda part, zero: jnp.broadcast_to(jnp.asarray(zero, part.dtype), part.shape),
-        shard,
-        identity,
-    )
-
-    def hop(k, before):
-        reached = k < here
-        new = combine(before, jax.tree.map(lambda part: part[k], everything))
-        return jax.tree.map(lambda a, b: jnp.where(reached, a, b), new, before)
-
-    return lax.fori_loop(0, length, hop, start)
+    received = from_behind(element, axis, 1)
+    before = received
+    total = combine(received, element)
+    shift = 2
+    while shift < length:
+        received = from_behind(total, axis, shift)
+        before = combine(received, before)
+        if 2 * shift < length:
+            total = combine(received, total)
+        shift *= 2
+    return before
 
 
 def from_behind(value, axis, steps):
@@ -86,8 +84,7 @@
         "egz,egc->gzc", key_product_lower, linear_value_rows, preferred_element_type=jnp.float32
     )
     falling = jnp.exp(cumulated[:, -1])
-    identity = (jnp.ones_like(falling), jnp.zeros_like(recurrent_state))
-    preceding_state = prefix((falling, recurrent_state), "seq", combine_states, identity)[1]
+    preceding_state = exclusive_scan((falling, recurrent_state), "seq", combine_states)[1]
     lin_scores = jnp.einsum(
         "thd,shd->hts", linear_query_rows, lin_keys, preferred_element_type=jnp.float32
     )
@@ -116,25 +113,25 @@
     query_rows = soft_queries.reshape(row_count, kv_here, group, head_width)
     block_index = lax.axis_index("seq")
     first_block = window_start[0]
-    carried_over_state = (
-        jnp.full((kv_here, group, row_count), -jnp.inf, jnp.float32),
-        jnp.zeros((kv_here, group, row_count), jnp.float32),
-        jnp.zeros((kv_here, group, row_count, head_width), jnp.float32),
+    previous = [from_behind((soft_keys, soft_values), "seq", back) for back in range(REACH, 0, -1)]
+    all_keys = jnp.concatenate([p[0] for p in previous] + [soft_keys], axis=0)
+    all_values = jnp.concatenate([p[1] for p in previous] + [soft_values], axis=0)
+    key_index = jnp.arange((REACH + 1) * row_count, dtype=jnp.int32)
+    key_block = block_index - REACH + key_index // row_count
+    causal = (key_index % row_count)[None, :] <= token_locations[:, None]
+    visible = ((key_block[None, :] < block_index) | causal) & (key_block[None, :] >= first_block)
+    logits = (
+        jnp.einsum("cphm,npm->phcn", query_rows, all_keys, preferred_element_type=jnp.float32)
+        * score_scale
     )
-    carried_over_state = attend(
-        carried_over_state, query_rows, soft_keys, soft_values, lower_mask, score_scale
+    masked = jnp.where(visible, logits, -jnp.inf)
+    top = jnp.max(masked, axis=-1)
+    exps = jnp.exp(masked - top[..., None])
+    total = jnp.sum(exps, axis=-1)
+    summed = jnp.einsum(
+        "qyjl,lqu->qyju", exps.astype(jnp.bfloat16), all_values, preferred_element_type=jnp.float32
     )
-    current = (soft_keys, soft_values)
-    for step_back in range(1, REACH + 1):
-        current = from_behind((current[0], current[1]), "seq", 1)
-        carried_over_state = attend(
-            carried_over_state,
-            query_rows,
-            current[0],
-            current[1],
-            block_index - step_back >= first_block,
-            score_scale,
-        )
+    carried_over_state = (top, total, summed)
     final_output = carried_over_state[2] / carried_over_state[1][..., None]
     soft_out = (
         final_output.transpose(2, 0, 1, 3)

time: 873 us -> 259 us (0.30)
  the two profiles are of different devices: /device:TPU:60 before, /device:TPU:89 now
where the time goes in v1:
time: 259 us
  waiting for transfers between devices  155 us (60%)
  starting transfers between devices  71.2 us (27%)
  blocking collectives  11.4 us (4%)
  matrix products  8.79 us (3%)
  other arithmetic  7.94 us (3%)
  local copies, waits for them, and re-layouts  2.7 us (1%)
    ppermute x17, waiting for transfers between devices, from_behind(): lax.ppermute(value, axis, [(source, source + steps) for source in range(f...  155 us
    ppermute x17, starting transfers between devices, from_behind(): lax.ppermute(value, axis, [(source, source + steps) for source in range(f...  71.2 us
    psum x1, blocking collectives, body(): squares = lax.psum(jnp.sum(mixed * mixed, axis=(1, 2)), 'head')  11.4 us
  transfers between devices with their start and end apart: 17, of which 9 were waited for; matrix products, arithmetic and copies ran while one was open for 4% of the time, Pallas kernels for 0%

profile of v1, /device:TPU:89, one launch (start us, length us, event | category | flops | bytes accessed | tf_op | source)
XLA Modules:
  0.0 258.6 jit_solution(11372396526609626094)
XLA Ops:
  2.1 1.4 subtract_convert_fusion.1
  3.5 1.4 fusion.28
  5.2 3.5 %collective-permute-start.5 = (f32[16,128,128]{2,1,0:T(8,128)S(1)}, f32[16,128,128]{2,1,0:T(8,128)S(1)}, u32[]{:S(2)}, u32[]{:S(2)}) collective-permute-start(f32[16,128,128]{2,1,0:T(8,128)S(1)} %convolution_add_fusion.1), channel_id=1, source_target_pairs={{0,4},{4,8},{8,12},{12,16},{16,20},{20,24},{24,28},{28,32},{32,36}... | collective-permute-start | bytes 3145736 | tf_op jit(solution)/shard_map/ppermute | solution.py:29
  8.8 22.3 %collective-permute-done.5 = f32[16,128,128]{2,1,0:T(8,128)S(1)} collective-permute-done((f32[16,128,128]{2,1,0:T(8,128)S(1)}, f32[16,128,128]{2,1,0:T(8,128)S(1)}, u32[]{:S(2)}, u32[]{:S(2)}) %collective-permute-start.5) | collective-permute-done | bytes 1048608 | tf_op jit(solution)/shard_map/ppermute | solution.py:29
  31.3 7.3 %collective-permute-start.6 = (f32[16,128,128]{2,1,0:T(8,128)S(1)}, f32[16,128,128]{2,1,0:T(8,128)S(1)}, u32[]{:S(2)}, u32[]{:S(2)}) collective-permute-start(f32[16,128,128]{2,1,0:T(8,128)S(1)} %multiply_add_fusion.4), channel_id=1, source_target_pairs={{0,8},{4,12},{8,16},{12,20},{16,24},{20,28},{24,32},{28,36},{32,40... | collective-permute-start | bytes 3145736 | tf_op jit(solution)/shard_map/ppermute | solution.py:29
  38.7 1.9 collective-permute-start
  40.6 41.4 %collective-permute-done = f32[16]{0:T(128)S(1)} collective-permute-done((f32[16]{0:T(128)S(1)}, f32[16]{0:T(128)S(1)}, u32[]{:S(2)}, u32[]{:S(2)}) %collective-permute-start) | collective-permute-done | bytes 96 | tf_op jit(solution)/shard_map/ppermute | solution.py:29
  82.0 2.1 collective-permute-done.6
  84.2 3.1 %collective-permute-start.7 = (f32[16,128,128]{2,1,0:T(8,128)S(1)}, f32[16,128,128]{2,1,0:T(8,128)S(1)}, u32[]{:S(2)}, u32[]{:S(2)}) collective-permute-start(f32[16,128,128]{2,1,0:T(8,128)S(1)} %multiply_add_fusion.3), channel_id=1, source_target_pairs={{0,16},{4,20},{8,24},{12,28},{16,32},{20,36},{24,40},{28,44},{32,4... | collective-permute-start | bytes 3145736 | tf_op jit(solution)/shard_map/ppermute | solution.py:29
  87.4 6.9 %collective-permute-start.1 = (f32[16]{0:T(128)S(1)}, f32[16]{0:T(128)S(1)}, u32[]{:S(2)}, u32[]{:S(2)}) collective-permute-start(f32[16]{0:T(128)S(1)} %exponential_multiply_fusion), channel_id=1, source_target_pairs={{0,8},{4,12},{8,16},{12,20},{16,24},{20,28},{24,32},{28,36},{32,40... | collective-permute-start | bytes 200 | tf_op jit(solution)/shard_map/ppermute | solution.py:29
  94.3 43.0 %collective-permute-done.1 = f32[16]{0:T(128)S(1)} collective-permute-done((f32[16]{0:T(128)S(1)}, f32[16]{0:T(128)S(1)}, u32[]{:S(2)}, u32[]{:S(2)}) %collective-permute-start.1) | collective-permute-done | bytes 96 | tf_op jit(solution)/shard_map/ppermute | solution.py:29
  137.5 3.0 %collective-permute-start.8 = (f32[16,128,128]{2,1,0:T(8,128)S(1)}, f32[16,128,128]{2,1,0:T(8,128)}, u32[]{:S(2)}, u32[]{:S(2)}) collective-permute-start(f32[16,128,128]{2,1,0:T(8,128)S(1)} %multiply_add_fusion.2), channel_id=1, source_target_pairs={{0,32},{4,36},{8,40},{12,44},{16,48},{20,52},{24,56},{28,60},{32,6... | collective-permute-start | bytes 3145736 | tf_op jit(solution)/shard_map/ppermute | solution.py:29
  140.6 1.9 collective-permute-start.11
  142.5 5.5 %collective-permute-start.12 = (bf16[128,2,128]{2,0,1:T(8,128)(2,1)S(1)}, bf16[128,2,128]{2,0,1:T(8,128)(2,1)S(1)}, u32[]{:S(2)}, u32[]{:S(2)}) collective-permute-start(bf16[128,2,128]{2,0,1:T(8,128)(2,1)S(1)} %copy.43), channel_id=1, source_target_pairs={{0,8},{4,12},{8,16},{12,20},{16,24},{20,28},{24,32},{28,36},{32,40... | collective-permute-start | bytes 196616 | tf_op jit(solution)/shard_map/ppermute | solution.py:29
  148.0 4.6 %collective-permute-start.13 = (bf16[128,2,128]{2,0,1:T(8,128)(2,1)S(1)}, bf16[128,2,128]{2,0,1:T(8,128)(2,1)}, u32[]{:S(2)}, u32[]{:S(2)}) collective-permute-start(bf16[128,2,128]{2,0,1:T(8,128)(2,1)S(1)} %copy.43), channel_id=1, source_target_pairs={{0,4},{4,8},{8,12},{12,16},{16,20},{20,24},{24,28},{28,32},{32,36}... | collective-permute-start | bytes 196616 | tf_op jit(solution)/shard_map/ppermute | solution.py:29
  153.3 4.6 %collective-permute-start.2 = (f32[16]{0:T(128)S(1)}, f32[16]{0:T(128)S(1)}, u32[]{:S(2)}, u32[]{:S(2)}) collective-permute-start(f32[16]{0:T(128)S(1)} %mul.154), channel_id=1, source_target_pairs={{0,16},{4,20},{8,24},{12,28},{16,32},{20,36},{24,40},{28,44},{32,4... | collective-permute-start | bytes 200 | tf_op jit(solution)/shard_map/ppermute | solution.py:29
  157.9 6.6 %collective-permute-done.2 = f32[16]{0:T(128)S(1)} collective-permute-done((f32[16]{0:T(128)S(1)}, f32[16]{0:T(128)S(1)}, u32[]{:S(2)}, u32[]{:S(2)}) %collective-permute-start.2) | collective-permute-done | bytes 96 | tf_op jit(solution)/shard_map/ppermute | solution.py:29
  164.5 2.6 %collective-permute-done.8 = f32[16,128,128]{2,1,0:T(8,128)} collective-permute-done((f32[16,128,128]{2,1,0:T(8,128)S(1)}, f32[16,128,128]{2,1,0:T(8,128)}, u32[]{:S(2)}, u32[]{:S(2)}) %collective-permute-start.8) | collective-permute-done | bytes 1048608 | tf_op jit(solution)/shard_map/ppermute | solution.py:29
  167.1 1.4 multiply_add_fusion.1
  168.5 1.9 collective-permute-start.9
  170.8 3.1 %convolution_bitcast_fusion = f32[128,16,128]{0,2,1:T(8,128)} fusion(bf16[128,16,128]{2,1,0:T(8,128)(2,1)} %param.10, f32[16,128]{1,0:T(8,128)S(1)} %reduce_window_sum.11, pred[128,128]{1,0:T(8,128)(4,1)S(1)} %iota_compare_fusion.1, bf16[128,16,128]{2,1,0:T(8,128)(2,1)S(1)} %copy-done.7, bf16[128,16,128]{2,1,0:T(8,128)(2,1)} %param.11), kind=kOutput, calls=%fused_computation.15 | convolution fusion | flops 135266304 | bytes 2646016 | tf_op jit(solution)/shard_map/hts,shd->thd/dot_general | solution.py:93
  173.8 1.9 collective-permute-start.3
  175.8 15.8 %collective-permute-done.3 = f32[16]{0:T(128)S(1)} collective-permute-done((f32[16]{0:T(128)S(1)}, f32[16]{0:T(128)S(1)}, u32[]{:S(2)}, u32[]{:S(2)}) %collective-permute-start.3) | collective-permute-done | bytes 96 | tf_op jit(solution)/shard_map/ppermute | solution.py:29
  191.6 1.9 collective-permute-start.4
  193.5 4.7 %collective-permute-done.4 = f32[16]{0:T(128)S(1)} collective-permute-done((f32[16]{0:T(128)S(1)}, f32[16]{0:T(128)S(1)}, u32[]{:S(2)}, u32[]{:S(2)}) %collective-permute-start.4) | collective-permute-done | bytes 96 | tf_op jit(solution)/shard_map/ppermute | solution.py:29
  198.2 1.9 collective-permute-start.14
  200.2 6.1 %collective-permute-start.15 = (bf16[128,2,128]{2,0,1:T(8,128)(2,1)S(1)}, bf16[128,2,128]{2,0,1:T(8,128)(2,1)S(1)}, u32[]{:S(2)}, u32[]{:S(2)}) collective-permute-start(bf16[128,2,128]{2,0,1:T(8,128)(2,1)S(1)} %copy.48), channel_id=1, source_target_pairs={{0,8},{4,12},{8,16},{12,20},{16,24},{20,28},{24,32},{28,36},{32,40... | collective-permute-start | bytes 196616 | tf_op jit(solution)/shard_map/ppermute | solution.py:29
  206.4 13.7 %collective-permute-start.16 = (bf16[128,2,128]{2,0,1:T(8,128)(2,1)S(1)}, bf16[128,2,128]{2,0,1:T(8,128)(2,1)S(1)}, u32[]{:S(2)}, u32[]{:S(2)}) collective-permute-start(bf16[128,2,128]{2,0,1:T(8,128)(2,1)S(1)} %copy.48), channel_id=1, source_target_pairs={{0,4},{4,8},{8,12},{12,16},{16,20},{20,24},{24,28},{28,32},{32,36}... | collective-permute-start | bytes 196616 | tf_op jit(solution)/shard_map/ppermute | solution.py:29
  221.5 1.6 fusion.2
  226.5 16.2 %collective-permute-done.10 = f32[16,128,128]{2,1,0:T(8,128)S(1)} collective-permute-done((f32[16,128,128]{2,1,0:T(8,128)S(1)}, f32[16,128,128]{2,1,0:T(8,128)S(1)}, u32[]{:S(2)}, u32[]{:S(2)}) %collective-permute-start.10) | collective-permute-done | bytes 1048608 | tf_op jit(solution)/shard_map/ppermute | solution.py:29
  242.8 1.8 add_add_fusion
  245.7 11.4 %psum.7 = f32[128]{0:T(128)S(1)} all-reduce(f32[128]{0:T(128)S(1)} %get-tuple-element.14), channel_id=1, replica_groups=mesh['seq'=64,'head'=4] {'head'}, use_global_device_ids=true, to_apply=%region_2.3 | all-reduce | flops 128 | bytes 1024 | tf_op jit(solution)/shard_map/psum | solution.py:104
  (65 shorter events, 10.1 us)
Async XLA Ops:
  0.6 220.9 %copy-start = (bf16[128,16,128]{2,1,0:T(8,128)(2,1)S(1)}, bf16[128,16,128]{2,1,0:T(8,128)(2,1)}, u32[]{:S(2)}) copy-start(bf16[128,16,128]{2,1,0:T(8,128)(2,1)} %param.14) | copy-start | bytes 1572868
  0.6 4.2 %copy-start.8 = (bf16[128,16,128]{2,1,0:T(8,128)(2,1)S(1)}, bf16[128,16,128]{2,1,0:T(8,128)(2,1)}, u32[]{:S(2)}) copy-start(bf16[128,16,128]{2,1,0:T(8,128)(2,1)} %param.11) | copy-start | bytes 1572868
  5.2 25.9 %collective-permute-start.5 = (f32[16,128,128]{2,1,0:T(8,128)S(1)}, f32[16,128,128]{2,1,0:T(8,128)S(1)}, u32[]{:S(2)}, u32[]{:S(2)}) collective-permute-start(f32[16,128,128]{2,1,0:T(8,128)S(1)} %convolution_add_fusion.1), channel_id=1, source_target_pairs={{0,4},{4,8},{8,12},{12,16},{16,20},{20,24},{24,28},{28,32},{32,36}... | collective-permute-start | bytes 3145736 | tf_op jit(solution)/shard_map/ppermute | solution.py:29
  8.8 131.7 %copy-start.10 = (bf16[128,2,128]{2,1,0:T(2,128)(2,1)S(1)}, bf16[128,2,128]{2,1,0:T(2,128)(2,1)}, u32[]{:S(2)}) copy-start(bf16[128,2,128]{2,1,0:T(2,128)(2,1)} %param.15) | copy-start | bytes 196612
  31.2 106.3 %copy-start.1 = (f32[16,128,128]{2,1,0:T(8,128)}, f32[16,128,128]{2,1,0:T(8,128)S(1)}, u32[]{:S(2)}) copy-start(f32[16,128,128]{2,1,0:T(8,128)S(1)} %collective-permute-done.5) | copy-start | bytes 3145732
  31.3 52.7 %collective-permute-start.6 = (f32[16,128,128]{2,1,0:T(8,128)S(1)}, f32[16,128,128]{2,1,0:T(8,128)S(1)}, u32[]{:S(2)}, u32[]{:S(2)}) collective-permute-start(f32[16,128,128]{2,1,0:T(8,128)S(1)} %multiply_add_fusion.4), channel_id=1, source_target_pairs={{0,8},{4,12},{8,16},{12,20},{16,24},{20,28},{24,32},{28,36},{32,40... | collective-permute-start | bytes 3145736 | tf_op jit(solution)/shard_map/ppermute | solution.py:29
  38.7 43.3 %collective-permute-start = (f32[16]{0:T(128)S(1)}, f32[16]{0:T(128)S(1)}, u32[]{:S(2)}, u32[]{:S(2)}) collective-permute-start(f32[16]{0:T(128)S(1)} %exp.30), channel_id=1, source_target_pairs={{0,4},{4,8},{8,12},{12,16},{16,20},{20,24},{24,28},{28,32},{32,36}... | collective-permute-start | bytes 200 | tf_op jit(solution)/shard_map/ppermute | solution.py:29
  82.0 88.8 %copy-start.7 = (bf16[128,16,128]{2,1,0:T(8,128)(2,1)S(1)}, bf16[128,16,128]{2,1,0:T(8,128)(2,1)}, u32[]{:S(2)}) copy-start(bf16[128,16,128]{2,1,0:T(8,128)(2,1)} %param.9) | copy-start | bytes 1572868
  84.1 56.5 %copy-start.3 = (f32[16,128,128]{2,1,0:T(8,128)}, f32[16,128,128]{2,1,0:T(8,128)S(1)}, u32[]{:S(2)}) copy-start(f32[16,128,128]{2,1,0:T(8,128)S(1)} %collective-permute-done.6) | copy-start | bytes 3145732
  84.2 53.1 %collective-permute-start.7 = (f32[16,128,128]{2,1,0:T(8,128)S(1)}, f32[16,128,128]{2,1,0:T(8,128)S(1)}, u32[]{:S(2)}, u32[]{:S(2)}) collective-permute-start(f32[16,128,128]{2,1,0:T(8,128)S(1)} %multiply_add_fusion.3), channel_id=1, source_target_pairs={{0,16},{4,20},{8,24},{12,28},{16,32},{20,36},{24,40},{28,44},{32,4... | collective-permute-start | bytes 3145736 | tf_op jit(solution)/shard_map/ppermute | solution.py:29
  87.4 49.9 %collective-permute-start.1 = (f32[16]{0:T(128)S(1)}, f32[16]{0:T(128)S(1)}, u32[]{:S(2)}, u32[]{:S(2)}) collective-permute-start(f32[16]{0:T(128)S(1)} %exponential_multiply_fusion), channel_id=1, source_target_pairs={{0,8},{4,12},{8,16},{12,20},{16,24},{20,28},{24,32},{28,36},{32,40... | collective-permute-start | bytes 200 | tf_op jit(solution)/shard_map/ppermute | solution.py:29
  137.3 38.4 %copy-start.11 = (bf16[128,2,128]{2,1,0:T(2,128)(2,1)S(1)}, bf16[128,2,128]{2,1,0:T(2,128)(2,1)}, u32[]{:S(2)}) copy-start(bf16[128,2,128]{2,1,0:T(2,128)(2,1)} %param.16) | copy-start | bytes 196612
  137.3 3.3 %copy-start.5 = (f32[16,128,128]{2,1,0:T(8,128)}, f32[16,128,128]{2,1,0:T(8,128)S(1)}, u32[]{:S(2)}) copy-start(f32[16,128,128]{2,1,0:T(8,128)S(1)} %collective-permute-done.7) | copy-start | bytes 3145732
  137.5 56.0 %copy-start.12 = (bf16[16,128]{1,0:T(8,128)(2,1)S(1)}, bf16[16,128]{1,0:T(8,128)(2,1)}, u32[]{:S(2)}) copy-start(bf16[16,128]{1,0:T(8,128)(2,1)} %param.13) | copy-start | bytes 12292
  137.5 29.6 %collective-permute-start.8 = (f32[16,128,128]{2,1,0:T(8,128)S(1)}, f32[16,128,128]{2,1,0:T(8,128)}, u32[]{:S(2)}, u32[]{:S(2)}) collective-permute-start(f32[16,128,128]{2,1,0:T(8,128)S(1)} %multiply_add_fusion.2), channel_id=1, source_target_pairs={{0,32},{4,36},{8,40},{12,44},{16,48},{20,52},{24,56},{28,60},{32,6... | collective-permute-start | bytes 3145736 | tf_op jit(solution)/shard_map/ppermute | solution.py:29
  140.6 65.8 %collective-permute-start.11 = (bf16[128,2,128]{2,0,1:T(8,128)(2,1)S(1)}, bf16[128,2,128]{2,0,1:T(8,128)(2,1)S(1)}, u32[]{:S(2)}, u32[]{:S(2)}) collective-permute-start(bf16[128,2,128]{2,0,1:T(8,128)(2,1)S(1)} %copy.43), channel_id=1, source_target_pairs={{0,12},{4,16},{8,20},{12,24},{16,28},{20,32},{24,36},{28,40},{32,4... | collective-permute-start | bytes 196616 | tf_op jit(solution)/shard_map/ppermute | solution.py:29
  142.5 77.7 %collective-permute-start.12 = (bf16[128,2,128]{2,0,1:T(8,128)(2,1)S(1)}, bf16[128,2,128]{2,0,1:T(8,128)(2,1)S(1)}, u32[]{:S(2)}, u32[]{:S(2)}) collective-permute-start(bf16[128,2,128]{2,0,1:T(8,128)(2,1)S(1)} %copy.43), channel_id=1, source_target_pairs={{0,8},{4,12},{8,16},{12,20},{16,24},{20,28},{24,32},{28,36},{32,40... | collective-permute-start | bytes 196616 | tf_op jit(solution)/shard_map/ppermute | solution.py:29
  148.0 73.5 %collective-permute-start.13 = (bf16[128,2,128]{2,0,1:T(8,128)(2,1)S(1)}, bf16[128,2,128]{2,0,1:T(8,128)(2,1)}, u32[]{:S(2)}, u32[]{:S(2)}) collective-permute-start(bf16[128,2,128]{2,0,1:T(8,128)(2,1)S(1)} %copy.43), channel_id=1, source_target_pairs={{0,4},{4,8},{8,12},{12,16},{16,20},{20,24},{24,28},{28,32},{32,36}... | collective-permute-start | bytes 196616 | tf_op jit(solution)/shard_map/ppermute | solution.py:29
  153.3 11.2 %collective-permute-start.2 = (f32[16]{0:T(128)S(1)}, f32[16]{0:T(128)S(1)}, u32[]{:S(2)}, u32[]{:S(2)}) collective-permute-start(f32[16]{0:T(128)S(1)} %mul.154), channel_id=1, source_target_pairs={{0,16},{4,20},{8,24},{12,28},{16,32},{20,36},{24,40},{28,44},{32,4... | collective-permute-start | bytes 200 | tf_op jit(solution)/shard_map/ppermute | solution.py:29
  168.5 31.7 %collective-permute-start.9 = (f32[16,128,128]{2,1,0:T(8,128)S(1)}, f32[16,128,128]{2,1,0:T(8,128)S(1)}, u32[]{:S(2)}, u32[]{:S(2)}) collective-permute-start(f32[16,128,128]{2,1,0:T(8,128)S(1)} %multiply_add_fusion.1), channel_id=1, source_target_pairs={{0,64},{4,68},{8,72},{12,76},{16,80},{20,84},{24,88},{28,92},{32,9... | collective-permute-start | bytes 3145736 | tf_op jit(solution)/shard_map/ppermute | solution.py:29
  173.8 17.7 %collective-permute-start.3 = (f32[16]{0:T(128)S(1)}, f32[16]{0:T(128)S(1)}, u32[]{:S(2)}, u32[]{:S(2)}) collective-permute-start(f32[16]{0:T(128)S(1)} %mul.155), channel_id=1, source_target_pairs={{0,32},{4,36},{8,40},{12,44},{16,48},{20,52},{24,56},{28,60},{32,6... | collective-permute-start | bytes 200 | tf_op jit(solution)/shard_map/ppermute | solution.py:29
  191.6 6.7 %collective-permute-start.4 = (f32[16]{0:T(128)S(1)}, f32[16]{0:T(128)S(1)}, u32[]{:S(2)}, u32[]{:S(2)}) collective-permute-start(f32[16]{0:T(128)S(1)} %mul.156), channel_id=1, source_target_pairs={{0,64},{4,68},{8,72},{12,76},{16,80},{20,84},{24,88},{28,92},{32,9... | collective-permute-start | bytes 200 | tf_op jit(solution)/shard_map/ppermute | solution.py:29
  198.2 25.7 %collective-permute-start.14 = (bf16[128,2,128]{2,0,1:T(8,128)(2,1)S(1)}, bf16[128,2,128]{2,0,1:T(8,128)(2,1)S(1)}, u32[]{:S(2)}, u32[]{:S(2)}) collective-permute-start(bf16[128,2,128]{2,0,1:T(8,128)(2,1)S(1)} %copy.48), channel_id=1, source_target_pairs={{0,12},{4,16},{8,20},{12,24},{16,28},{20,32},{24,36},{28,40},{32,4... | collective-permute-start | bytes 196616 | tf_op jit(solution)/shard_map/ppermute | solution.py:29
  200.2 23.8 %collective-permute-start.15 = (bf16[128,2,128]{2,0,1:T(8,128)(2,1)S(1)}, bf16[128,2,128]{2,0,1:T(8,128)(2,1)S(1)}, u32[]{:S(2)}, u32[]{:S(2)}) collective-permute-start(bf16[128,2,128]{2,0,1:T(8,128)(2,1)S(1)} %copy.48), channel_id=1, source_target_pairs={{0,8},{4,12},{8,16},{12,20},{16,24},{20,28},{24,32},{28,36},{32,40... | collective-permute-start | bytes 196616 | tf_op jit(solution)/shard_map/ppermute | solution.py:29
  206.4 17.5 %collective-permute-start.16 = (bf16[128,2,128]{2,0,1:T(8,128)(2,1)S(1)}, bf16[128,2,128]{2,0,1:T(8,128)(2,1)S(1)}, u32[]{:S(2)}, u32[]{:S(2)}) collective-permute-start(bf16[128,2,128]{2,0,1:T(8,128)(2,1)S(1)} %copy.48), channel_id=1, source_target_pairs={{0,4},{4,8},{8,12},{12,16},{16,20},{20,24},{24,28},{28,32},{32,36}... | collective-permute-start | bytes 196616 | tf_op jit(solution)/shard_map/ppermute | solution.py:29
  220.2 22.6 %collective-permute-start.10 = (f32[16,128,128]{2,1,0:T(8,128)S(1)}, f32[16,128,128]{2,1,0:T(8,128)S(1)}, u32[]{:S(2)}, u32[]{:S(2)}) collective-permute-start(f32[16,128,128]{2,1,0:T(8,128)S(1)} %multiply_add_fusion), channel_id=1, source_target_pairs={{0,128},{4,132},{8,136},{12,140},{16,144},{20,148},{24,152},{28,15... | collective-permute-start | bytes 3145736 | tf_op jit(solution)/shard_map/ppermute | solution.py:29
  224.0 18.8 %copy-start.2 = (f32[16,128,128]{2,1,0:T(8,128)S(1)}, f32[16,128,128]{2,1,0:T(8,128)}, u32[]{:S(2)}) copy-start(f32[16,128,128]{2,1,0:T(8,128)} %copy-done.1) | copy-start | bytes 3145732
  224.0 18.8 %copy-start.4 = (f32[16,128,128]{2,1,0:T(8,128)S(1)}, f32[16,128,128]{2,1,0:T(8,128)}, u32[]{:S(2)}) copy-start(f32[16,128,128]{2,1,0:T(8,128)} %copy-done.3) | copy-start | bytes 3145732
  224.0 18.8 %copy-start.6 = (f32[16,128,128]{2,1,0:T(8,128)S(1)}, f32[16,128,128]{2,1,0:T(8,128)}, u32[]{:S(2)}) copy-start(f32[16,128,128]{2,1,0:T(8,128)} %copy-done.5) | copy-start | bytes 3145732
  242.8 2.4 copy-start.9

commit v2 on v1

--- a/solution.py
+++ b/solution.py
@@ -9,13 +9,18 @@
 
 
 def exclusive_scan(element, axis, combine):
-    length, here = (lax.axis_size(axis), lax.axis_index(axis))
-    received = from_behind(element, axis, 1)
+    length = lax.axis_size(axis)
+
+    def send(value, shift):
+        fall, state = from_behind((value[0], value[1].astype(jnp.bfloat16)), axis, shift)
+        return (fall, state.astype(jnp.float32))
+
+    received = send(element, 1)
     before = received
     total = combine(received, element)
     shift = 2
     while shift < length:
-        received = from_behind(total, axis, shift)
+        received = send(total, shift)
         before = combine(received, before)
         if 2 * shift < length:
             total = combine(received, total)

time: 259 us -> 177 us (0.68)
  the two profiles are of different devices: /device:TPU:89 before, /device:TPU:25 now
where the time goes in v2:
time: 177 us; the launch traced here: 176 us
  waiting for transfers between devices  95.6 us (54%)
  starting transfers between devices  44.5 us (25%)
  blocking collectives  13 us (7%)
  other arithmetic  9.34 us (5%)
  matrix products  8.08 us (5%)
  local copies, waits for them, and re-layouts  3.48 us (2%)
    ppermute x17, waiting for transfers between devices, from_behind(): lax.ppermute(value, axis, [(source, source + steps) for source in range(f...  95.6 us
    ppermute x17, starting transfers between devices, from_behind(): lax.ppermute(value, axis, [(source, source + steps) for source in range(f...  44.5 us
    psum x1, blocking collectives, body(): squares = lax.psum(jnp.sum(mixed * mixed, axis=(1, 2)), 'head')  13 us
    convert_element_type x5, other arithmetic, send(): value[1].astype(jnp.bfloat16)  3.55 us
  transfers between devices with their start and end apart: 17, of which 10 were waited for; matrix products, arithmetic and copies ran while one was open for 6% of the time, Pallas kernels for 0%

profile of v2, /device:TPU:25, one launch (start us, length us, event | category | flops | bytes accessed | tf_op | source)
XLA Modules:
  0.0 175.8 jit_solution(12449341329791081557)
XLA Ops:
  2.1 1.4 subtract_convert_fusion.1
  3.5 1.4 fusion.40
  5.3 3.5 %collective-permute-start.5 = (bf16[16,128,128]{2,1,0:T(8,128)(2,1)S(1)}, bf16[16,128,128]{2,1,0:T(8,128)(2,1)S(1)}, u32[]{:S(2)}, u32[]{:S(2)}) collective-permute-start(bf16[16,128,128]{2,1,0:T(8,128)(2,1)S(1)} %get-tuple-element.16), channel_id=1, source_target_pairs={{0,4},{4,8},{8,12},{12,16},{16,20},{20,24},{24,28},{28,32},{32,36}... | collective-permute-start | bytes 1572872 | tf_op jit(solution)/shard_map/ppermute | solution.py:34
  8.8 17.9 %collective-permute-done.5 = bf16[16,128,128]{2,1,0:T(8,128)(2,1)S(1)} collective-permute-done((bf16[16,128,128]{2,1,0:T(8,128)(2,1)S(1)}, bf16[16,128,128]{2,1,0:T(8,128)(2,1)S(1)}, u32[]{:S(2)}, u32[]{:S(2)}) %collective-permute-start.5) | collective-permute-done | bytes 524320 | tf_op jit(solution)/shard_map/ppermute | solution.py:34
  27.0 1.9 %collective-permute-start.6 = (bf16[16,128,128]{2,1,0:T(8,128)(2,1)S(1)}, bf16[16,128,128]{2,1,0:T(8,128)(2,1)S(1)}, u32[]{:S(2)}, u32[]{:S(2)}) collective-permute-start(bf16[16,128,128]{2,1,0:T(8,128)(2,1)S(1)} %fusion.82), channel_id=1, source_target_pairs={{0,8},{4,12},{8,16},{12,20},{16,24},{20,28},{24,32},{28,36},{32,40... | collective-permute-start | bytes 1572872 | tf_op jit(solution)/shard_map/ppermute | solution.py:34
  28.9 1.9 %collective-permute-start = (f32[16]{0:T(128)S(1)}, f32[16]{0:T(128)S(1)}, u32[]{:S(2)}, u32[]{:S(2)}) collective-permute-start(f32[16]{0:T(128)S(1)} %exp.30), channel_id=1, source_target_pairs={{0,4},{4,8},{8,12},{12,16},{16,20},{20,24},{24,28},{28,32},{32,36}... | collective-permute-start | bytes 200 | tf_op jit(solution)/shard_map/ppermute | solution.py:34
  30.8 19.5 %collective-permute-done = f32[16]{0:T(128)S(1)} collective-permute-done((f32[16]{0:T(128)S(1)}, f32[16]{0:T(128)S(1)}, u32[]{:S(2)}, u32[]{:S(2)}) %collective-permute-start) | collective-permute-done | bytes 96 | tf_op jit(solution)/shard_map/ppermute | solution.py:34
  50.3 7.1 %collective-permute-done.6 = bf16[16,128,128]{2,1,0:T(8,128)(2,1)S(1)} collective-permute-done((bf16[16,128,128]{2,1,0:T(8,128)(2,1)S(1)}, bf16[16,128,128]{2,1,0:T(8,128)(2,1)S(1)}, u32[]{:S(2)}, u32[]{:S(2)}) %collective-permute-start.6) | collective-permute-done | bytes 524320 | tf_op jit(solution)/shard_map/ppermute | solution.py:34
  58.5 2.1 %collective-permute-start.7 = (bf16[16,128,128]{2,1,0:T(8,128)(2,1)S(1)}, bf16[16,128,128]{2,1,0:T(8,128)(2,1)}, u32[]{:S(2)}, u32[]{:S(2)}) collective-permute-start(bf16[16,128,128]{2,1,0:T(8,128)(2,1)S(1)} %fusion.33), channel_id=1, source_target_pairs={{0,16},{4,20},{8,24},{12,28},{16,32},{20,36},{24,40},{28,44},{32,4... | collective-permute-start | bytes 1572872 | tf_op jit(solution)/shard_map/ppermute | solution.py:34
  60.6 1.9 %collective-permute-start.11 = (bf16[128,2,128]{2,0,1:T(8,128)(2,1)S(1)}, bf16[128,2,128]{2,0,1:T(8,128)(2,1)S(1)}, u32[]{:S(2)}, u32[]{:S(2)}) collective-permute-start(bf16[128,2,128]{2,0,1:T(8,128)(2,1)S(1)} %copy.43), channel_id=1, source_target_pairs={{0,12},{4,16},{8,20},{12,24},{16,28},{20,32},{24,36},{28,40},{32,4... | collective-permute-start | bytes 196616 | tf_op jit(solution)/shard_map/ppermute | solution.py:34
  62.6 1.9 %collective-permute-start.12 = (bf16[128,2,128]{2,0,1:T(8,128)(2,1)S(1)}, bf16[128,2,128]{2,0,1:T(8,128)(2,1)S(1)}, u32[]{:S(2)}, u32[]{:S(2)}) collective-permute-start(bf16[128,2,128]{2,0,1:T(8,128)(2,1)S(1)} %copy.43), channel_id=1, source_target_pairs={{0,8},{4,12},{8,16},{12,20},{16,24},{20,28},{24,32},{28,36},{32,40... | collective-permute-start | bytes 196616 | tf_op jit(solution)/shard_map/ppermute | solution.py:34
  64.5 4.1 %collective-permute-start.13 = (bf16[128,2,128]{2,0,1:T(8,128)(2,1)S(1)}, bf16[128,2,128]{2,0,1:T(8,128)(2,1)S(1)}, u32[]{:S(2)}, u32[]{:S(2)}) collective-permute-start(bf16[128,2,128]{2,0,1:T(8,128)(2,1)S(1)} %copy.43), channel_id=1, source_target_pairs={{0,4},{4,8},{8,12},{12,16},{16,20},{20,24},{24,28},{28,32},{32,36}... | collective-permute-start | bytes 196616 | tf_op jit(solution)/shard_map/ppermute | solution.py:34
  69.3 5.4 %collective-permute-start.1 = (f32[16]{0:T(128)S(1)}, f32[16]{0:T(128)S(1)}, u32[]{:S(2)}, u32[]{:S(2)}) collective-permute-start(f32[16]{0:T(128)S(1)} %exponential_multiply_fusion), channel_id=1, source_target_pairs={{0,8},{4,12},{8,16},{12,20},{16,24},{20,28},{24,32},{28,36},{32,40... | collective-permute-start | bytes 200 | tf_op jit(solution)/shard_map/ppermute | solution.py:34
  74.6 16.2 %collective-permute-done.1 = f32[16]{0:T(128)S(1)} collective-permute-done((f32[16]{0:T(128)S(1)}, f32[16]{0:T(128)S(1)}, u32[]{:S(2)}, u32[]{:S(2)}) %collective-permute-start.1) | collective-permute-done | bytes 96 | tf_op jit(solution)/shard_map/ppermute | solution.py:34
  92.0 2.5 %fusion.84 = (bf16[16,128,128]{2,1,0:T(8,128)(2,1)}, f32[16,128,128]{2,1,0:T(8,128)S(1)}) fusion(f32[16,128,128]{2,1,0:T(8,128)S(1)} %get-tuple-element.17, bf16[16,128,128]{2,1,0:T(8,128)(2,1)S(1)} %collective-permute-done.5, f32[16]{0:T(128)S(1)} %exp.30, bf16[16,128,128]{2,1,0:T(8,128)(2,1)} %copy-done.1, f32[16]{0:T(128)S(1)} %exponential_multiply_fusion, ...), kind=kLoop, calls=%fused_computation.114 | loop fusion | flops 2621440 | bytes 4194496 | tf_op jit(solution)/shard_map/convert_element_type | solution.py:15
  94.5 2.0 %collective-permute-start.8 = (bf16[16,128,128]{2,1,0:T(8,128)(2,1)}, bf16[16,128,128]{2,1,0:T(8,128)(2,1)S(1)}, u32[]{:S(2)}, u32[]{:S(2)}) collective-permute-start(bf16[16,128,128]{2,1,0:T(8,128)(2,1)} %get-tuple-element.10), channel_id=1, source_target_pairs={{0,32},{4,36},{8,40},{12,44},{16,48},{20,52},{24,56},{28,60},{32,6... | collective-permute-start | bytes 1572872 | tf_op jit(solution)/shard_map/ppermute | solution.py:34
  96.8 3.2 %convolution_bitcast_fusion = f32[128,16,128]{0,2,1:T(8,128)} fusion(bf16[128,16,128]{2,1,0:T(8,128)(2,1)} %param.10, f32[16,128]{1,0:T(8,128)S(1)} %reduce_window_sum.11, pred[128,128]{1,0:T(8,128)(4,1)S(1)} %iota_compare_fusion.1, bf16[128,16,128]{2,1,0:T(8,128)(2,1)} %param.9, bf16[128,16,128]{2,1,0:T(8,128)(2,1)} %param.11), kind=kOutput, calls=%fused_computation.15 | convolution fusion | flops 135266304 | bytes 2646016 | tf_op jit(solution)/shard_map/hts,shd->thd/dot_general | solution.py:98
  100.0 3.2 %collective-permute-start.2 = (f32[16]{0:T(128)S(1)}, f32[16]{0:T(128)S(1)}, u32[]{:S(2)}, u32[]{:S(2)}) collective-permute-start(f32[16]{0:T(128)S(1)} %mul.154), channel_id=1, source_target_pairs={{0,16},{4,20},{8,24},{12,28},{16,32},{20,36},{24,40},{28,44},{32,4... | collective-permute-start | bytes 200 | tf_op jit(solution)/shard_map/ppermute | solution.py:34
  103.3 7.9 %collective-permute-done.2 = f32[16]{0:T(128)S(1)} collective-permute-done((f32[16]{0:T(128)S(1)}, f32[16]{0:T(128)S(1)}, u32[]{:S(2)}, u32[]{:S(2)}) %collective-permute-start.2) | collective-permute-done | bytes 96 | tf_op jit(solution)/shard_map/ppermute | solution.py:34
  111.2 1.9 %collective-permute-start.3 = (f32[16]{0:T(128)S(1)}, f32[16]{0:T(128)S(1)}, u32[]{:S(2)}, u32[]{:S(2)}) collective-permute-start(f32[16]{0:T(128)S(1)} %mul.155), channel_id=1, source_target_pairs={{0,32},{4,36},{8,40},{12,44},{16,48},{20,52},{24,56},{28,60},{32,6... | collective-permute-start | bytes 200 | tf_op jit(solution)/shard_map/ppermute | solution.py:34
  113.1 4.4 %collective-permute-done.3 = f32[16]{0:T(128)S(1)} collective-permute-done((f32[16]{0:T(128)S(1)}, f32[16]{0:T(128)S(1)}, u32[]{:S(2)}, u32[]{:S(2)}) %collective-permute-start.3) | collective-permute-done | bytes 96 | tf_op jit(solution)/shard_map/ppermute | solution.py:34
  117.6 5.3 %collective-permute-start.14 = (bf16[128,2,128]{2,0,1:T(8,128)(2,1)S(1)}, bf16[128,2,128]{2,0,1:T(8,128)(2,1)S(1)}, u32[]{:S(2)}, u32[]{:S(2)}) collective-permute-start(bf16[128,2,128]{2,0,1:T(8,128)(2,1)S(1)} %copy.48), channel_id=1, source_target_pairs={{0,12},{4,16},{8,20},{12,24},{16,28},{20,32},{24,36},{28,40},{32,4... | collective-permute-start | bytes 196616 | tf_op jit(solution)/shard_map/ppermute | solution.py:34
  123.0 1.9 %collective-permute-start.4 = (f32[16]{0:T(128)S(1)}, f32[16]{0:T(128)S(1)}, u32[]{:S(2)}, u32[]{:S(2)}) collective-permute-start(f32[16]{0:T(128)S(1)} %mul.156), channel_id=1, source_target_pairs={{0,64},{4,68},{8,72},{12,76},{16,80},{20,84},{24,88},{28,92},{32,9... | collective-permute-start | bytes 200 | tf_op jit(solution)/shard_map/ppermute | solution.py:34
  125.1 4.5 %collective-permute-done.4 = f32[16]{0:T(128)S(1)} collective-permute-done((f32[16]{0:T(128)S(1)}, f32[16]{0:T(128)S(1)}, u32[]{:S(2)}, u32[]{:S(2)}) %collective-permute-start.4) | collective-permute-done | bytes 96 | tf_op jit(solution)/shard_map/ppermute | solution.py:34
  129.6 1.9 %collective-permute-start.9 = (bf16[16,128,128]{2,1,0:T(8,128)(2,1)S(1)}, bf16[16,128,128]{2,1,0:T(8,128)(2,1)S(1)}, u32[]{:S(2)}, u32[]{:S(2)}) collective-permute-start(bf16[16,128,128]{2,1,0:T(8,128)(2,1)S(1)} %fusion.32), channel_id=1, source_target_pairs={{0,64},{4,68},{8,72},{12,76},{16,80},{20,84},{24,88},{28,92},{32,9... | collective-permute-start | bytes 1572872 | tf_op jit(solution)/shard_map/ppermute | solution.py:34
  131.6 1.9 %collective-permute-start.15 = (bf16[128,2,128]{2,0,1:T(8,128)(2,1)S(1)}, bf16[128,2,128]{2,0,1:T(8,128)(2,1)S(1)}, u32[]{:S(2)}, u32[]{:S(2)}) collective-permute-start(bf16[128,2,128]{2,0,1:T(8,128)(2,1)S(1)} %copy.48), channel_id=1, source_target_pairs={{0,8},{4,12},{8,16},{12,20},{16,24},{20,28},{24,32},{28,36},{32,40... | collective-permute-start | bytes 196616 | tf_op jit(solution)/shard_map/ppermute | solution.py:34
  133.5 2.2 %collective-permute-start.16 = (bf16[128,2,128]{2,0,1:T(8,128)(2,1)S(1)}, bf16[128,2,128]{2,0,1:T(8,128)(2,1)S(1)}, u32[]{:S(2)}, u32[]{:S(2)}) collective-permute-start(bf16[128,2,128]{2,0,1:T(8,128)(2,1)S(1)} %copy.48), channel_id=1, source_target_pairs={{0,4},{4,8},{8,12},{12,16},{16,20},{20,24},{24,28},{28,32},{32,36}... | collective-permute-start | bytes 196616 | tf_op jit(solution)/shard_map/ppermute | solution.py:34
  136.5 11.7 %collective-permute-done.9 = bf16[16,128,128]{2,1,0:T(8,128)(2,1)S(1)} collective-permute-done((bf16[16,128,128]{2,1,0:T(8,128)(2,1)S(1)}, bf16[16,128,128]{2,1,0:T(8,128)(2,1)S(1)}, u32[]{:S(2)}, u32[]{:S(2)}) %collective-permute-start.9) | collective-permute-done | bytes 524320 | tf_op jit(solution)/shard_map/ppermute | solution.py:34
  150.7 1.4 divide_convert_fusion
  153.2 5.2 %collective-permute-done.10 = bf16[16,128,128]{2,1,0:T(8,128)(2,1)S(1)} collective-permute-done((bf16[16,128,128]{2,1,0:T(8,128)(2,1)S(1)}, bf16[16,128,128]{2,1,0:T(8,128)(2,1)S(1)}, u32[]{:S(2)}, u32[]{:S(2)}) %collective-permute-start.10) | collective-permute-done | bytes 524320 | tf_op jit(solution)/shard_map/ppermute | solution.py:34
  158.4 1.7 fusion.20
  161.2 13.0 %psum.7 = f32[128]{0:T(128)S(1)} all-reduce(f32[128]{0:T(128)S(1)} %get-tuple-element.18), channel_id=1, replica_groups=mesh['seq'=64,'head'=4] {'head'}, use_global_device_ids=true, to_apply=%region_2.3 | all-reduce | flops 128 | bytes 1024 | tf_op jit(solution)/shard_map/psum | solution.py:109
  (57 shorter events, 11.8 us)
Async XLA Ops:
  0.6 135.1 %copy-start = (bf16[128,16,128]{2,1,0:T(8,128)(2,1)S(1)}, bf16[128,16,128]{2,1,0:T(8,128)(2,1)}, u32[]{:S(2)}) copy-start(bf16[128,16,128]{2,1,0:T(8,128)(2,1)} %param.14) | copy-start | bytes 1572868
  0.6 4.2 %copy-start.4 = (bf16[128,16,128]{2,1,0:T(8,128)(2,1)S(1)}, bf16[128,16,128]{2,1,0:T(8,128)(2,1)}, u32[]{:S(2)}) copy-start(bf16[128,16,128]{2,1,0:T(8,128)(2,1)} %param.11) | copy-start | bytes 1572868
  4.9 55.7 %copy-start.6 = (bf16[128,2,128]{2,1,0:T(2,128)(2,1)S(1)}, bf16[128,2,128]{2,1,0:T(2,128)(2,1)}, u32[]{:S(2)}) copy-start(bf16[128,2,128]{2,1,0:T(2,128)(2,1)} %param.15) | copy-start | bytes 196612
  5.3 21.5 %collective-permute-start.5 = (bf16[16,128,128]{2,1,0:T(8,128)(2,1)S(1)}, bf16[16,128,128]{2,1,0:T(8,128)(2,1)S(1)}, u32[]{:S(2)}, u32[]{:S(2)}) collective-permute-start(bf16[16,128,128]{2,1,0:T(8,128)(2,1)S(1)} %get-tuple-element.16), channel_id=1, source_target_pairs={{0,4},{4,8},{8,12},{12,16},{16,20},{20,24},{24,28},{28,32},{32,36}... | collective-permute-start | bytes 1572872 | tf_op jit(solution)/shard_map/ppermute | solution.py:34
  27.0 30.4 %collective-permute-start.6 = (bf16[16,128,128]{2,1,0:T(8,128)(2,1)S(1)}, bf16[16,128,128]{2,1,0:T(8,128)(2,1)S(1)}, u32[]{:S(2)}, u32[]{:S(2)}) collective-permute-start(bf16[16,128,128]{2,1,0:T(8,128)(2,1)S(1)} %fusion.82), channel_id=1, source_target_pairs={{0,8},{4,12},{8,16},{12,20},{16,24},{20,28},{24,32},{28,36},{32,40... | collective-permute-start | bytes 1572872 | tf_op jit(solution)/shard_map/ppermute | solution.py:34
  28.9 21.4 %collective-permute-start = (f32[16]{0:T(128)S(1)}, f32[16]{0:T(128)S(1)}, u32[]{:S(2)}, u32[]{:S(2)}) collective-permute-start(f32[16]{0:T(128)S(1)} %exp.30), channel_id=1, source_target_pairs={{0,4},{4,8},{8,12},{12,16},{16,20},{20,24},{24,28},{28,32},{32,36}... | collective-permute-start | bytes 200 | tf_op jit(solution)/shard_map/ppermute | solution.py:34
  57.4 0.8 copy-start.1
  58.5 44.7 %copy-start.7 = (bf16[128,2,128]{2,1,0:T(2,128)(2,1)S(1)}, bf16[128,2,128]{2,1,0:T(2,128)(2,1)}, u32[]{:S(2)}) copy-start(bf16[128,2,128]{2,1,0:T(2,128)(2,1)} %param.16) | copy-start | bytes 196612
  58.5 54.6 %copy-start.8 = (bf16[16,128]{1,0:T(8,128)(2,1)S(1)}, bf16[16,128]{1,0:T(8,128)(2,1)}, u32[]{:S(2)}) copy-start(bf16[16,128]{1,0:T(8,128)(2,1)} %param.13) | copy-start | bytes 12292
  58.5 33.4 %collective-permute-start.7 = (bf16[16,128,128]{2,1,0:T(8,128)(2,1)S(1)}, bf16[16,128,128]{2,1,0:T(8,128)(2,1)}, u32[]{:S(2)}, u32[]{:S(2)}) collective-permute-start(bf16[16,128,128]{2,1,0:T(8,128)(2,1)S(1)} %fusion.33), channel_id=1, source_target_pairs={{0,16},{4,20},{8,24},{12,28},{16,32},{20,36},{24,40},{28,44},{32,4... | collective-permute-start | bytes 1572872 | tf_op jit(solution)/shard_map/ppermute | solution.py:34
  60.6 71.0 %collective-permute-start.11 = (bf16[128,2,128]{2,0,1:T(8,128)(2,1)S(1)}, bf16[128,2,128]{2,0,1:T(8,128)(2,1)S(1)}, u32[]{:S(2)}, u32[]{:S(2)}) collective-permute-start(bf16[128,2,128]{2,0,1:T(8,128)(2,1)S(1)} %copy.43), channel_id=1, source_target_pairs={{0,12},{4,16},{8,20},{12,24},{16,28},{20,32},{24,36},{28,40},{32,4... | collective-permute-start | bytes 196616 | tf_op jit(solution)/shard_map/ppermute | solution.py:34
  62.6 71.0 %collective-permute-start.12 = (bf16[128,2,128]{2,0,1:T(8,128)(2,1)S(1)}, bf16[128,2,128]{2,0,1:T(8,128)(2,1)S(1)}, u32[]{:S(2)}, u32[]{:S(2)}) collective-permute-start(bf16[128,2,128]{2,0,1:T(8,128)(2,1)S(1)} %copy.43), channel_id=1, source_target_pairs={{0,8},{4,12},{8,16},{12,20},{16,24},{20,28},{24,32},{28,36},{32,40... | collective-permute-start | bytes 196616 | tf_op jit(solution)/shard_map/ppermute | solution.py:34
  64.5 71.2 %collective-permute-start.13 = (bf16[128,2,128]{2,0,1:T(8,128)(2,1)S(1)}, bf16[128,2,128]{2,0,1:T(8,128)(2,1)S(1)}, u32[]{:S(2)}, u32[]{:S(2)}) collective-permute-start(bf16[128,2,128]{2,0,1:T(8,128)(2,1)S(1)} %copy.43), channel_id=1, source_target_pairs={{0,4},{4,8},{8,12},{12,16},{16,20},{20,24},{24,28},{28,32},{32,36}... | collective-permute-start | bytes 196616 | tf_op jit(solution)/shard_map/ppermute | solution.py:34
  69.3 21.6 %collective-permute-start.1 = (f32[16]{0:T(128)S(1)}, f32[16]{0:T(128)S(1)}, u32[]{:S(2)}, u32[]{:S(2)}) collective-permute-start(f32[16]{0:T(128)S(1)} %exponential_multiply_fusion), channel_id=1, source_target_pairs={{0,8},{4,12},{8,16},{12,20},{16,24},{20,28},{24,32},{28,36},{32,40... | collective-permute-start | bytes 200 | tf_op jit(solution)/shard_map/ppermute | solution.py:34
  94.5 28.5 %collective-permute-start.8 = (bf16[16,128,128]{2,1,0:T(8,128)(2,1)}, bf16[16,128,128]{2,1,0:T(8,128)(2,1)S(1)}, u32[]{:S(2)}, u32[]{:S(2)}) collective-permute-start(bf16[16,128,128]{2,1,0:T(8,128)(2,1)} %get-tuple-element.10), channel_id=1, source_target_pairs={{0,32},{4,36},{8,40},{12,44},{16,48},{20,52},{24,56},{28,60},{32,6... | collective-permute-start | bytes 1572872 | tf_op jit(solution)/shard_map/ppermute | solution.py:34
  100.0 11.2 %collective-permute-start.2 = (f32[16]{0:T(128)S(1)}, f32[16]{0:T(128)S(1)}, u32[]{:S(2)}, u32[]{:S(2)}) collective-permute-start(f32[16]{0:T(128)S(1)} %mul.154), channel_id=1, source_target_pairs={{0,16},{4,20},{8,24},{12,28},{16,32},{20,36},{24,40},{28,44},{32,4... | collective-permute-start | bytes 200 | tf_op jit(solution)/shard_map/ppermute | solution.py:34
  111.2 6.4 %collective-permute-start.3 = (f32[16]{0:T(128)S(1)}, f32[16]{0:T(128)S(1)}, u32[]{:S(2)}, u32[]{:S(2)}) collective-permute-start(f32[16]{0:T(128)S(1)} %mul.155), channel_id=1, source_target_pairs={{0,32},{4,36},{8,40},{12,44},{16,48},{20,52},{24,56},{28,60},{32,6... | collective-permute-start | bytes 200 | tf_op jit(solution)/shard_map/ppermute | solution.py:34
  117.6 33.1 %collective-permute-start.14 = (bf16[128,2,128]{2,0,1:T(8,128)(2,1)S(1)}, bf16[128,2,128]{2,0,1:T(8,128)(2,1)S(1)}, u32[]{:S(2)}, u32[]{:S(2)}) collective-permute-start(bf16[128,2,128]{2,0,1:T(8,128)(2,1)S(1)} %copy.48), channel_id=1, source_target_pairs={{0,12},{4,16},{8,20},{12,24},{16,28},{20,32},{24,36},{28,40},{32,4... | collective-permute-start | bytes 196616 | tf_op jit(solution)/shard_map/ppermute | solution.py:34
  123.0 6.7 %collective-permute-start.4 = (f32[16]{0:T(128)S(1)}, f32[16]{0:T(128)S(1)}, u32[]{:S(2)}, u32[]{:S(2)}) collective-permute-start(f32[16]{0:T(128)S(1)} %mul.156), channel_id=1, source_target_pairs={{0,64},{4,68},{8,72},{12,76},{16,80},{20,84},{24,88},{28,92},{32,9... | collective-permute-start | bytes 200 | tf_op jit(solution)/shard_map/ppermute | solution.py:34
  129.6 18.5 %collective-permute-start.9 = (bf16[16,128,128]{2,1,0:T(8,128)(2,1)S(1)}, bf16[16,128,128]{2,1,0:T(8,128)(2,1)S(1)}, u32[]{:S(2)}, u32[]{:S(2)}) collective-permute-start(bf16[16,128,128]{2,1,0:T(8,128)(2,1)S(1)} %fusion.32), channel_id=1, source_target_pairs={{0,64},{4,68},{8,72},{12,76},{16,80},{20,84},{24,88},{28,92},{32,9... | collective-permute-start | bytes 1572872 | tf_op jit(solution)/shard_map/ppermute | solution.py:34
  131.6 19.1 %collective-permute-start.15 = (bf16[128,2,128]{2,0,1:T(8,128)(2,1)S(1)}, bf16[128,2,128]{2,0,1:T(8,128)(2,1)S(1)}, u32[]{:S(2)}, u32[]{:S(2)}) collective-permute-start(bf16[128,2,128]{2,0,1:T(8,128)(2,1)S(1)} %copy.48), channel_id=1, source_target_pairs={{0,8},{4,12},{8,16},{12,20},{16,24},{20,28},{24,32},{28,36},{32,40... | collective-permute-start | bytes 196616 | tf_op jit(solution)/shard_map/ppermute | solution.py:34
  133.5 17.2 %collective-permute-start.16 = (bf16[128,2,128]{2,0,1:T(8,128)(2,1)S(1)}, bf16[128,2,128]{2,0,1:T(8,128)(2,1)S(1)}, u32[]{:S(2)}, u32[]{:S(2)}) collective-permute-start(bf16[128,2,128]{2,0,1:T(8,128)(2,1)S(1)} %copy.48), channel_id=1, source_target_pairs={{0,4},{4,8},{8,12},{12,16},{16,20},{20,24},{24,28},{28,32},{32,36}... | collective-permute-start | bytes 196616 | tf_op jit(solution)/shard_map/ppermute | solution.py:34
  148.5 9.9 %collective-permute-start.10 = (bf16[16,128,128]{2,1,0:T(8,128)(2,1)S(1)}, bf16[16,128,128]{2,1,0:T(8,128)(2,1)S(1)}, u32[]{:S(2)}, u32[]{:S(2)}) collective-permute-start(bf16[16,128,128]{2,1,0:T(8,128)(2,1)S(1)} %fusion.25), channel_id=1, source_target_pairs={{0,128},{4,132},{8,136},{12,140},{16,144},{20,148},{24,152},{28,15... | collective-permute-start | bytes 1572872 | tf_op jit(solution)/shard_map/ppermute | solution.py:34
  150.7 7.7 %copy-start.2 = (bf16[16,128,128]{2,1,0:T(8,128)(2,1)S(1)}, bf16[16,128,128]{2,1,0:T(8,128)(2,1)}, u32[]{:S(2)}) copy-start(bf16[16,128,128]{2,1,0:T(8,128)(2,1)} %copy-done.1) | copy-start | bytes 1572868
  152.1 8.1 %copy-start.3 = (bf16[128,16,128]{2,1,0:T(8,128)(2,1)S(1)}, bf16[128,16,128]{2,1,0:T(8,128)(2,1)}, u32[]{:S(2)}) copy-start(bf16[128,16,128]{2,1,0:T(8,128)(2,1)} %param.9) | copy-start | bytes 1572868
  152.1 8.6 %copy-start.5 = (f32[128,16,128]{0,2,1:T(8,128)S(1)}, f32[128,16,128]{0,2,1:T(8,128)}, u32[]{:S(2)}) copy-start(f32[128,16,128]{0,2,1:T(8,128)} %convolution_bitcast_fusion) | copy-start | bytes 3145732

commit v3 on v1

--- a/solution.py
+++ b/solution.py
@@ -1,26 +1,169 @@
+import functools
+
 import jax
 import jax.numpy as jnp
 from jax import lax
+from jax.experimental import pallas as pl
+from jax.experimental.pallas import tpu as pltpu
 from jax.sharding import PartitionSpec as P
+
+MESH = pl.DeviceIdType.MESH
 
 DH = 128
 HEADS = 64
 REACH = 3
 
 
-def exclusive_scan(element, axis, combine):
-    length, here = (lax.axis_size(axis), lax.axis_index(axis))
-    received = from_behind(element, axis, 1)
-    before = received
-    total = combine(received, element)
-    shift = 2
-    while shift < length:
-        received = from_behind(total, axis, shift)
-        before = combine(received, before)
-        if 2 * shift < length:
-            total = combine(received, total)
-        shift *= 2
-    return before
+def scan_kernel(
+    rounds,
+    chunks,
+    fall_ref,
+    state_ref,
+    sent0_ref,
+    out_ref,
+    whole,
+    whole_fall,
+    out_fall,
+    got,
+    got_fall,
+    outgoing,
+    outgoing_fall,
+    send_sem,
+    recv_sem,
+    fsend_sem,
+    frecv_sem,
+):
+    me = lax.axis_index("seq")
+    head = lax.axis_index("head")
+    length = 2**rounds
+    width = state_ref.shape[0] // chunks
+
+    def receives(k):
+        return (me - 2**k + length) // length
+
+    def can_send(k):
+        return 1 - (me + 2**k) // length
+
+    barrier = pltpu.get_barrier_semaphore()
+    partners = 0
+    for k in range(rounds):
+        ahead, behind = can_send(k), receives(k)
+        partners = partners + ahead + behind
+
+        @pl.when(ahead == 1)
+        def _():
+            pl.semaphore_signal(barrier, inc=1, device_id=(me + 2**k, head), device_id_type=MESH)
+
+        @pl.when(behind == 1)
+        def _():
+            pl.semaphore_signal(barrier, inc=1, device_id=(me - 2**k, head), device_id_type=MESH)
+
+    pl.semaphore_wait(barrier, partners)
+
+    def state_copy(k, c, source, device):
+        rows = pl.ds(c * width, width)
+        return pltpu.make_async_remote_copy(
+            src_ref=source.at[rows],
+            dst_ref=got.at[k, rows],
+            send_sem=send_sem.at[k, c],
+            recv_sem=recv_sem.at[k, c],
+            device_id=(device, head),
+            device_id_type=MESH,
+        )
+
+    def fall_copy(k, device):
+        return pltpu.make_async_remote_copy(
+            src_ref=outgoing_fall.at[k],
+            dst_ref=got_fall.at[k],
+            send_sem=fsend_sem.at[k],
+            recv_sem=frecv_sem.at[k],
+            device_id=(device, head),
+            device_id_type=MESH,
+        )
+
+    outgoing_fall[0] = fall_ref[...]
+
+    @pl.when(can_send(0) == 1)
+    def _():
+        fall_copy(0, me + 1).start()
+        for c in range(chunks):
+            state_copy(0, c, sent0_ref, me + 1).start()
+
+    whole[...] = state_ref[...]
+    whole_fall[...] = fall_ref[...]
+    out_ref[...] = jnp.zeros_like(out_ref)
+    out_fall[...] = jnp.ones_like(out_fall)
+    for k in range(rounds):
+        last = k == rounds - 1
+        for c in range(chunks):
+            rows = pl.ds(c * width, width)
+
+            @pl.when(receives(k) == 1)
+            def _():
+                state_copy(k, c, got.at[k], me - 2**k).wait_recv()
+                arrived = got[k, rows].astype(jnp.float32)
+                out_ref[rows] = out_fall[rows][:, None, :] * arrived + out_ref[rows]
+                if not last:
+                    whole[rows] = whole_fall[rows][:, None, :] * arrived + whole[rows]
+
+            if not last:
+
+                @pl.when(can_send(k + 1) == 1)
+                def _():
+                    outgoing[k + 1, rows] = whole[rows].astype(jnp.bfloat16)
+                    state_copy(k + 1, c, outgoing.at[k + 1], me + 2 ** (k + 1)).start()
+
+        @pl.when(receives(k) == 1)
+        def _():
+            fall_copy(k, me - 2**k).wait_recv()
+            arrived = got_fall[k]
+            out_fall[...] = arrived * out_fall[...]
+            if not last:
+                whole_fall[...] = arrived * whole_fall[...]
+
+        if not last:
+
+            @pl.when(can_send(k + 1) == 1)
+            def _():
+                outgoing_fall[k + 1] = whole_fall[...]
+                fall_copy(k + 1, me + 2 ** (k + 1)).start()
+
+    for k in range(rounds):
+
+        @pl.when(can_send(k) == 1)
+        def _():
+            fall_copy(k, me + 2**k).wait_send()
+            for c in range(chunks):
+                state_copy(k, c, got.at[k], me + 2**k).wait_send()
+
+
+def exclusive_scan(falling, state, axis):
+    length = lax.axis_size(axis)
+    rounds = length.bit_length() - 1
+    chunks = 4
+    heads, rows, columns = state.shape
+    fall_rows = jnp.broadcast_to(falling[:, None], (heads, columns))
+    vmem = pl.BlockSpec(memory_space=pltpu.VMEM)
+    return pl.pallas_call(
+        functools.partial(scan_kernel, rounds, chunks),
+        out_shape=jax.ShapeDtypeStruct(state.shape, jnp.float32),
+        in_specs=[vmem] * 3,
+        out_specs=vmem,
+        scratch_shapes=[
+            pltpu.VMEM(state.shape, jnp.float32),
+            pltpu.VMEM((heads, columns), jnp.float32),
+            pltpu.VMEM((heads, columns), jnp.float32),
+            pltpu.VMEM((rounds,) + state.shape, jnp.bfloat16),
+            pltpu.VMEM((rounds, heads, columns), jnp.float32),
+            pltpu.VMEM((rounds,) + state.shape, jnp.bfloat16),
+            pltpu.VMEM((rounds, heads, columns), jnp.float32),
+            pltpu.SemaphoreType.DMA((rounds, chunks)),
+            pltpu.SemaphoreType.DMA((rounds, chunks)),
+            pltpu.SemaphoreType.DMA((rounds,)),
+            pltpu.SemaphoreType.DMA((rounds,)),
+        ],
+        compiler_params=pltpu.CompilerParams(collective_id=0, has_side_effects=True),
+    )(fall_rows, state, state.astype(jnp.bfloat16))
 
 
 def from_behind(value, axis, steps):
@@ -84,7 +227,7 @@
         "egz,egc->gzc", key_product_lower, linear_value_rows, preferred_element_type=jnp.float32
     )
     falling = jnp.exp(cumulated[:, -1])
-    preceding_state = exclusive_scan((falling, recurrent_state), "seq", combine_states)[1]
+    preceding_state = exclusive_scan(falling, recurrent_state, "seq")
     lin_scores = jnp.einsum(
         "thd,shd->hts", linear_query_rows, lin_keys, preferred_element_type=jnp.float32
     )

time: 259 us -> 157 us (0.61)
  the two profiles are of different devices: /device:TPU:89 before, /device:TPU:60 now
where the time goes in v3:
time: 157 us; the launch traced here: 155 us
  Pallas kernels  98.1 us (62%)
  starting transfers between devices  25 us (16%)
  matrix products  12.7 us (8%)
  blocking collectives  7.27 us (5%)
  local copies, waits for them, and re-layouts  5.11 us (3%)
  other arithmetic  3.93 us (3%)
  waiting for transfers between devices  1.71 us (1%)
    pallas_call x1, Pallas kernels, exclusive_scan(): pl.pallas_call(functools.partial(scan_kernel, rounds, chunks), out_shape=...  98.1 us
    ppermute x6, starting transfers between devices, from_behind(): lax.ppermute(value, axis, [(source, source + steps) for source in range(f...  25 us
    psum x1, blocking collectives, body(): squares = lax.psum(jnp.sum(mixed * mixed, axis=(1, 2)), 'head')  7.27 us
    unnamed x16, local copies, waits for them, and re-layouts  4.15 us
  transfers between devices with their start and end apart: 6, of which 1 were waited for; matrix products, arithmetic and copies ran while one was open for 12% of the time, Pallas kernels for 63%

profile of v3, /device:TPU:60, one launch (start us, length us, event | category | flops | bytes accessed | tf_op | source)
XLA Modules:
  0.0 155.3 jit_solution(13100143240086810965)
XLA Ops:
  0.6 0.0 copy-start
  0.6 0.0 copy-start.3
  0.7 0.9 copy.43
  1.6 7.7 %collective-permute-start = (bf16[128,2,128]{2,0,1:T(8,128)(2,1)S(1)}, bf16[128,2,128]{2,0,1:T(8,128)(2,1)S(1)}, u32[]{:S(2)}, u32[]{:S(2)}) collective-permute-start(bf16[128,2,128]{2,0,1:T(8,128)(2,1)S(1)} %copy.43), channel_id=1, source_target_pairs={{0,12},{4,16},{8,20},{12,24},{16,28},{20,32},{24,36},{28,40},{32,4... | collective-permute-start | bytes 196616 | tf_op jit(solution)/shard_map/ppermute | solution.py:172
  9.3 3.4 %collective-permute-start.1 = (bf16[128,2,128]{2,0,1:T(8,128)(2,1)S(1)}, bf16[128,2,128]{2,0,1:T(8,128)(2,1)}, u32[]{:S(2)}, u32[]{:S(2)}) collective-permute-start(bf16[128,2,128]{2,0,1:T(8,128)(2,1)S(1)} %copy.43), channel_id=1, source_target_pairs={{0,8},{4,12},{8,16},{12,20},{16,24},{20,28},{24,32},{28,36},{32,40... | collective-permute-start | bytes 196616 | tf_op jit(solution)/shard_map/ppermute | solution.py:172
  12.7 2.9 %collective-permute-start.2 = (bf16[128,2,128]{2,0,1:T(8,128)(2,1)S(1)}, bf16[128,2,128]{2,0,1:T(8,128)(2,1)}, u32[]{:S(2)}, u32[]{:S(2)}) collective-permute-start(bf16[128,2,128]{2,0,1:T(8,128)(2,1)S(1)} %copy.43), channel_id=1, source_target_pairs={{0,4},{4,8},{8,12},{12,16},{16,20},{20,24},{24,28},{28,32},{32,36}... | collective-permute-start | bytes 196616 | tf_op jit(solution)/shard_map/ppermute | solution.py:172
  15.7 0.9 copy.48
  16.5 2.6 %collective-permute-start.3 = (bf16[128,2,128]{2,0,1:T(8,128)(2,1)S(1)}, bf16[128,2,128]{2,0,1:T(8,128)(2,1)S(1)}, u32[]{:S(2)}, u32[]{:S(2)}) collective-permute-start(bf16[128,2,128]{2,0,1:T(8,128)(2,1)S(1)} %copy.48), channel_id=1, source_target_pairs={{0,12},{4,16},{8,20},{12,24},{16,28},{20,32},{24,36},{28,40},{32,4... | collective-permute-start | bytes 196616 | tf_op jit(solution)/shard_map/ppermute | solution.py:172
  19.2 6.4 %collective-permute-start.4 = (bf16[128,2,128]{2,0,1:T(8,128)(2,1)S(1)}, bf16[128,2,128]{2,0,1:T(8,128)(2,1)S(1)}, u32[]{:S(2)}, u32[]{:S(2)}) collective-permute-start(bf16[128,2,128]{2,0,1:T(8,128)(2,1)S(1)} %copy.48), channel_id=1, source_target_pairs={{0,8},{4,12},{8,16},{12,20},{16,24},{20,28},{24,32},{28,36},{32,40... | collective-permute-start | bytes 196616 | tf_op jit(solution)/shard_map/ppermute | solution.py:172
  26.3 1.0 reduce_window_sum.11
  27.2 0.2 slice_reduce_fusion
  27.4 0.1 exponential_bitcast_fusion.1
  27.5 0.1 copy.34
  27.6 1.4 subtract_convert_fusion.1
  29.0 0.0 copy-start.2
  29.0 1.4 fusion.27
  30.5 1.5 fusion.70
  32.0 0.7 broadcast_in_dim.25.fall_ref
  32.6 98.1 %shard_map.104 = f32[16,128,128]{2,1,0:T(8,128)} custom-call(f32[16,128]{1,0:T(8,128)} %broadcast_in_dim.25.fall_ref, f32[16,128,128]{2,1,0:T(8,128)} %get-tuple-element.13.state_ref, bf16[16,128,128]{2,1,0:T(8,128)(2,1)} %get-tuple-element.12.sent0_ref), custom_call_target="tpu_custom_call" | custom-call | tf_op jit(solution)/shard_map/pallas_call | solution.py:147
  130.7 2.8 %fusion.36 = f32[16,128,128]{2,1,0:T(8,128)} fusion(bf16[128,16,128]{2,1,0:T(8,128)(2,1)S(1)} %copy-done.2, f32[16,128,128]{2,1,0:T(8,128)} %shard_map.104), kind=kOutput, calls=%fused_computation.41 | convolution fusion | flops 67371008 | bytes 2621440 | tf_op jit(solution)/shard_map/nwg,wgq->nwq/dot_general | solution.py:240
  133.6 1.9 %convolution_bitcast_fusion = f32[128,16,128]{0,2,1:T(8,128)} fusion(bf16[128,16,128]{2,1,0:T(8,128)(2,1)S(1)} %copy-done.4, f32[16,128]{1,0:T(8,128)S(1)} %reduce_window_sum.11, pred[128,128]{1,0:T(8,128)(4,1)S(1)} %iota_compare_fusion.1, bf16[128,16,128]{2,1,0:T(8,128)(2,1)S(1)} %copy-done.2, bf16[128,16,128]{2,1,0:T(8,128)(2,1)S(1)} %copy-done.3), kind=kOutput, calls=%fused_computation.15 | convolution fusion | flops 135266304 | bytes 2646016 | tf_op jit(solution)/shard_map/hts,shd->thd/dot_general | solution.py:236
  135.5 2.0 %multiply_reduce_fusion = (f32[128]{0:T(128)S(1)}, f32[128,16,128]{0,2,1:T(8,128)S(1)}) fusion(f32[128,16,128]{0,2,1:T(8,128)} %convolution_bitcast_fusion, f32[16,128,128]{2,1,0:T(8,128)} %fusion.36, bf16[128,16,128]{2,1,0:T(8,128)(2,1)S(1)} %copy-done.2, f32[16,128,128]{2,1,0:T(8,128)S(1)} %copy-done.1, f32[128,16]{0,1:T(8,128)S(1)} %get-tuple-element.10), kind=kOutput, calls=%fused_computation.21 | convolution fusion | flops 69468032 | bytes 4727296 | tf_op jit(solution)/shard_map/nwg,wgq->nwq/dot_general | solution.py:243
  137.5 7.3 %psum.7 = f32[128]{0:T(128)S(1)} all-reduce(f32[128]{0:T(128)S(1)} %get-tuple-element.14), channel_id=1, replica_groups=mesh['seq'=64,'head'=4] {'head'}, use_global_device_ids=true, to_apply=%region_2.3 | all-reduce | flops 128 | bytes 1024 | tf_op jit(solution)/shard_map/psum | solution.py:247
  144.8 0.3 multiply_convert_fusion
  145.2 0.3 fusion.56
  145.4 1.2 copy.53
  146.6 1.9 %collective-permute-start.5 = (bf16[128,2,128]{2,0,1:T(8,128)(2,1)S(1)}, bf16[128,2,128]{2,0,1:T(8,128)(2,1)S(1)}, u32[]{:S(2)}, u32[]{:S(2)}) collective-permute-start(bf16[128,2,128]{2,0,1:T(8,128)(2,1)S(1)} %copy.48), channel_id=1, source_target_pairs={{0,4},{4,8},{8,12},{12,16},{16,20},{20,24},{24,28},{28,32},{32,36}... | collective-permute-start | bytes 196616 | tf_op jit(solution)/shard_map/ppermute | solution.py:172
  148.6 1.6 %fusion.2 = (f32[2,8,128]{2,1,0:T(8,128)S(1)}, f32[2,512,128,8]{2,1,3,0:T(8,128)S(1)}) fusion(pred[128,512]{0,1:T(8,128)(4,1)S(1)} %fusion.56, bf16[128,2,8,128]{3,2,1,0:T(8,128)(2,1)S(1)} %bitcast.46, bf16[128,2,128]{2,0,1:T(8,128)(2,1)S(1)} %copy.43, bf16[128,2,128]{2,0,1:T(8,128)(2,1)} %collective-permute-done.2, ...), kind=kOutput, calls=%fused_computation.4 | convolution fusion | flops 272627712 | bytes 5054464 | tf_op jit(solution)/shard_map/cphm,npm->phcn/dot_general | solution.py:267
  150.2 0.9 fusion
  151.1 1.7 %collective-permute-done.5 = bf16[128,2,128]{2,0,1:T(8,128)(2,1)S(1)} collective-permute-done((bf16[128,2,128]{2,0,1:T(8,128)(2,1)S(1)}, bf16[128,2,128]{2,0,1:T(8,128)(2,1)S(1)}, u32[]{:S(2)}, u32[]{:S(2)}) %collective-permute-start.5) | collective-permute-done | bytes 65568 | tf_op jit(solution)/shard_map/ppermute | solution.py:172
  152.8 1.4 divide_convert_fusion
  154.2 1.1 copy.54
  (19 shorter events, 0.1 us)
Async XLA Ops:
  0.6 147.9 %copy-start = (bf16[128,16,128]{2,1,0:T(8,128)(2,1)S(1)}, bf16[128,16,128]{2,1,0:T(8,128)(2,1)}, u32[]{:S(2)}) copy-start(bf16[128,16,128]{2,1,0:T(8,128)(2,1)} %param.14) | copy-start | bytes 1572868
  0.6 29.8 %copy-start.3 = (bf16[128,16,128]{2,1,0:T(8,128)(2,1)S(1)}, bf16[128,16,128]{2,1,0:T(8,128)(2,1)}, u32[]{:S(2)}) copy-start(bf16[128,16,128]{2,1,0:T(8,128)(2,1)} %param.11) | copy-start | bytes 1572868
  1.6 145.0 %collective-permute-start = (bf16[128,2,128]{2,0,1:T(8,128)(2,1)S(1)}, bf16[128,2,128]{2,0,1:T(8,128)(2,1)S(1)}, u32[]{:S(2)}, u32[]{:S(2)}) collective-permute-start(bf16[128,2,128]{2,0,1:T(8,128)(2,1)S(1)} %copy.43), channel_id=1, source_target_pairs={{0,12},{4,16},{8,20},{12,24},{16,28},{20,32},{24,36},{28,40},{32,4... | collective-permute-start | bytes 196616 | tf_op jit(solution)/shard_map/ppermute | solution.py:172
  9.3 139.2 %collective-permute-start.1 = (bf16[128,2,128]{2,0,1:T(8,128)(2,1)S(1)}, bf16[128,2,128]{2,0,1:T(8,128)(2,1)}, u32[]{:S(2)}, u32[]{:S(2)}) collective-permute-start(bf16[128,2,128]{2,0,1:T(8,128)(2,1)S(1)} %copy.43), channel_id=1, source_target_pairs={{0,8},{4,12},{8,16},{12,20},{16,24},{20,28},{24,32},{28,36},{32,40... | collective-permute-start | bytes 196616 | tf_op jit(solution)/shard_map/ppermute | solution.py:172
  12.7 135.8 %collective-permute-start.2 = (bf16[128,2,128]{2,0,1:T(8,128)(2,1)S(1)}, bf16[128,2,128]{2,0,1:T(8,128)(2,1)}, u32[]{:S(2)}, u32[]{:S(2)}) collective-permute-start(bf16[128,2,128]{2,0,1:T(8,128)(2,1)S(1)} %copy.43), channel_id=1, source_target_pairs={{0,4},{4,8},{8,12},{12,16},{16,20},{20,24},{24,28},{28,32},{32,36}... | collective-permute-start | bytes 196616 | tf_op jit(solution)/shard_map/ppermute | solution.py:172
  16.5 134.5 %collective-permute-start.3 = (bf16[128,2,128]{2,0,1:T(8,128)(2,1)S(1)}, bf16[128,2,128]{2,0,1:T(8,128)(2,1)S(1)}, u32[]{:S(2)}, u32[]{:S(2)}) collective-permute-start(bf16[128,2,128]{2,0,1:T(8,128)(2,1)S(1)} %copy.48), channel_id=1, source_target_pairs={{0,12},{4,16},{8,20},{12,24},{16,28},{20,32},{24,36},{28,40},{32,4... | collective-permute-start | bytes 196616 | tf_op jit(solution)/shard_map/ppermute | solution.py:172
  19.2 131.9 %collective-permute-start.4 = (bf16[128,2,128]{2,0,1:T(8,128)(2,1)S(1)}, bf16[128,2,128]{2,0,1:T(8,128)(2,1)S(1)}, u32[]{:S(2)}, u32[]{:S(2)}) collective-permute-start(bf16[128,2,128]{2,0,1:T(8,128)(2,1)S(1)} %copy.48), channel_id=1, source_target_pairs={{0,8},{4,12},{8,16},{12,20},{16,24},{20,28},{24,32},{28,36},{32,40... | collective-permute-start | bytes 196616 | tf_op jit(solution)/shard_map/ppermute | solution.py:172
  29.0 101.7 %copy-start.2 = (bf16[128,16,128]{2,1,0:T(8,128)(2,1)S(1)}, bf16[128,16,128]{2,1,0:T(8,128)(2,1)}, u32[]{:S(2)}) copy-start(bf16[128,16,128]{2,1,0:T(8,128)(2,1)} %param.9) | copy-start | bytes 1572868
  30.5 103.1 %copy-start.4 = (bf16[128,16,128]{2,1,0:T(8,128)(2,1)S(1)}, bf16[128,16,128]{2,1,0:T(8,128)(2,1)}, u32[]{:S(2)}) copy-start(bf16[128,16,128]{2,1,0:T(8,128)(2,1)} %param.10) | copy-start | bytes 1572868
  130.7 4.7 %copy-start.1 = (f32[16,128,128]{2,1,0:T(8,128)S(1)}, f32[16,128,128]{2,1,0:T(8,128)}, u32[]{:S(2)}) copy-start(f32[16,128,128]{2,1,0:T(8,128)} %shard_map.104) | copy-start | bytes 3145732
  133.6 11.2 %copy-start.5 = (bf16[16,128]{1,0:T(8,128)(2,1)S(1)}, bf16[16,128]{1,0:T(8,128)(2,1)}, u32[]{:S(2)}) copy-start(bf16[16,128]{1,0:T(8,128)(2,1)} %param.13) | copy-start | bytes 12292
  146.6 6.1 %collective-permute-start.5 = (bf16[128,2,128]{2,0,1:T(8,128)(2,1)S(1)}, bf16[128,2,128]{2,0,1:T(8,128)(2,1)S(1)}, u32[]{:S(2)}, u32[]{:S(2)}) collective-permute-start(bf16[128,2,128]{2,0,1:T(8,128)(2,1)S(1)} %copy.48), channel_id=1, source_target_pairs={{0,4},{4,8},{8,12},{12,16},{16,20},{20,24},{24,28},{28,32},{32,36}... | collective-permute-start | bytes 196616 | tf_op jit(solution)/shard_map/ppermute | solution.py:172

commit v4 on v3

--- a/solution.py
+++ b/solution.py
@@ -17,10 +17,13 @@
 def scan_kernel(
     rounds,
     chunks,
+    reach,
     fall_ref,
     state_ref,
     sent0_ref,
+    kv_ref,
     out_ref,
+    kv_out,
     whole,
     whole_fall,
     out_fall,
@@ -32,6 +35,9 @@
     recv_sem,
     fsend_sem,
     frecv_sem,
+    kv_got,
+    kv_send,
+    kv_recv,
 ):
     me = lax.axis_index("seq")
     head = lax.axis_index("head")
@@ -44,21 +50,42 @@
     def can_send(k):
         return 1 - (me + 2**k) // length
 
+    def ahead(dist):
+        return 1 - (me + dist) // length
+
+    def behind(dist):
+        return (me - dist + length) // length
+
     barrier = pltpu.get_barrier_semaphore()
     partners = 0
-    for k in range(rounds):
-        ahead, behind = can_send(k), receives(k)
-        partners = partners + ahead + behind
-
-        @pl.when(ahead == 1)
-        def _():
-            pl.semaphore_signal(barrier, inc=1, device_id=(me + 2**k, head), device_id_type=MESH)
-
-        @pl.when(behind == 1)
-        def _():
-            pl.semaphore_signal(barrier, inc=1, device_id=(me - 2**k, head), device_id_type=MESH)
+    for dist in sorted(set([2**k for k in range(rounds)] + list(range(1, reach + 1)))):
+        partners = partners + ahead(dist) + behind(dist)
+
+        @pl.when(ahead(dist) == 1)
+        def _():
+            pl.semaphore_signal(barrier, inc=1, device_id=(me + dist, head), device_id_type=MESH)
+
+        @pl.when(behind(dist) == 1)
+        def _():
+            pl.semaphore_signal(barrier, inc=1, device_id=(me - dist, head), device_id_type=MESH)
 
     pl.semaphore_wait(barrier, partners)
+
+    def kv_copy(dist, device):
+        return pltpu.make_async_remote_copy(
+            src_ref=kv_ref,
+            dst_ref=kv_got.at[dist - 1],
+            send_sem=kv_send.at[dist - 1],
+            recv_sem=kv_recv.at[dist - 1],
+            device_id=(device, head),
+            device_id_type=MESH,
+        )
+
+    for dist in range(1, reach + 1):
+
+        @pl.when(ahead(dist) == 1)
+        def _():
+            kv_copy(dist, me + dist).start()
 
     def state_copy(k, c, source, device):
         rows = pl.ds(c * width, width)
@@ -128,6 +155,21 @@
                 outgoing_fall[k + 1] = whole_fall[...]
                 fall_copy(k + 1, me + 2 ** (k + 1)).start()
 
+    for dist in range(1, reach + 1):
+
+        @pl.when(behind(dist) == 1)
+        def _():
+            kv_copy(dist, me - dist).wait_recv()
+            kv_out[dist - 1] = kv_got[dist - 1]
+
+        @pl.when(behind(dist) == 0)
+        def _():
+            kv_out[dist - 1] = jnp.zeros_like(kv_out.at[dist - 1])
+
+        @pl.when(ahead(dist) == 1)
+        def _():
+            kv_copy(dist, me + dist).wait_send()
+
     for k in range(rounds):
 
         @pl.when(can_send(k) == 1)
@@ -137,7 +179,7 @@
                 state_copy(k, c, got.at[k], me + 2**k).wait_send()
 
 
-def exclusive_scan(falling, state, axis):
+def exclusive_scan(falling, state, kv, axis):
     length = lax.axis_size(axis)
     rounds = length.bit_length() - 1
     chunks = 4
@@ -145,10 +187,13 @@
     fall_rows = jnp.broadcast_to(falling[:, None], (heads, columns))
     vmem = pl.BlockSpec(memory_space=pltpu.VMEM)
     return pl.pallas_call(
-        functools.partial(scan_kernel, rounds, chunks),
-        out_shape=jax.ShapeDtypeStruct(state.shape, jnp.float32),
-        in_specs=[vmem] * 3,
-        out_specs=vmem,
+        functools.partial(scan_kernel, rounds, chunks, REACH),
+        out_shape=(
+            jax.ShapeDtypeStruct(state.shape, jnp.float32),
+            jax.ShapeDtypeStruct((REACH,) + kv.shape, kv.dtype),
+        ),
+        in_specs=[vmem] * 4,
+        out_specs=(vmem, vmem),
         scratch_shapes=[
             pltpu.VMEM(state.shape, jnp.float32),
             pltpu.VMEM((heads, columns), jnp.float32),
@@ -161,9 +206,72 @@
             pltpu.SemaphoreType.DMA((rounds, chunks)),
             pltpu.SemaphoreType.DMA((rounds,)),
             pltpu.SemaphoreType.DMA((rounds,)),
+            pltpu.VMEM((REACH,) + kv.shape, kv.dtype),
+            pltpu.SemaphoreType.DMA((REACH,)),
+            pltpu.SemaphoreType.DMA((REACH,)),
         ],
         compiler_params=pltpu.CompilerParams(collective_id=0, has_side_effects=True),
-    )(fall_rows, state, state.astype(jnp.bfloat16))
+    )(fall_rows, state, state.astype(jnp.bfloat16), kv)
+
+
+def head_sum_kernel(count, value_ref, out_ref, slots, send_sem, recv_sem):
+    me = lax.axis_index("seq")
+    head = lax.axis_index("head")
+    barrier = pltpu.get_barrier_semaphore()
+    for other in range(count):
+
+        @pl.when(other != head)
+        def _():
+            pl.semaphore_signal(barrier, inc=1, device_id=(me, other), device_id_type=MESH)
+
+    pl.semaphore_wait(barrier, count - 1)
+    slots[head] = value_ref[...]
+
+    def copy(other, slot):
+        return pltpu.make_async_remote_copy(
+            src_ref=value_ref,
+            dst_ref=slots.at[slot],
+            send_sem=send_sem.at[other],
+            recv_sem=recv_sem.at[slot],
+            device_id=(me, other),
+            device_id_type=MESH,
+        )
+
+    for other in range(count):
+
+        @pl.when(other != head)
+        def _():
+            copy(other, head).start()
+
+    for other in range(count):
+
+        @pl.when(other != head)
+        def _():
+            copy(other, other).wait_recv()
+            copy(other, head).wait_send()
+
+    total = slots[0]
+    for other in range(1, count):
+        total = total + slots[other]
+    out_ref[...] = total
+
+
+def head_sum(value, axis):
+    count = lax.axis_size(axis)
+    vmem = pl.BlockSpec(memory_space=pltpu.VMEM)
+    row = value.reshape(1, -1)
+    return pl.pallas_call(
+        functools.partial(head_sum_kernel, count),
+        out_shape=jax.ShapeDtypeStruct(row.shape, row.dtype),
+        in_specs=[vmem],
+        out_specs=vmem,
+        scratch_shapes=[
+            pltpu.VMEM((count,) + row.shape, row.dtype),
+            pltpu.SemaphoreType.DMA((count,)),
+            pltpu.SemaphoreType.DMA((count,)),
+        ],
+        compiler_params=pltpu.CompilerParams(collective_id=1, has_side_effects=True),
+    )(row).reshape(value.shape)
 
 
 def from_behind(value, axis, steps):
@@ -227,7 +335,9 @@
         "egz,egc->gzc", key_product_lower, linear_value_rows, preferred_element_type=jnp.float32
     )
     falling = jnp.exp(cumulated[:, -1])
-    preceding_state = exclusive_scan(falling, recurrent_state, "seq")
+    preceding_state, previous = exclusive_scan(
+        falling, recurrent_state, jnp.stack([soft_keys, soft_values]), "seq"
+    )
     lin_scores = jnp.einsum(
         "thd,shd->hts", linear_query_rows, lin_keys, preferred_element_type=jnp.float32
     )
@@ -244,7 +354,7 @@
         "nwg,wgq->nwq", linear_query_rows, preceding_lower, preferred_element_type=jnp.float32
     )
     mixed = local_part + jnp.exp(cumulated).T[:, :, None] * carried_part
-    squares = lax.psum(jnp.sum(mixed * mixed, axis=(1, 2)), "head")
+    squares = head_sum(jnp.sum(mixed * mixed, axis=(1, 2)), "head")
     lin_out = (
         mixed
         * lax.rsqrt(squares / (HEADS * DH) + 1e-06)[:, None, None]
@@ -256,9 +366,10 @@
     query_rows = soft_queries.reshape(row_count, kv_here, group, head_width)
     block_index = lax.axis_index("seq")
     first_block = window_start[0]
-    previous = [from_behind((soft_keys, soft_values), "seq", back) for back in range(REACH, 0, -1)]
-    all_keys = jnp.concatenate([p[0] for p in previous] + [soft_keys], axis=0)
-    all_values = jnp.concatenate([p[1] for p in previous] + [soft_values], axis=0)
+    all_keys = jnp.concatenate([previous[back, 0] for back in range(REACH - 1, -1, -1)] + [soft_keys], axis=0)
+    all_values = jnp.concatenate(
+        [previous[back, 1] for back in range(REACH - 1, -1, -1)] + [soft_values], axis=0
+    )
     key_index = jnp.arange((REACH + 1) * row_count, dtype=jnp.int32)
     key_block = block_index - REACH + key_index // row_count
     causal = (key_index % row_count)[None, :] <= token_locations[:, None]

time: 157 us -> 146 us (0.930)
  the two profiles are of different devices: /device:TPU:60 before, /device:TPU:216 now
where the time goes in v4:
time: 146 us
  Pallas kernels  120 us (82%)
  matrix products  10 us (7%)
  other arithmetic  9.32 us (6%)
  local copies, waits for them, and re-layouts  4.97 us (3%)
  between operations  1.51 us (1%)
    pallas_call x1, Pallas kernels, exclusive_scan(): pl.pallas_call(functools.partial(scan_kernel, rounds, chunks, REACH), out...  113 us
    pallas_call x1, Pallas kernels, head_sum(): pl.pallas_call(functools.partial(head_sum_kernel, count), out_shape=jax.S...  6.37 us
    dot_general x1, matrix products, body(): jnp.einsum('hts,shd->thd', lin_weights, linear_value_rows, preferred_elem...  3.22 us

profile of v4, /device:TPU:216, one launch (start us, length us, event | category | flops | bytes accessed | tf_op | source)
XLA Modules:
  0.0 145.6 jit_solution(6001075481188791687)
XLA Ops:
  0.6 0.0 copy-start
  0.6 0.0 copy-start.3
  1.4 0.3 copy-done
  1.7 1.0 reduce_window_sum.11
  2.7 0.2 slice_reduce_fusion
  2.9 0.7 broadcast_in_dim.25.fall_ref
  3.5 0.7 convert_element_type.51
  4.2 0.1 exponential_bitcast_fusion.1
  4.3 0.3 fusion.46
  4.6 0.1 copy.28
  4.7 1.7 %pad_maximum_fusion.kv_ref = bf16[2,128,2,128]{3,2,1,0:T(2,128)(2,1)} fusion(bf16[1,128,2,128]{3,2,1,0:T(2,128)(2,1)} %bitcast.57, bf16[1,128,2,128]{3,2,1,0:T(2,128)(2,1)} %bitcast.58), kind=kLoop, calls=%fused_computation.55 | loop fusion | flops 65536 | bytes 262144 | tf_op jit(solution)/shard_map/stack | solution.py:339
  6.4 1.4 subtract_convert_fusion.1
  7.8 3.2 %convolution_bitcast_fusion = f32[128,16,128]{0,2,1:T(8,128)} fusion(bf16[128,16,128]{2,1,0:T(8,128)(2,1)} %param.10, f32[16,128]{1,0:T(8,128)S(1)} %reduce_window_sum.11, pred[128,128]{1,0:T(8,128)(4,1)S(1)} %iota_compare_fusion.1, bf16[128,16,128]{2,1,0:T(8,128)(2,1)} %param.9, bf16[128,16,128]{2,1,0:T(8,128)(2,1)} %param.11), kind=kOutput, calls=%fused_computation.15 | convolution fusion | flops 135266304 | bytes 2646016 | tf_op jit(solution)/shard_map/hts,shd->thd/dot_general | solution.py:346
  11.0 0.0 copy-done.3
  11.0 0.3 fusion.27
  11.4 0.0 copy-start.4
  11.4 1.5 %fusion.58 = (bf16[16,128,128]{2,1,0:T(8,128)(2,1)}, f32[16,128,128]{2,1,0:T(8,128)}) fusion(f32[16,128,128]{2,1,0:T(8,128)S(1)} %fusion.27, bf16[128,16,128]{2,1,0:T(8,128)(2,1)S(1)} %copy-done.3, bf16[128,16,128]{2,1,0:T(8,128)(2,1)S(1)} %get-tuple-element.12), kind=kOutput, calls=%fused_computation.85 | convolution fusion | flops 67633152 | bytes 3670016 | tf_op jit(solution)/shard_map/egz,egc->gzc/dot_general | solution.py:334
  12.9 113.4 %shard_map.104 = (f32[16,128,128]{2,1,0:T(8,128)}, bf16[3,2,128,2,128]{4,3,2,1,0:T(2,128)(2,1)}) custom-call(f32[16,128]{1,0:T(8,128)} %broadcast_in_dim.25.fall_ref, f32[16,128,128]{2,1,0:T(8,128)} %get-tuple-element.23.state_ref, bf16[16,128,128]{2,1,0:T(8,128)(2,1)} %get-tuple-element.22.sent0_ref, bf16[2,128,2,128]{3,2,1,0:T(2,128)(2,1)} %pad_maximum_fusion.kv_ref), custom_call_target="tpu_custom_call" | custom-call | tf_op jit(solution)/shard_map/pallas_call | solution.py:189
  126.3 1.4 slice_bitcast_fusion.2
  127.7 0.0 copy-done.5
  127.7 2.3 %maximum_bitcast_fusion = (bf16[512,2,128,1]{2,1,0,3:T(2,128)(2,1)S(1)}, bf16[512,2,128,1]{2,1,0,3:T(2,128)(2,1)}) fusion(bf16[128,2,128]{2,1,0:T(2,128)(2,1)} %param.15, bf16[128,2,128]{2,1,0:T(2,128)(2,1)S(1)} %get-tuple-element.17, bf16[128,2,128]{2,1,0:T(2,128)(2,1)S(1)} %get-tuple-element.18, bf16[128,2,128]{2,1,0:T(2,128)(2,1)S(1)} %get-tuple-element.19, ...), kind=kLoop, calls=%fused_computation.46 | loop fusion | flops 786432 | bytes 1048576 | tf_op jit(solution)/shard_map/concatenate | solution.py:369
  130.0 1.7 %fusion.36 = f32[16,128,128]{2,1,0:T(8,128)S(1)} fusion(bf16[128,16,128]{2,1,0:T(8,128)(2,1)S(1)} %copy-done.2, f32[16,128,128]{2,1,0:T(8,128)} %get-tuple-element.4), kind=kOutput, calls=%fused_computation.41 | convolution fusion | flops 67371008 | bytes 2621440 | tf_op jit(solution)/shard_map/nwg,wgq->nwq/dot_general | solution.py:350
  131.7 0.0 copy-done.4
  131.7 1.0 multiply_reduce_fusion
  132.8 6.4 %shard_map.105 = f32[1,128]{1,0:T(1,128)} custom-call(f32[1,128]{1,0:T(1,128)} %bitcast.60), custom_call_target="tpu_custom_call" | custom-call | tf_op jit(solution)/shard_map/pallas_call | solution.py:263
  139.2 0.7 rsqrt_bitcast_fusion
  139.8 0.3 multiply_convert_fusion
  140.2 1.2 copy.41
  141.4 0.8 fusion.2
  142.2 0.9 fusion
  143.1 1.4 divide_convert_fusion
  144.4 1.1 copy.42
  (10 shorter events, 0.0 us)
Async XLA Ops:
  0.6 1.1 copy-start
  0.6 10.4 %copy-start.3 = (bf16[128,16,128]{2,1,0:T(8,128)(2,1)S(1)}, bf16[128,16,128]{2,1,0:T(8,128)(2,1)}, u32[]{:S(2)}) copy-start(bf16[128,16,128]{2,1,0:T(8,128)(2,1)} %param.11) | copy-start | bytes 1572868
  11.0 116.6 %copy-start.5 = (bf16[128,2,128]{2,1,0:T(2,128)(2,1)S(1)}, bf16[128,2,128]{2,1,0:T(2,128)(2,1)}, u32[]{:S(2)}) copy-start(bf16[128,2,128]{2,1,0:T(2,128)(2,1)} %param.16) | copy-start | bytes 196612
  11.0 119.0 %copy-start.2 = (bf16[128,16,128]{2,1,0:T(8,128)(2,1)S(1)}, bf16[128,16,128]{2,1,0:T(8,128)(2,1)}, u32[]{:S(2)}) copy-start(bf16[128,16,128]{2,1,0:T(8,128)(2,1)} %param.9) | copy-start | bytes 1572868
  11.4 120.3 %copy-start.4 = (f32[128,16,128]{0,2,1:T(8,128)S(1)}, f32[128,16,128]{0,2,1:T(8,128)}, u32[]{:S(2)}) copy-start(f32[128,16,128]{0,2,1:T(8,128)} %convolution_bitcast_fusion) | copy-start | bytes 3145732
  126.3 5.4 %copy-start.1 = (f32[16,128,128]{2,1,0:T(8,128)S(1)}, f32[16,128,128]{2,1,0:T(8,128)}, u32[]{:S(2)}) copy-start(f32[16,128,128]{2,1,0:T(8,128)} %get-tuple-element.4) | copy-start | bytes 3145732
  141.4 1.7 %copy-start.6 = (bf16[512,2,128,1]{2,1,0,3:T(2,128)(2,1)S(1)}, bf16[512,2,128,1]{2,1,0,3:T(2,128)(2,1)}, u32[]{:S(2)}) copy-start(bf16[512,2,128,1]{2,1,0,3:T(2,128)(2,1)} %get-tuple-element.31) | copy-start | bytes 786436

commit v5 on v4

--- a/solution.py
+++ b/solution.py
@@ -182,7 +182,7 @@
 def exclusive_scan(falling, state, kv, axis):
     length = lax.axis_size(axis)
     rounds = length.bit_length() - 1
-    chunks = 4
+    chunks = 8
     heads, rows, columns = state.shape
     fall_rows = jnp.broadcast_to(falling[:, None], (heads, columns))
     vmem = pl.BlockSpec(memory_space=pltpu.VMEM)

time: 146 us -> 145 us (level)
  the two profiles are of different devices: /device:TPU:216 before, /device:TPU:60 now
where the time goes in v5:
time: 145 us; the launch traced here: 142 us
  Pallas kernels  116 us (80%)
  matrix products  10 us (7%)
  other arithmetic  9.32 us (6%)
  local copies, waits for them, and re-layouts  4.97 us (3%)
  between operations  1.51 us (1%)
    pallas_call x1, Pallas kernels, exclusive_scan(): pl.pallas_call(functools.partial(scan_kernel, rounds, chunks, REACH), out...  110 us
    pallas_call x1, Pallas kernels, head_sum(): pl.pallas_call(functools.partial(head_sum_kernel, count), out_shape=jax.S...  6.37 us
    dot_general x1, matrix products, body(): jnp.einsum('hts,shd->thd', lin_weights, linear_value_rows, preferred_elem...  3.22 us

profile of v5, /device:TPU:60, one launch (start us, length us, event | category | flops | bytes accessed | tf_op | source)
XLA Modules:
  0.0 142.2 jit_solution(9135934110136418375)
XLA Ops:
  0.6 0.0 copy-start
  0.6 0.0 copy-start.3
  1.4 0.3 copy-done
  1.7 1.0 reduce_window_sum.11
  2.7 0.2 slice_reduce_fusion
  2.9 0.7 broadcast_in_dim.25.fall_ref
  3.5 0.7 convert_element_type.51
  4.2 0.1 exponential_bitcast_fusion.1
  4.3 0.3 fusion.46
  4.6 0.1 copy.28
  4.7 1.7 %pad_maximum_fusion.kv_ref = bf16[2,128,2,128]{3,2,1,0:T(2,128)(2,1)} fusion(bf16[1,128,2,128]{3,2,1,0:T(2,128)(2,1)} %bitcast.57, bf16[1,128,2,128]{3,2,1,0:T(2,128)(2,1)} %bitcast.58), kind=kLoop, calls=%fused_computation.55 | loop fusion | flops 65536 | bytes 262144 | tf_op jit(solution)/shard_map/stack | solution.py:339
  6.4 1.4 subtract_convert_fusion.1
  7.8 3.2 %convolution_bitcast_fusion = f32[128,16,128]{0,2,1:T(8,128)} fusion(bf16[128,16,128]{2,1,0:T(8,128)(2,1)} %param.10, f32[16,128]{1,0:T(8,128)S(1)} %reduce_window_sum.11, pred[128,128]{1,0:T(8,128)(4,1)S(1)} %iota_compare_fusion.1, bf16[128,16,128]{2,1,0:T(8,128)(2,1)} %param.9, bf16[128,16,128]{2,1,0:T(8,128)(2,1)} %param.11), kind=kOutput, calls=%fused_computation.15 | convolution fusion | flops 135266304 | bytes 2646016 | tf_op jit(solution)/shard_map/hts,shd->thd/dot_general | solution.py:346
  11.0 0.0 copy-done.3
  11.0 0.3 fusion.27
  11.4 0.0 copy-start.4
  11.4 1.5 %fusion.58 = (bf16[16,128,128]{2,1,0:T(8,128)(2,1)}, f32[16,128,128]{2,1,0:T(8,128)}) fusion(f32[16,128,128]{2,1,0:T(8,128)S(1)} %fusion.27, bf16[128,16,128]{2,1,0:T(8,128)(2,1)S(1)} %copy-done.3, bf16[128,16,128]{2,1,0:T(8,128)(2,1)S(1)} %get-tuple-element.12), kind=kOutput, calls=%fused_computation.85 | convolution fusion | flops 67633152 | bytes 3670016 | tf_op jit(solution)/shard_map/egz,egc->gzc/dot_general | solution.py:334
  12.9 110.1 %shard_map.104 = (f32[16,128,128]{2,1,0:T(8,128)}, bf16[3,2,128,2,128]{4,3,2,1,0:T(2,128)(2,1)}) custom-call(f32[16,128]{1,0:T(8,128)} %broadcast_in_dim.25.fall_ref, f32[16,128,128]{2,1,0:T(8,128)} %get-tuple-element.23.state_ref, bf16[16,128,128]{2,1,0:T(8,128)(2,1)} %get-tuple-element.22.sent0_ref, bf16[2,128,2,128]{3,2,1,0:T(2,128)(2,1)} %pad_maximum_fusion.kv_ref), custom_call_target="tpu_custom_call" | custom-call | tf_op jit(solution)/shard_map/pallas_call | solution.py:189
  123.0 0.0 copy-start.1
  123.0 1.4 slice_bitcast_fusion.2
  124.3 0.0 copy-done.5
  124.4 2.3 %maximum_bitcast_fusion = (bf16[512,2,128,1]{2,1,0,3:T(2,128)(2,1)S(1)}, bf16[512,2,128,1]{2,1,0,3:T(2,128)(2,1)}) fusion(bf16[128,2,128]{2,1,0:T(2,128)(2,1)} %param.15, bf16[128,2,128]{2,1,0:T(2,128)(2,1)S(1)} %get-tuple-element.17, bf16[128,2,128]{2,1,0:T(2,128)(2,1)S(1)} %get-tuple-element.18, bf16[128,2,128]{2,1,0:T(2,128)(2,1)S(1)} %get-tuple-element.19, ...), kind=kLoop, calls=%fused_computation.46 | loop fusion | flops 786432 | bytes 1048576 | tf_op jit(solution)/shard_map/concatenate | solution.py:369
  126.7 1.7 %fusion.36 = f32[16,128,128]{2,1,0:T(8,128)S(1)} fusion(bf16[128,16,128]{2,1,0:T(8,128)(2,1)S(1)} %copy-done.2, f32[16,128,128]{2,1,0:T(8,128)} %get-tuple-element.4), kind=kOutput, calls=%fused_computation.41 | convolution fusion | flops 67371008 | bytes 2621440 | tf_op jit(solution)/shard_map/nwg,wgq->nwq/dot_general | solution.py:350
  128.4 1.0 multiply_reduce_fusion
  129.4 6.4 %shard_map.105 = f32[1,128]{1,0:T(1,128)} custom-call(f32[1,128]{1,0:T(1,128)} %bitcast.60), custom_call_target="tpu_custom_call" | custom-call | tf_op jit(solution)/shard_map/pallas_call | solution.py:263
  135.8 0.7 rsqrt_bitcast_fusion
  136.5 0.3 multiply_convert_fusion
  136.9 1.2 copy.41
  138.0 0.8 fusion.2
  138.9 0.9 fusion
  139.7 1.4 divide_convert_fusion
  141.1 1.1 copy.42
  (10 shorter events, 0.0 us)
Async XLA Ops:
  0.6 1.1 copy-start
  0.6 10.4 %copy-start.3 = (bf16[128,16,128]{2,1,0:T(8,128)(2,1)S(1)}, bf16[128,16,128]{2,1,0:T(8,128)(2,1)}, u32[]{:S(2)}) copy-start(bf16[128,16,128]{2,1,0:T(8,128)(2,1)} %param.11) | copy-start | bytes 1572868
  11.0 113.3 %copy-start.5 = (bf16[128,2,128]{2,1,0:T(2,128)(2,1)S(1)}, bf16[128,2,128]{2,1,0:T(2,128)(2,1)}, u32[]{:S(2)}) copy-start(bf16[128,2,128]{2,1,0:T(2,128)(2,1)} %param.16) | copy-start | bytes 196612
  11.0 115.6 %copy-start.2 = (bf16[128,16,128]{2,1,0:T(8,128)(2,1)S(1)}, bf16[128,16,128]{2,1,0:T(8,128)(2,1)}, u32[]{:S(2)}) copy-start(bf16[128,16,128]{2,1,0:T(8,128)(2,1)} %param.9) | copy-start | bytes 1572868
  11.4 117.0 %copy-start.4 = (f32[128,16,128]{0,2,1:T(8,128)S(1)}, f32[128,16,128]{0,2,1:T(8,128)}, u32[]{:S(2)}) copy-start(f32[128,16,128]{0,2,1:T(8,128)} %convolution_bitcast_fusion) | copy-start | bytes 3145732
  123.0 5.4 %copy-start.1 = (f32[16,128,128]{2,1,0:T(8,128)S(1)}, f32[16,128,128]{2,1,0:T(8,128)}, u32[]{:S(2)}) copy-start(f32[16,128,128]{2,1,0:T(8,128)} %get-tuple-element.4) | copy-start | bytes 3145732
  138.0 1.7 %copy-start.6 = (bf16[512,2,128,1]{2,1,0,3:T(2,128)(2,1)S(1)}, bf16[512,2,128,1]{2,1,0,3:T(2,128)(2,1)}, u32[]{:S(2)}) copy-start(bf16[512,2,128,1]{2,1,0,3:T(2,128)(2,1)} %get-tuple-element.31) | copy-start | bytes 786436

commit v6 on v5

--- a/solution.py
+++ b/solution.py
@@ -15,18 +15,22 @@
 
 
 def scan_kernel(
+    line,
     rounds,
     chunks,
     reach,
     fall_ref,
     state_ref,
-    sent0_ref,
     kv_ref,
     out_ref,
     kv_out,
     whole,
     whole_fall,
     out_fall,
+    inline,
+    inline_fall,
+    before_fall,
+    after_fall,
     got,
     got_fall,
     outgoing,
@@ -41,14 +45,10 @@
 ):
     me = lax.axis_index("seq")
     head = lax.axis_index("head")
-    length = 2**rounds
+    length = line * 2**rounds
     width = state_ref.shape[0] // chunks
-
-    def receives(k):
-        return (me - 2**k + length) // length
-
-    def can_send(k):
-        return 1 - (me + 2**k) // length
+    z = me % line
+    forward, backward, diagonal = 0, 1, 2
 
     def ahead(dist):
         return 1 - (me + dist) // length
@@ -56,9 +56,15 @@
     def behind(dist):
         return (me - dist + length) // length
 
+    not_first = (z + line - 1) // line
+    not_last = 1 - (z + 1) // line
+    diag_send = not_first * ahead(line - 1)
+    diag_recv = not_last * behind(line - 1)
+
     barrier = pltpu.get_barrier_semaphore()
     partners = 0
-    for dist in sorted(set([2**k for k in range(rounds)] + list(range(1, reach + 1)))):
+    distances = [line - 1] + [line * 2**r for r in range(rounds)] + list(range(1, reach + 1))
+    for dist in sorted(set(distances)):
         partners = partners + ahead(dist) + behind(dist)
 
         @pl.when(ahead(dist) == 1)
@@ -87,73 +93,192 @@
         def _():
             kv_copy(dist, me + dist).start()
 
-    def state_copy(k, c, source, device):
+    def state_copy(stage, source, c, device):
         rows = pl.ds(c * width, width)
         return pltpu.make_async_remote_copy(
-            src_ref=source.at[rows],
-            dst_ref=got.at[k, rows],
-            send_sem=send_sem.at[k, c],
-            recv_sem=recv_sem.at[k, c],
+            src_ref=outgoing.at[source, rows],
+            dst_ref=got.at[stage, rows],
+            send_sem=send_sem.at[stage, c],
+            recv_sem=recv_sem.at[stage, c],
             device_id=(device, head),
             device_id_type=MESH,
         )
 
-    def fall_copy(k, device):
+    def fall_copy(stage, source, device):
         return pltpu.make_async_remote_copy(
-            src_ref=outgoing_fall.at[k],
-            dst_ref=got_fall.at[k],
-            send_sem=fsend_sem.at[k],
-            recv_sem=frecv_sem.at[k],
+            src_ref=outgoing_fall.at[source],
+            dst_ref=got_fall.at[stage],
+            send_sem=fsend_sem.at[stage],
+            recv_sem=frecv_sem.at[stage],
             device_id=(device, head),
             device_id_type=MESH,
         )
 
-    outgoing_fall[0] = fall_ref[...]
-
-    @pl.when(can_send(0) == 1)
+    def forward_fall():
+        before_fall[...] = jnp.ones_like(before_fall)
+
+        @pl.when(not_first == 1)
+        def _():
+            fall_copy(forward, forward, me - 1).wait_recv()
+            before_fall[...] = got_fall[forward]
+
+        inline_fall[...] = before_fall[...] * fall_ref[...]
+
+        @pl.when(not_last == 1)
+        def _():
+            outgoing_fall[forward] = inline_fall[...]
+            fall_copy(forward, forward, me + 1).start()
+
+    def backward_fall():
+        after_fall[...] = jnp.ones_like(after_fall)
+
+        @pl.when(not_last == 1)
+        def _():
+            fall_copy(backward, backward, me + 1).wait_recv()
+            after_fall[...] = got_fall[backward]
+
+        @pl.when(not_first == 1)
+        def _():
+            outgoing_fall[backward] = fall_ref[...] * after_fall[...]
+            fall_copy(backward, backward, me - 1).start()
+
+        @pl.when(diag_send == 1)
+        def _():
+            fall_copy(diagonal, backward, me + line - 1).start()
+
+    def forward_chunk(c):
+        rows = pl.ds(c * width, width)
+        out_ref[rows] = jnp.zeros_like(out_ref.at[rows])
+
+        @pl.when(not_first == 1)
+        def _():
+            state_copy(forward, forward, c, me - 1).wait_recv()
+            out_ref[rows] = got[forward, rows].astype(jnp.float32)
+
+        inline[rows] = fall_ref[rows][:, None, :] * out_ref[rows] + state_ref[rows]
+
+        @pl.when(not_last == 1)
+        def _():
+            outgoing[forward, rows] = inline[rows].astype(jnp.bfloat16)
+            state_copy(forward, forward, c, me + 1).start()
+
+    def backward_chunk(c):
+        rows = pl.ds(c * width, width)
+
+        @pl.when(not_last == 1)
+        def _():
+            state_copy(backward, backward, c, me + 1).wait_recv()
+
+        @pl.when(not_first == 1)
+        def _():
+            @pl.when(not_last == 1)
+            def _():
+                later = got[backward, rows].astype(jnp.float32)
+                total = after_fall[rows][:, None, :] * state_ref[rows] + later
+                outgoing[backward, rows] = total.astype(jnp.bfloat16)
+
+            @pl.when(not_last == 0)
+            def _():
+                outgoing[backward, rows] = state_ref[rows].astype(jnp.bfloat16)
+
+            state_copy(backward, backward, c, me - 1).start()
+
+            @pl.when(diag_send == 1)
+            def _():
+                state_copy(diagonal, backward, c, me + line - 1).start()
+
+    def chains(forward_first):
+        if forward_first:
+            forward_fall()
+            backward_fall()
+        else:
+            backward_fall()
+            forward_fall()
+        for c in range(chunks):
+            if forward_first:
+                forward_chunk(c)
+                backward_chunk(c)
+            else:
+                backward_chunk(c)
+                forward_chunk(c)
+
+    @pl.when(z < line // 2)
     def _():
-        fall_copy(0, me + 1).start()
-        for c in range(chunks):
-            state_copy(0, c, sent0_ref, me + 1).start()
-
-    whole[...] = state_ref[...]
-    whole_fall[...] = fall_ref[...]
-    out_ref[...] = jnp.zeros_like(out_ref)
-    out_fall[...] = jnp.ones_like(out_fall)
-    for k in range(rounds):
-        last = k == rounds - 1
+        chains(True)
+
+    @pl.when(z >= line // 2)
+    def _():
+        chains(False)
+
+    whole_fall[...] = inline_fall[...]
+    out_fall[...] = before_fall[...]
+
+    @pl.when(diag_recv == 1)
+    def _():
+        fall_copy(diagonal, backward, me - line + 1).wait_recv()
+        whole_fall[...] = got_fall[diagonal] * inline_fall[...]
+        out_fall[...] = got_fall[diagonal] * before_fall[...]
+
+    first_stage = 3
+    if rounds > 0:
+
+        @pl.when(ahead(line) == 1)
+        def _():
+            outgoing_fall[first_stage] = whole_fall[...]
+            fall_copy(first_stage, first_stage, me + line).start()
+
+    for c in range(chunks):
+        rows = pl.ds(c * width, width)
+        whole[rows] = inline[rows]
+
+        @pl.when(diag_recv == 1)
+        def _():
+            state_copy(diagonal, backward, c, me - line + 1).wait_recv()
+            earlier = got[diagonal, rows].astype(jnp.float32)
+            whole[rows] = inline_fall[rows][:, None, :] * earlier + inline[rows]
+            out_ref[rows] = before_fall[rows][:, None, :] * earlier + out_ref[rows]
+
+        if rounds > 0:
+
+            @pl.when(ahead(line) == 1)
+            def _():
+                outgoing[first_stage, rows] = whole[rows].astype(jnp.bfloat16)
+                state_copy(first_stage, first_stage, c, me + line).start()
+
+    for r in range(rounds):
+        stage, shift, last = first_stage + r, line * 2**r, r == rounds - 1
         for c in range(chunks):
             rows = pl.ds(c * width, width)
 
-            @pl.when(receives(k) == 1)
+            @pl.when(behind(shift) == 1)
             def _():
-                state_copy(k, c, got.at[k], me - 2**k).wait_recv()
-                arrived = got[k, rows].astype(jnp.float32)
+                state_copy(stage, stage, c, me - shift).wait_recv()
+                arrived = got[stage, rows].astype(jnp.float32)
                 out_ref[rows] = out_fall[rows][:, None, :] * arrived + out_ref[rows]
                 if not last:
                     whole[rows] = whole_fall[rows][:, None, :] * arrived + whole[rows]
 
             if not last:
 
-                @pl.when(can_send(k + 1) == 1)
+                @pl.when(ahead(2 * shift) == 1)
                 def _():
-                    outgoing[k + 1, rows] = whole[rows].astype(jnp.bfloat16)
-                    state_copy(k + 1, c, outgoing.at[k + 1], me + 2 ** (k + 1)).start()
-
-        @pl.when(receives(k) == 1)
-        def _():
-            fall_copy(k, me - 2**k).wait_recv()
-            arrived = got_fall[k]
+                    outgoing[stage + 1, rows] = whole[rows].astype(jnp.bfloat16)
+                    state_copy(stage + 1, stage + 1, c, me + 2 * shift).start()
+
+        @pl.when(behind(shift) == 1)
+        def _():
+            fall_copy(stage, stage, me - shift).wait_recv()
+            arrived = got_fall[stage]
             out_fall[...] = arrived * out_fall[...]
             if not last:
                 whole_fall[...] = arrived * whole_fall[...]
 
         if not last:
 
-            @pl.when(can_send(k + 1) == 1)
+            @pl.when(ahead(2 * shift) == 1)
             def _():
-                outgoing_fall[k + 1] = whole_fall[...]
-                fall_copy(k + 1, me + 2 ** (k + 1)).start()
+                outgoing_fall[stage + 1] = whole_fall[...]
+                fall_copy(stage + 1, stage + 1, me + 2 * shift).start()
 
     for dist in range(1, reach + 1):
 
@@ -170,48 +295,57 @@
         def _():
             kv_copy(dist, me + dist).wait_send()
 
-    for k in range(rounds):
-
-        @pl.when(can_send(k) == 1)
-        def _():
-            fall_copy(k, me + 2**k).wait_send()
+    sends = [(forward, forward, 1, not_last), (backward, backward, -1, not_first)]
+    sends.append((diagonal, backward, line - 1, diag_send))
+    sends += [(first_stage + r, first_stage + r, line * 2**r, ahead(line * 2**r)) for r in range(rounds)]
+    for stage, source, dist, flag in sends:
+
+        @pl.when(flag == 1)
+        def _():
+            fall_copy(stage, source, me + dist).wait_send()
             for c in range(chunks):
-                state_copy(k, c, got.at[k], me + 2**k).wait_send()
+                state_copy(stage, source, c, me + dist).wait_send()
 
 
 def exclusive_scan(falling, state, kv, axis):
+    line = 8
     length = lax.axis_size(axis)
-    rounds = length.bit_length() - 1
+    rounds = (length // line).bit_length() - 1
+    stages = 3 + rounds
     chunks = 8
     heads, rows, columns = state.shape
     fall_rows = jnp.broadcast_to(falling[:, None], (heads, columns))
     vmem = pl.BlockSpec(memory_space=pltpu.VMEM)
     return pl.pallas_call(
-        functools.partial(scan_kernel, rounds, chunks, REACH),
+        functools.partial(scan_kernel, line, rounds, chunks, REACH),
         out_shape=(
             jax.ShapeDtypeStruct(state.shape, jnp.float32),
             jax.ShapeDtypeStruct((REACH,) + kv.shape, kv.dtype),
         ),
-        in_specs=[vmem] * 4,
+        in_specs=[vmem] * 3,
         out_specs=(vmem, vmem),
         scratch_shapes=[
             pltpu.VMEM(state.shape, jnp.float32),
             pltpu.VMEM((heads, columns), jnp.float32),
             pltpu.VMEM((heads, columns), jnp.float32),
-            pltpu.VMEM((rounds,) + state.shape, jnp.bfloat16),
-            pltpu.VMEM((rounds, heads, columns), jnp.float32),
-            pltpu.VMEM((rounds,) + state.shape, jnp.bfloat16),
-            pltpu.VMEM((rounds, heads, columns), jnp.float32),
-            pltpu.SemaphoreType.DMA((rounds, chunks)),
-            pltpu.SemaphoreType.DMA((rounds, chunks)),
-            pltpu.SemaphoreType.DMA((rounds,)),
-            pltpu.SemaphoreType.DMA((rounds,)),
+            pltpu.VMEM(state.shape, jnp.float32),
+            pltpu.VMEM((heads, columns), jnp.float32),
+            pltpu.VMEM((heads, columns), jnp.float32),
+            pltpu.VMEM((heads, columns), jnp.float32),
+            pltpu.VMEM((stages,) + state.shape, jnp.bfloat16),
+            pltpu.VMEM((stages, heads, columns), jnp.float32),
+            pltpu.VMEM((stages,) + state.shape, jnp.bfloat16),
+            pltpu.VMEM((stages, heads, columns), jnp.float32),
+            pltpu.SemaphoreType.DMA((stages, chunks)),
+            pltpu.SemaphoreType.DMA((stages, chunks)),
+            pltpu.SemaphoreType.DMA((stages,)),
+            pltpu.SemaphoreType.DMA((stages,)),
             pltpu.VMEM((REACH,) + kv.shape, kv.dtype),
             pltpu.SemaphoreType.DMA((REACH,)),
             pltpu.SemaphoreType.DMA((REACH,)),
         ],
         compiler_params=pltpu.CompilerParams(collective_id=0, has_side_effects=True),
-    )(fall_rows, state, state.astype(jnp.bfloat16), kv)
+    )(fall_rows, state, kv)
 
 
 def head_sum_kernel(count, value_ref, out_ref, slots, send_sem, recv_sem):

time: 145 us -> 285 us (1.97)
  Pallas kernels: 116 us -> 256 us
    pallas_call x1, Pallas kernels: 110 us -> 249 us  [exclusive_scan(): pl.pallas_call(functools.partial(scan_kernel, line, rounds, chunks, REACH...]
where the time goes in v6:
time: 285 us; the launch traced here: 281 us
  Pallas kernels  256 us (90%)
  matrix products  9.84 us (3%)
  other arithmetic  8.48 us (3%)
  local copies, waits for them, and re-layouts  4.98 us (2%)
    pallas_call x1, Pallas kernels, exclusive_scan(): pl.pallas_call(functools.partial(scan_kernel, line, rounds, chunks, REACH...  249 us
    pallas_call x1, Pallas kernels, head_sum(): pl.pallas_call(functools.partial(head_sum_kernel, count), out_shape=jax.S...  6.37 us

profile of v6, /device:TPU:60, one launch (start us, length us, event | category | flops | bytes accessed | tf_op | source)
XLA Modules:
  0.0 280.6 jit_solution(3896697330338924062)
XLA Ops:
  0.6 0.0 copy-start
  0.6 0.0 copy-start.3
  1.4 0.3 copy-done
  1.7 1.0 reduce_window_sum.11
  2.7 0.2 slice_reduce_fusion
  2.9 0.7 broadcast_in_dim.25.fall_ref
  3.5 0.7 convert_element_type.47
  4.2 0.1 exponential_bitcast_fusion.1
  4.3 0.3 fusion.46
  4.6 0.1 copy.28
  4.7 1.7 pad_maximum_fusion.kv_ref
  6.4 1.4 subtract_convert_fusion.1
  7.8 3.2 %convolution_bitcast_fusion = f32[128,16,128]{0,2,1:T(8,128)} fusion(bf16[128,16,128]{2,1,0:T(8,128)(2,1)} %param.10, f32[16,128]{1,0:T(8,128)S(1)} %reduce_window_sum.11, pred[128,128]{1,0:T(8,128)(4,1)S(1)} %iota_compare_fusion.1, bf16[128,16,128]{2,1,0:T(8,128)(2,1)} %param.9, bf16[128,16,128]{2,1,0:T(8,128)(2,1)} %param.11), kind=kOutput, calls=%fused_computation.15 | convolution fusion | flops 135266304 | bytes 2646016 | tf_op jit(solution)/shard_map/hts,shd->thd/dot_general | solution.py:480
  11.0 0.0 copy-done.3
  11.0 0.3 fusion.27
  11.4 0.0 copy-start.6
  11.4 1.3 convolution_add_fusion.1.state_ref
  12.8 249.4 %shard_map.104 = (f32[16,128,128]{2,1,0:T(8,128)}, bf16[3,2,128,2,128]{4,3,2,1,0:T(2,128)(2,1)}) custom-call(f32[16,128]{1,0:T(8,128)} %broadcast_in_dim.25.fall_ref, f32[16,128,128]{2,1,0:T(8,128)} %convolution_add_fusion.1.state_ref, bf16[2,128,2,128]{3,2,1,0:T(2,128)(2,1)} %pad_maximum_fusion.kv_ref), custom_call_target="tpu_custom_call" | custom-call | tf_op jit(solution)/shard_map/pallas_call | solution.py:319
  262.1 0.0 copy-start.1
  262.1 1.4 slice_bitcast_fusion.2
  263.5 1.5 maximum_bitcast_fusion
  265.0 1.7 fusion.36
  266.7 0.0 copy-done.4
  266.7 1.0 multiply_reduce_fusion
  267.8 6.4 %shard_map.105 = f32[1,128]{1,0:T(1,128)} custom-call(f32[1,128]{1,0:T(1,128)} %bitcast.60), custom_call_target="tpu_custom_call" | custom-call | tf_op jit(solution)/shard_map/pallas_call | solution.py:397
  274.1 0.7 rsqrt_bitcast_fusion
  274.8 0.3 multiply_convert_fusion
  275.2 1.2 copy.41
  276.4 0.8 fusion.2
  277.2 0.9 fusion
  278.0 1.4 divide_convert_fusion
  279.4 1.1 copy.42
  (12 shorter events, 0.0 us)
Async XLA Ops:
  0.6 1.1 copy-start
  0.6 10.4 %copy-start.3 = (bf16[128,16,128]{2,1,0:T(8,128)(2,1)S(1)}, bf16[128,16,128]{2,1,0:T(8,128)(2,1)}, u32[]{:S(2)}) copy-start(bf16[128,16,128]{2,1,0:T(8,128)(2,1)} %param.11) | copy-start | bytes 1572868
  11.0 252.5 %copy-start.5 = (bf16[128,2,128]{2,1,0:T(2,128)(2,1)S(1)}, bf16[128,2,128]{2,1,0:T(2,128)(2,1)}, u32[]{:S(2)}) copy-start(bf16[128,2,128]{2,1,0:T(2,128)(2,1)} %param.16) | copy-start | bytes 196612
  11.0 253.9 %copy-start.2 = (bf16[128,16,128]{2,1,0:T(8,128)(2,1)S(1)}, bf16[128,16,128]{2,1,0:T(8,128)(2,1)}, u32[]{:S(2)}) copy-start(bf16[128,16,128]{2,1,0:T(8,128)(2,1)} %param.9) | copy-start | bytes 1572868
  11.4 252.1 %copy-start.6 = (bf16[128,2,128]{2,1,0:T(2,128)(2,1)S(1)}, bf16[128,2,128]{2,1,0:T(2,128)(2,1)}, u32[]{:S(2)}) copy-start(bf16[128,2,128]{2,1,0:T(2,128)(2,1)} %param.15) | copy-start | bytes 196612
  12.8 254.0 %copy-start.4 = (f32[128,16,128]{0,2,1:T(8,128)S(1)}, f32[128,16,128]{0,2,1:T(8,128)}, u32[]{:S(2)}) copy-start(f32[128,16,128]{0,2,1:T(8,128)} %convolution_bitcast_fusion) | copy-start | bytes 3145732
  262.1 4.6 %copy-start.1 = (f32[16,128,128]{2,1,0:T(8,128)S(1)}, f32[16,128,128]{2,1,0:T(8,128)}, u32[]{:S(2)}) copy-start(f32[16,128,128]{2,1,0:T(8,128)} %get-tuple-element.4) | copy-start | bytes 3145732
  276.4 1.7 copy-start.7

commit v7 on v5

--- a/solution.py
+++ b/solution.py
@@ -27,6 +27,8 @@
     whole,
     whole_fall,
     out_fall,
+    suffix,
+    suffix_fall,
     got,
     got_fall,
     outgoing,
@@ -43,12 +45,8 @@
     head = lax.axis_index("head")
     length = 2**rounds
     width = state_ref.shape[0] // chunks
-
-    def receives(k):
-        return (me - 2**k + length) // length
-
-    def can_send(k):
-        return 1 - (me + 2**k) // length
+    jump = 7
+    back0, back1, near = rounds, rounds + 1, rounds + 2
 
     def ahead(dist):
         return 1 - (me + dist) // length
@@ -56,9 +54,14 @@
     def behind(dist):
         return (me - dist + length) // length
 
+    far_recv = behind(jump)
+    near_recv = behind(4) * (1 - far_recv)
+    near_send = 1 - (me + length - 3) // length
+
     barrier = pltpu.get_barrier_semaphore()
     partners = 0
-    for dist in sorted(set([2**k for k in range(rounds)] + list(range(1, reach + 1)))):
+    distances = [2**k for k in range(rounds)] + list(range(1, reach + 1)) + [jump]
+    for dist in sorted(set(distances)):
         partners = partners + ahead(dist) + behind(dist)
 
         @pl.when(ahead(dist) == 1)
@@ -87,62 +90,153 @@
         def _():
             kv_copy(dist, me + dist).start()
 
-    def state_copy(k, c, source, device):
+    def state_copy(stage, source, c, device):
         rows = pl.ds(c * width, width)
         return pltpu.make_async_remote_copy(
             src_ref=source.at[rows],
-            dst_ref=got.at[k, rows],
-            send_sem=send_sem.at[k, c],
-            recv_sem=recv_sem.at[k, c],
+            dst_ref=got.at[stage, rows],
+            send_sem=send_sem.at[stage, c],
+            recv_sem=recv_sem.at[stage, c],
             device_id=(device, head),
             device_id_type=MESH,
         )
 
-    def fall_copy(k, device):
+    def fall_copy(stage, source, device):
         return pltpu.make_async_remote_copy(
-            src_ref=outgoing_fall.at[k],
-            dst_ref=got_fall.at[k],
-            send_sem=fsend_sem.at[k],
-            recv_sem=frecv_sem.at[k],
+            src_ref=source,
+            dst_ref=got_fall.at[stage],
+            send_sem=fsend_sem.at[stage],
+            recv_sem=frecv_sem.at[stage],
             device_id=(device, head),
             device_id_type=MESH,
         )
 
     outgoing_fall[0] = fall_ref[...]
 
-    @pl.when(can_send(0) == 1)
+    @pl.when(ahead(1) == 1)
     def _():
-        fall_copy(0, me + 1).start()
+        fall_copy(0, outgoing_fall.at[0], me + 1).start()
         for c in range(chunks):
-            state_copy(0, c, sent0_ref, me + 1).start()
+            state_copy(0, sent0_ref, c, me + 1).start()
+
+    @pl.when(behind(1) == 1)
+    def _():
+        fall_copy(back0, outgoing_fall.at[0], me - 1).start()
+        for c in range(chunks):
+            state_copy(back0, sent0_ref, c, me - 1).start()
 
     whole[...] = state_ref[...]
     whole_fall[...] = fall_ref[...]
+    suffix[...] = state_ref[...]
+    suffix_fall[...] = fall_ref[...]
     out_ref[...] = jnp.zeros_like(out_ref)
     out_fall[...] = jnp.ones_like(out_fall)
-    for k in range(rounds):
-        last = k == rounds - 1
+
+    def forward_fall(stage, shift):
+        @pl.when(behind(shift) == 1)
+        def _():
+            fall_copy(stage, outgoing_fall.at[stage], me - shift).wait_recv()
+            arrived = got_fall[stage]
+            out_fall[...] = arrived * out_fall[...]
+            whole_fall[...] = arrived * whole_fall[...]
+
+    def forward_chunk(stage, shift, c, update_whole=True):
+        rows = pl.ds(c * width, width)
+
+        @pl.when(behind(shift) == 1)
+        def _():
+            state_copy(stage, outgoing.at[stage], c, me - shift).wait_recv()
+            arrived = got[stage, rows].astype(jnp.float32)
+            out_ref[rows] = out_fall[rows][:, None, :] * arrived + out_ref[rows]
+            if update_whole:
+                whole[rows] = whole_fall[rows][:, None, :] * arrived + whole[rows]
+
+    def backward_fall(stage, shift):
+        @pl.when(ahead(shift) == 1)
+        def _():
+            fall_copy(stage, outgoing_fall.at[stage], me + shift).wait_recv()
+
+    def backward_chunk(stage, shift, c):
+        rows = pl.ds(c * width, width)
+
+        @pl.when(ahead(shift) == 1)
+        def _():
+            state_copy(stage, outgoing.at[stage], c, me + shift).wait_recv()
+            arrived = got[stage, rows].astype(jnp.float32)
+            suffix[rows] = got_fall[stage][rows][:, None, :] * suffix[rows] + arrived
+
+    def backward_fall_update(stage, shift):
+        @pl.when(ahead(shift) == 1)
+        def _():
+            suffix_fall[...] = suffix_fall[...] * got_fall[stage]
+
+    def send(stage, flag, buffer, buffer_fall, dist, c):
+        rows = pl.ds(c * width, width)
+
+        @pl.when(flag == 1)
+        def _():
+            if c == 0:
+                outgoing_fall[stage] = buffer_fall[...]
+                fall_copy(stage, outgoing_fall.at[stage], me + dist).start()
+            outgoing[stage, rows] = buffer[rows].astype(jnp.bfloat16)
+            state_copy(stage, outgoing.at[stage], c, me + dist).start()
+
+    for stage, back, shift in ((0, back0, 1), (1, back1, 2)):
+        backward_fall(back, shift)
         for c in range(chunks):
             rows = pl.ds(c * width, width)
-
-            @pl.when(receives(k) == 1)
+            forward_chunk(stage, shift, c)
+            backward_chunk(back, shift, c)
+        forward_fall(stage, shift)
+        backward_fall_update(back, shift)
+        if stage == 0:
+            for c in range(chunks):
+                send(1, ahead(2), whole, whole_fall, 2, c)
+                send(back1, behind(2), suffix, suffix_fall, -2, c)
+        else:
+            for c in range(chunks):
+                send(2, ahead(jump), suffix, suffix_fall, jump, c)
+                send(near, near_send, whole, whole_fall, 4, c)
+
+    for c in range(chunks):
+        rows = pl.ds(c * width, width)
+        for flag, dist, stage in ((far_recv, jump, 2), (near_recv, 4, near)):
+
+            @pl.when(flag == 1)
             def _():
-                state_copy(k, c, got.at[k], me - 2**k).wait_recv()
-                arrived = got[k, rows].astype(jnp.float32)
+                state_copy(stage, outgoing.at[stage], c, me - dist).wait_recv()
+                arrived = got[stage, rows].astype(jnp.float32)
                 out_ref[rows] = out_fall[rows][:, None, :] * arrived + out_ref[rows]
-                if not last:
-                    whole[rows] = whole_fall[rows][:, None, :] * arrived + whole[rows]
-
+                whole[rows] = whole_fall[rows][:, None, :] * arrived + whole[rows]
+
+    for flag, dist, stage in ((far_recv, jump, 2), (near_recv, 4, near)):
+
+        @pl.when(flag == 1)
+        def _():
+            fall_copy(stage, outgoing_fall.at[stage], me - dist).wait_recv()
+            arrived = got_fall[stage]
+            out_fall[...] = arrived * out_fall[...]
+            whole_fall[...] = arrived * whole_fall[...]
+
+    if rounds > 3:
+        for c in range(chunks):
+            send(3, ahead(8), whole, whole_fall, 8, c)
+
+    for k in range(3, rounds):
+        shift, last = 2**k, k == rounds - 1
+        for c in range(chunks):
+            forward_chunk(k, shift, c, update_whole=not last)
             if not last:
-
-                @pl.when(can_send(k + 1) == 1)
+                rows = pl.ds(c * width, width)
+
+                @pl.when(ahead(2 * shift) == 1)
                 def _():
                     outgoing[k + 1, rows] = whole[rows].astype(jnp.bfloat16)
-                    state_copy(k + 1, c, outgoing.at[k + 1], me + 2 ** (k + 1)).start()
-
-        @pl.when(receives(k) == 1)
-        def _():
-            fall_copy(k, me - 2**k).wait_recv()
+                    state_copy(k + 1, outgoing.at[k + 1], c, me + 2 * shift).start()
+
+        @pl.when(behind(shift) == 1)
+        def _():
+            fall_copy(k, outgoing_fall.at[k], me - shift).wait_recv()
             arrived = got_fall[k]
             out_fall[...] = arrived * out_fall[...]
             if not last:
@@ -150,10 +244,10 @@
 
         if not last:
 
-            @pl.when(can_send(k + 1) == 1)
+            @pl.when(ahead(2 * shift) == 1)
             def _():
                 outgoing_fall[k + 1] = whole_fall[...]
-                fall_copy(k + 1, me + 2 ** (k + 1)).start()
+                fall_copy(k + 1, outgoing_fall.at[k + 1], me + 2 * shift).start()
 
     for dist in range(1, reach + 1):
 
@@ -170,18 +264,22 @@
         def _():
             kv_copy(dist, me + dist).wait_send()
 
-    for k in range(rounds):
-
-        @pl.when(can_send(k) == 1)
-        def _():
-            fall_copy(k, me + 2**k).wait_send()
+    sends = [(0, 1, ahead(1)), (back0, -1, behind(1)), (1, 2, ahead(2)), (back1, -2, behind(2))]
+    sends += [(2, jump, ahead(jump)), (near, 4, near_send)]
+    sends += [(k, 2**k, ahead(2**k)) for k in range(3, rounds)]
+    for stage, dist, flag in sends:
+
+        @pl.when(flag == 1)
+        def _():
+            fall_copy(stage, outgoing_fall.at[stage], me + dist).wait_send()
             for c in range(chunks):
-                state_copy(k, c, got.at[k], me + 2**k).wait_send()
+                state_copy(stage, outgoing.at[stage], c, me + dist).wait_send()
 
 
 def exclusive_scan(falling, state, kv, axis):
     length = lax.axis_size(axis)
     rounds = length.bit_length() - 1
+    stages = rounds + 3
     chunks = 8
     heads, rows, columns = state.shape
     fall_rows = jnp.broadcast_to(falling[:, None], (heads, columns))
@@ -198,14 +296,16 @@
             pltpu.VMEM(state.shape, jnp.float32),
             pltpu.VMEM((heads, columns), jnp.float32),
             pltpu.VMEM((heads, columns), jnp.float32),
-            pltpu.VMEM((rounds,) + state.shape, jnp.bfloat16),
-            pltpu.VMEM((rounds, heads, columns), jnp.float32),
-            pltpu.VMEM((rounds,) + state.shape, jnp.bfloat16),
-            pltpu.VMEM((rounds, heads, columns), jnp.float32),
-            pltpu.SemaphoreType.DMA((rounds, chunks)),
-            pltpu.SemaphoreType.DMA((rounds, chunks)),
-            pltpu.SemaphoreType.DMA((rounds,)),
-            pltpu.SemaphoreType.DMA((rounds,)),
+            pltpu.VMEM(state.shape, jnp.float32),
+            pltpu.VMEM((heads, columns), jnp.float32),
+            pltpu.VMEM((stages,) + state.shape, jnp.bfloat16),
+            pltpu.VMEM((stages, heads, columns), jnp.float32),
+            pltpu.VMEM((stages,) + state.shape, jnp.bfloat16),
+            pltpu.VMEM((stages, heads, columns), jnp.float32),
+            pltpu.SemaphoreType.DMA((stages, chunks)),
+            pltpu.SemaphoreType.DMA((stages, chunks)),
+            pltpu.SemaphoreType.DMA((stages,)),
+            pltpu.SemaphoreType.DMA((stages,)),
             pltpu.VMEM((REACH,) + kv.shape, kv.dtype),
             pltpu.SemaphoreType.DMA((REACH,)),
             pltpu.SemaphoreType.DMA((REACH,)),

time: 145 us -> 156 us (1.076)
  the two profiles are of different devices: /device:TPU:60 before, /device:TPU:188 now
where the time goes in v7:
time: 156 us
  Pallas kernels  130 us (83%)
  matrix products  10 us (6%)
  other arithmetic  9.32 us (6%)
  local copies, waits for them, and re-layouts  4.97 us (3%)
    pallas_call x1, Pallas kernels, exclusive_scan(): pl.pallas_call(functools.partial(scan_kernel, rounds, chunks, REACH), out...  123 us
    pallas_call x1, Pallas kernels, head_sum(): pl.pallas_call(functools.partial(head_sum_kernel, count), out_shape=jax.S...  6.37 us
    dot_general x1, matrix products, body(): jnp.einsum('hts,shd->thd', lin_weights, linear_value_rows, preferred_elem...  3.22 us

profile of v7, /device:TPU:188, one launch (start us, length us, event | category | flops | bytes accessed | tf_op | source)
XLA Modules:
  0.0 155.6 jit_solution(1983400495998924664)
XLA Ops:
  0.6 0.0 copy-start
  0.6 0.0 copy-start.3
  1.4 0.3 copy-done
  1.7 1.0 reduce_window_sum.11
  2.7 0.2 slice_reduce_fusion
  2.9 0.7 broadcast_in_dim.25.fall_ref
  3.5 0.7 convert_element_type.51
  4.2 0.1 exponential_bitcast_fusion.1
  4.3 0.3 fusion.46
  4.6 0.1 copy.28
  4.7 1.7 %pad_maximum_fusion.kv_ref = bf16[2,128,2,128]{3,2,1,0:T(2,128)(2,1)} fusion(bf16[1,128,2,128]{3,2,1,0:T(2,128)(2,1)} %bitcast.57, bf16[1,128,2,128]{3,2,1,0:T(2,128)(2,1)} %bitcast.58), kind=kLoop, calls=%fused_computation.55 | loop fusion | flops 65536 | bytes 262144 | tf_op jit(solution)/shard_map/stack | solution.py:439
  6.4 1.4 subtract_convert_fusion.1
  7.8 3.2 %convolution_bitcast_fusion = f32[128,16,128]{0,2,1:T(8,128)} fusion(bf16[128,16,128]{2,1,0:T(8,128)(2,1)} %param.10, f32[16,128]{1,0:T(8,128)S(1)} %reduce_window_sum.11, pred[128,128]{1,0:T(8,128)(4,1)S(1)} %iota_compare_fusion.1, bf16[128,16,128]{2,1,0:T(8,128)(2,1)} %param.9, bf16[128,16,128]{2,1,0:T(8,128)(2,1)} %param.11), kind=kOutput, calls=%fused_computation.15 | convolution fusion | flops 135266304 | bytes 2646016 | tf_op jit(solution)/shard_map/hts,shd->thd/dot_general | solution.py:446
  11.0 0.0 copy-done.3
  11.0 0.3 fusion.27
  11.4 0.0 copy-start.4
  11.4 1.5 fusion.58
  12.9 123.4 %shard_map.104 = (f32[16,128,128]{2,1,0:T(8,128)}, bf16[3,2,128,2,128]{4,3,2,1,0:T(2,128)(2,1)}) custom-call(f32[16,128]{1,0:T(8,128)} %broadcast_in_dim.25.fall_ref, f32[16,128,128]{2,1,0:T(8,128)} %get-tuple-element.23.state_ref, bf16[16,128,128]{2,1,0:T(8,128)(2,1)} %get-tuple-element.22.sent0_ref, bf16[2,128,2,128]{3,2,1,0:T(2,128)(2,1)} %pad_maximum_fusion.kv_ref), custom_call_target="tpu_custom_call" | custom-call | tf_op jit(solution)/shard_map/pallas_call | solution.py:287
  136.4 1.4 slice_bitcast_fusion.2
  137.7 2.3 %maximum_bitcast_fusion = (bf16[512,2,128,1]{2,1,0,3:T(2,128)(2,1)S(1)}, bf16[512,2,128,1]{2,1,0,3:T(2,128)(2,1)}) fusion(bf16[128,2,128]{2,1,0:T(2,128)(2,1)} %param.15, bf16[128,2,128]{2,1,0:T(2,128)(2,1)S(1)} %get-tuple-element.17, bf16[128,2,128]{2,1,0:T(2,128)(2,1)S(1)} %get-tuple-element.18, bf16[128,2,128]{2,1,0:T(2,128)(2,1)S(1)} %get-tuple-element.19, ...), kind=kLoop, calls=%fused_computation.46 | loop fusion | flops 786432 | bytes 1048576 | tf_op jit(solution)/shard_map/concatenate | solution.py:469
  140.0 0.0 copy-done.2
  140.0 1.7 %fusion.36 = f32[16,128,128]{2,1,0:T(8,128)S(1)} fusion(bf16[128,16,128]{2,1,0:T(8,128)(2,1)S(1)} %copy-done.2, f32[16,128,128]{2,1,0:T(8,128)} %get-tuple-element.4), kind=kOutput, calls=%fused_computation.41 | convolution fusion | flops 67371008 | bytes 2621440 | tf_op jit(solution)/shard_map/nwg,wgq->nwq/dot_general | solution.py:450
  141.8 0.0 copy-done.4
  141.8 1.0 multiply_reduce_fusion
  142.8 6.4 %shard_map.105 = f32[1,128]{1,0:T(1,128)} custom-call(f32[1,128]{1,0:T(1,128)} %bitcast.60), custom_call_target="tpu_custom_call" | custom-call | tf_op jit(solution)/shard_map/pallas_call | solution.py:363
  149.2 0.7 rsqrt_bitcast_fusion
  149.9 0.3 multiply_convert_fusion
  150.2 1.2 copy.41
  151.4 0.8 fusion.2
  152.2 0.9 fusion
  153.1 1.4 divide_convert_fusion
  154.5 1.1 copy.42
  (10 shorter events, 0.0 us)
Async XLA Ops:
  0.6 1.1 copy-start
  0.6 10.4 %copy-start.3 = (bf16[128,16,128]{2,1,0:T(8,128)(2,1)S(1)}, bf16[128,16,128]{2,1,0:T(8,128)(2,1)}, u32[]{:S(2)}) copy-start(bf16[128,16,128]{2,1,0:T(8,128)(2,1)} %param.11) | copy-start | bytes 1572868
  11.0 126.7 %copy-start.5 = (bf16[128,2,128]{2,1,0:T(2,128)(2,1)S(1)}, bf16[128,2,128]{2,1,0:T(2,128)(2,1)}, u32[]{:S(2)}) copy-start(bf16[128,2,128]{2,1,0:T(2,128)(2,1)} %param.16) | copy-start | bytes 196612
  11.0 129.0 %copy-start.2 = (bf16[128,16,128]{2,1,0:T(8,128)(2,1)S(1)}, bf16[128,16,128]{2,1,0:T(8,128)(2,1)}, u32[]{:S(2)}) copy-start(bf16[128,16,128]{2,1,0:T(8,128)(2,1)} %param.9) | copy-start | bytes 1572868
  11.4 130.4 %copy-start.4 = (f32[128,16,128]{0,2,1:T(8,128)S(1)}, f32[128,16,128]{0,2,1:T(8,128)}, u32[]{:S(2)}) copy-start(f32[128,16,128]{0,2,1:T(8,128)} %convolution_bitcast_fusion) | copy-start | bytes 3145732
  136.3 5.4 %copy-start.1 = (f32[16,128,128]{2,1,0:T(8,128)S(1)}, f32[16,128,128]{2,1,0:T(8,128)}, u32[]{:S(2)}) copy-start(f32[16,128,128]{2,1,0:T(8,128)} %get-tuple-element.4) | copy-start | bytes 3145732
  151.4 1.7 %copy-start.6 = (bf16[512,2,128,1]{2,1,0,3:T(2,128)(2,1)S(1)}, bf16[512,2,128,1]{2,1,0,3:T(2,128)(2,1)}, u32[]{:S(2)}) copy-start(bf16[512,2,128,1]{2,1,0,3:T(2,128)(2,1)} %get-tuple-element.31) | copy-start | bytes 786436

commit v8 on v7

--- a/solution.py
+++ b/solution.py
@@ -155,6 +155,7 @@
         @pl.when(ahead(shift) == 1)
         def _():
             fall_copy(stage, outgoing_fall.at[stage], me + shift).wait_recv()
+            suffix_fall[...] = suffix_fall[...] * got_fall[stage]
 
     def backward_chunk(stage, shift, c):
         rows = pl.ds(c * width, width)
@@ -165,38 +166,39 @@
             arrived = got[stage, rows].astype(jnp.float32)
             suffix[rows] = got_fall[stage][rows][:, None, :] * suffix[rows] + arrived
 
-    def backward_fall_update(stage, shift):
-        @pl.when(ahead(shift) == 1)
-        def _():
-            suffix_fall[...] = suffix_fall[...] * got_fall[stage]
-
-    def send(stage, flag, buffer, buffer_fall, dist, c):
+    def send_chunk(stage, flag, buffer, dist, c):
         rows = pl.ds(c * width, width)
 
         @pl.when(flag == 1)
         def _():
-            if c == 0:
-                outgoing_fall[stage] = buffer_fall[...]
-                fall_copy(stage, outgoing_fall.at[stage], me + dist).start()
             outgoing[stage, rows] = buffer[rows].astype(jnp.bfloat16)
             state_copy(stage, outgoing.at[stage], c, me + dist).start()
 
-    for stage, back, shift in ((0, back0, 1), (1, back1, 2)):
-        backward_fall(back, shift)
-        for c in range(chunks):
-            rows = pl.ds(c * width, width)
-            forward_chunk(stage, shift, c)
-            backward_chunk(back, shift, c)
-        forward_fall(stage, shift)
-        backward_fall_update(back, shift)
-        if stage == 0:
-            for c in range(chunks):
-                send(1, ahead(2), whole, whole_fall, 2, c)
-                send(back1, behind(2), suffix, suffix_fall, -2, c)
-        else:
-            for c in range(chunks):
-                send(2, ahead(jump), suffix, suffix_fall, jump, c)
-                send(near, near_send, whole, whole_fall, 4, c)
+    def send_fall(stage, flag, buffer_fall, dist):
+        @pl.when(flag == 1)
+        def _():
+            outgoing_fall[stage] = buffer_fall[...]
+            fall_copy(stage, outgoing_fall.at[stage], me + dist).start()
+
+    backward_fall(back0, 1)
+    send_fall(back1, behind(2), suffix_fall, -2)
+    for c in range(chunks):
+        forward_chunk(0, 1, c)
+        send_chunk(1, ahead(2), whole, 2, c)
+        backward_chunk(back0, 1, c)
+        send_chunk(back1, behind(2), suffix, -2, c)
+    forward_fall(0, 1)
+    send_fall(1, ahead(2), whole_fall, 2)
+
+    backward_fall(back1, 2)
+    send_fall(2, ahead(jump), suffix_fall, jump)
+    for c in range(chunks):
+        forward_chunk(1, 2, c)
+        send_chunk(near, near_send, whole, 4, c)
+        backward_chunk(back1, 2, c)
+        send_chunk(2, ahead(jump), suffix, jump, c)
+    forward_fall(1, 2)
+    send_fall(near, near_send, whole_fall, 4)
 
     for c in range(chunks):
         rows = pl.ds(c * width, width)
@@ -209,6 +211,9 @@
                 out_ref[rows] = out_fall[rows][:, None, :] * arrived + out_ref[rows]
                 whole[rows] = whole_fall[rows][:, None, :] * arrived + whole[rows]
 
+        if rounds > 3:
+            send_chunk(3, ahead(8), whole, 8, c)
+
     for flag, dist, stage in ((far_recv, jump, 2), (near_recv, 4, near)):
 
         @pl.when(flag == 1)
@@ -219,8 +224,7 @@
             whole_fall[...] = arrived * whole_fall[...]
 
     if rounds > 3:
-        for c in range(chunks):
-            send(3, ahead(8), whole, whole_fall, 8, c)
+        send_fall(3, ahead(8), whole_fall, 8)
 
     for k in range(3, rounds):
         shift, last = 2**k, k == rounds - 1

time: 156 us -> 140 us (0.90)
  the two profiles are of different devices: /device:TPU:188 before, /device:TPU:60 now
where the time goes in v8:
time: 140 us; the launch traced here: 139 us
  Pallas kernels  114 us (81%)
  matrix products  10 us (7%)
  other arithmetic  9.32 us (7%)
  local copies, waits for them, and re-layouts  4.97 us (4%)
  between operations  1.51 us (1%)
    pallas_call x1, Pallas kernels, exclusive_scan(): pl.pallas_call(functools.partial(scan_kernel, rounds, chunks, REACH), out...  107 us
    pallas_call x1, Pallas kernels, head_sum(): pl.pallas_call(functools.partial(head_sum_kernel, count), out_shape=jax.S...  6.37 us
    dot_general x1, matrix products, body(): jnp.einsum('hts,shd->thd', lin_weights, linear_value_rows, preferred_elem...  3.22 us

profile of v8, /device:TPU:60, one launch (start us, length us, event | category | flops | bytes accessed | tf_op | source)
XLA Modules:
  0.0 139.5 jit_solution(11621410937152006885)
XLA Ops:
  0.6 0.0 copy-start
  0.6 0.0 copy-start.3
  1.4 0.3 copy-done
  1.7 1.0 reduce_window_sum.11
  2.7 0.2 slice_reduce_fusion
  2.9 0.7 broadcast_in_dim.25.fall_ref
  3.5 0.7 convert_element_type.51
  4.2 0.1 exponential_bitcast_fusion.1
  4.3 0.3 fusion.46
  4.6 0.1 copy.28
  4.7 1.7 %pad_maximum_fusion.kv_ref = bf16[2,128,2,128]{3,2,1,0:T(2,128)(2,1)} fusion(bf16[1,128,2,128]{3,2,1,0:T(2,128)(2,1)} %bitcast.57, bf16[1,128,2,128]{3,2,1,0:T(2,128)(2,1)} %bitcast.58), kind=kLoop, calls=%fused_computation.55 | loop fusion | flops 65536 | bytes 262144 | tf_op jit(solution)/shard_map/stack | solution.py:443
  6.4 1.4 subtract_convert_fusion.1
  7.8 3.2 %convolution_bitcast_fusion = f32[128,16,128]{0,2,1:T(8,128)} fusion(bf16[128,16,128]{2,1,0:T(8,128)(2,1)} %param.10, f32[16,128]{1,0:T(8,128)S(1)} %reduce_window_sum.11, pred[128,128]{1,0:T(8,128)(4,1)S(1)} %iota_compare_fusion.1, bf16[128,16,128]{2,1,0:T(8,128)(2,1)} %param.9, bf16[128,16,128]{2,1,0:T(8,128)(2,1)} %param.11), kind=kOutput, calls=%fused_computation.15 | convolution fusion | flops 135266304 | bytes 2646016 | tf_op jit(solution)/shard_map/hts,shd->thd/dot_general | solution.py:450
  11.0 0.0 copy-done.3
  11.0 0.3 fusion.27
  11.4 0.0 copy-start.4
  11.4 1.5 %fusion.58 = (bf16[16,128,128]{2,1,0:T(8,128)(2,1)}, f32[16,128,128]{2,1,0:T(8,128)}) fusion(f32[16,128,128]{2,1,0:T(8,128)S(1)} %fusion.27, bf16[128,16,128]{2,1,0:T(8,128)(2,1)S(1)} %copy-done.3, bf16[128,16,128]{2,1,0:T(8,128)(2,1)S(1)} %get-tuple-element.12), kind=kOutput, calls=%fused_computation.85 | convolution fusion | flops 67633152 | bytes 3670016 | tf_op jit(solution)/shard_map/egz,egc->gzc/dot_general | solution.py:438
  12.9 107.3 %shard_map.104 = (f32[16,128,128]{2,1,0:T(8,128)}, bf16[3,2,128,2,128]{4,3,2,1,0:T(2,128)(2,1)}) custom-call(f32[16,128]{1,0:T(8,128)} %broadcast_in_dim.25.fall_ref, f32[16,128,128]{2,1,0:T(8,128)} %get-tuple-element.23.state_ref, bf16[16,128,128]{2,1,0:T(8,128)(2,1)} %get-tuple-element.22.sent0_ref, bf16[2,128,2,128]{3,2,1,0:T(2,128)(2,1)} %pad_maximum_fusion.kv_ref), custom_call_target="tpu_custom_call" | custom-call | tf_op jit(solution)/shard_map/pallas_call | solution.py:291
  120.2 0.0 copy-start.1
  120.2 1.4 slice_bitcast_fusion.2
  121.6 2.3 %maximum_bitcast_fusion = (bf16[512,2,128,1]{2,1,0,3:T(2,128)(2,1)S(1)}, bf16[512,2,128,1]{2,1,0,3:T(2,128)(2,1)}) fusion(bf16[128,2,128]{2,1,0:T(2,128)(2,1)} %param.15, bf16[128,2,128]{2,1,0:T(2,128)(2,1)S(1)} %get-tuple-element.17, bf16[128,2,128]{2,1,0:T(2,128)(2,1)S(1)} %get-tuple-element.18, bf16[128,2,128]{2,1,0:T(2,128)(2,1)S(1)} %get-tuple-element.19, ...), kind=kLoop, calls=%fused_computation.46 | loop fusion | flops 786432 | bytes 1048576 | tf_op jit(solution)/shard_map/concatenate | solution.py:473
  123.9 0.0 copy-done.2
  123.9 1.7 %fusion.36 = f32[16,128,128]{2,1,0:T(8,128)S(1)} fusion(bf16[128,16,128]{2,1,0:T(8,128)(2,1)S(1)} %copy-done.2, f32[16,128,128]{2,1,0:T(8,128)} %get-tuple-element.4), kind=kOutput, calls=%fused_computation.41 | convolution fusion | flops 67371008 | bytes 2621440 | tf_op jit(solution)/shard_map/nwg,wgq->nwq/dot_general | solution.py:454
  125.7 1.0 multiply_reduce_fusion
  126.7 6.4 %shard_map.105 = f32[1,128]{1,0:T(1,128)} custom-call(f32[1,128]{1,0:T(1,128)} %bitcast.60), custom_call_target="tpu_custom_call" | custom-call | tf_op jit(solution)/shard_map/pallas_call | solution.py:367
  133.1 0.7 rsqrt_bitcast_fusion
  133.8 0.3 multiply_convert_fusion
  134.1 1.2 copy.41
  135.3 0.8 fusion.2
  136.1 0.9 fusion
  137.0 1.4 divide_convert_fusion
  138.4 1.1 copy.42
  (10 shorter events, 0.0 us)
Async XLA Ops:
  0.6 1.1 copy-start
  0.6 10.4 %copy-start.3 = (bf16[128,16,128]{2,1,0:T(8,128)(2,1)S(1)}, bf16[128,16,128]{2,1,0:T(8,128)(2,1)}, u32[]{:S(2)}) copy-start(bf16[128,16,128]{2,1,0:T(8,128)(2,1)} %param.11) | copy-start | bytes 1572868
  11.0 110.6 %copy-start.5 = (bf16[128,2,128]{2,1,0:T(2,128)(2,1)S(1)}, bf16[128,2,128]{2,1,0:T(2,128)(2,1)}, u32[]{:S(2)}) copy-start(bf16[128,2,128]{2,1,0:T(2,128)(2,1)} %param.16) | copy-start | bytes 196612
  11.0 112.9 %copy-start.2 = (bf16[128,16,128]{2,1,0:T(8,128)(2,1)S(1)}, bf16[128,16,128]{2,1,0:T(8,128)(2,1)}, u32[]{:S(2)}) copy-start(bf16[128,16,128]{2,1,0:T(8,128)(2,1)} %param.9) | copy-start | bytes 1572868
  11.4 114.3 %copy-start.4 = (f32[128,16,128]{0,2,1:T(8,128)S(1)}, f32[128,16,128]{0,2,1:T(8,128)}, u32[]{:S(2)}) copy-start(f32[128,16,128]{0,2,1:T(8,128)} %convolution_bitcast_fusion) | copy-start | bytes 3145732
  120.2 5.4 %copy-start.1 = (f32[16,128,128]{2,1,0:T(8,128)S(1)}, f32[16,128,128]{2,1,0:T(8,128)}, u32[]{:S(2)}) copy-start(f32[16,128,128]{2,1,0:T(8,128)} %get-tuple-element.4) | copy-start | bytes 3145732
  135.3 1.7 %copy-start.6 = (bf16[512,2,128,1]{2,1,0,3:T(2,128)(2,1)S(1)}, bf16[512,2,128,1]{2,1,0,3:T(2,128)(2,1)}, u32[]{:S(2)}) copy-start(bf16[512,2,128,1]{2,1,0,3:T(2,128)(2,1)} %get-tuple-element.31) | copy-start | bytes 786436

commit v9 on v8

--- a/solution.py
+++ b/solution.py
@@ -22,8 +22,10 @@
     state_ref,
     sent0_ref,
     kv_ref,
+    q_ref,
+    bias_ref,
     out_ref,
-    kv_out,
+    soft_ref,
     whole,
     whole_fall,
     out_fall,
@@ -226,8 +228,46 @@
     if rounds > 3:
         send_fall(3, ahead(8), whole_fall, 8)
 
+    def attention():
+        for dist in range(1, reach + 1):
+
+            @pl.when(behind(dist) == 1)
+            def _():
+                kv_copy(dist, me - dist).wait_recv()
+
+            @pl.when(behind(dist) == 0)
+            def _():
+                kv_got[dist - 1] = jnp.zeros_like(kv_got.at[dist - 1])
+
+            @pl.when(ahead(dist) == 1)
+            def _():
+                kv_copy(dist, me + dist).wait_send()
+
+        tokens, groups, group = q_ref.shape[0], q_ref.shape[1], q_ref.shape[2]
+        scale = float(q_ref.shape[3]) ** (-0.5)
+        for g in range(groups):
+            q = q_ref[:, g].astype(jnp.float32).reshape(tokens * group, -1).astype(jnp.bfloat16)
+            keys = [kv_got[slot, 0, g] for slot in range(reach - 1, -1, -1)] + [kv_ref[0, g]]
+            values = [kv_got[slot, 1, g] for slot in range(reach - 1, -1, -1)] + [kv_ref[1, g]]
+            logits = jnp.concatenate(
+                [
+                    lax.dot_general(q, k, (((1,), (1,)), ((), ())), preferred_element_type=jnp.float32)
+                    for k in keys
+                ],
+                axis=1,
+            )
+            masked = (logits * scale).reshape(tokens, group, -1) + bias_ref[...][:, None, :]
+            top = jnp.max(masked, axis=-1, keepdims=True)
+            exps = jnp.exp(masked - top)
+            total = jnp.sum(exps, axis=-1, keepdims=True)
+            probs = exps.reshape(tokens * group, -1).astype(jnp.bfloat16)
+            summed = jnp.dot(probs, jnp.concatenate(values, axis=0), preferred_element_type=jnp.float32)
+            soft_ref[:, g] = (summed.reshape(tokens, group, -1) / total).astype(soft_ref.dtype)
+
     for k in range(3, rounds):
         shift, last = 2**k, k == rounds - 1
+        if last:
+            attention()
         for c in range(chunks):
             forward_chunk(k, shift, c, update_whole=not last)
             if not last:
@@ -253,21 +293,6 @@
                 outgoing_fall[k + 1] = whole_fall[...]
                 fall_copy(k + 1, outgoing_fall.at[k + 1], me + 2 * shift).start()
 
-    for dist in range(1, reach + 1):
-
-        @pl.when(behind(dist) == 1)
-        def _():
-            kv_copy(dist, me - dist).wait_recv()
-            kv_out[dist - 1] = kv_got[dist - 1]
-
-        @pl.when(behind(dist) == 0)
-        def _():
-            kv_out[dist - 1] = jnp.zeros_like(kv_out.at[dist - 1])
-
-        @pl.when(ahead(dist) == 1)
-        def _():
-            kv_copy(dist, me + dist).wait_send()
-
     sends = [(0, 1, ahead(1)), (back0, -1, behind(1)), (1, 2, ahead(2)), (back1, -2, behind(2))]
     sends += [(2, jump, ahead(jump)), (near, 4, near_send)]
     sends += [(k, 2**k, ahead(2**k)) for k in range(3, rounds)]
@@ -280,7 +305,7 @@
                 state_copy(stage, outgoing.at[stage], c, me + dist).wait_send()
 
 
-def exclusive_scan(falling, state, kv, axis):
+def exclusive_scan(falling, state, kv, queries, bias, axis):
     length = lax.axis_size(axis)
     rounds = length.bit_length() - 1
     stages = rounds + 3
@@ -292,9 +317,9 @@
         functools.partial(scan_kernel, rounds, chunks, REACH),
         out_shape=(
             jax.ShapeDtypeStruct(state.shape, jnp.float32),
-            jax.ShapeDtypeStruct((REACH,) + kv.shape, kv.dtype),
+            jax.ShapeDtypeStruct(queries.shape, queries.dtype),
         ),
-        in_specs=[vmem] * 4,
+        in_specs=[vmem] * 6,
         out_specs=(vmem, vmem),
         scratch_shapes=[
             pltpu.VMEM(state.shape, jnp.float32),
@@ -315,7 +340,7 @@
             pltpu.SemaphoreType.DMA((REACH,)),
         ],
         compiler_params=pltpu.CompilerParams(collective_id=0, has_side_effects=True),
-    )(fall_rows, state, state.astype(jnp.bfloat16), kv)
+    )(fall_rows, state, state.astype(jnp.bfloat16), kv, queries, bias)
 
 
 def head_sum_kernel(count, value_ref, out_ref, slots, send_sem, recv_sem):
@@ -439,8 +464,20 @@
         "egz,egc->gzc", key_product_lower, linear_value_rows, preferred_element_type=jnp.float32
     )
     falling = jnp.exp(cumulated[:, -1])
-    preceding_state, previous = exclusive_scan(
-        falling, recurrent_state, jnp.stack([soft_keys, soft_values]), "seq"
+    kv_here = soft_keys.shape[1]
+    group = heads_here // kv_here
+    block_index = lax.axis_index("seq")
+    key_index = jnp.arange((REACH + 1) * row_count, dtype=jnp.int32)
+    key_block = block_index - REACH + key_index // row_count
+    causal = (key_index % row_count)[None, :] <= token_locations[:, None]
+    visible = ((key_block[None, :] < block_index) | causal) & (key_block[None, :] >= window_start[0])
+    preceding_state, soft_out = exclusive_scan(
+        falling,
+        recurrent_state,
+        jnp.stack([soft_keys, soft_values]).transpose(0, 2, 1, 3),
+        soft_queries.reshape(row_count, kv_here, group, head_width),
+        jnp.where(visible, 0.0, -jnp.inf).astype(jnp.float32),
+        "seq",
     )
     lin_scores = jnp.einsum(
         "thd,shd->hts", linear_query_rows, lin_keys, preferred_element_type=jnp.float32
@@ -464,38 +501,7 @@
         * lax.rsqrt(squares / (HEADS * DH) + 1e-06)[:, None, None]
         * norm_gain.astype(jnp.float32)
     ).astype(jnp.bfloat16)
-    kv_here = soft_keys.shape[1]
-    group = heads_here // kv_here
-    score_scale = float(head_width) ** (-0.5)
-    query_rows = soft_queries.reshape(row_count, kv_here, group, head_width)
-    block_index = lax.axis_index("seq")
-    first_block = window_start[0]
-    all_keys = jnp.concatenate([previous[back, 0] for back in range(REACH - 1, -1, -1)] + [soft_keys], axis=0)
-    all_values = jnp.concatenate(
-        [previous[back, 1] for back in range(REACH - 1, -1, -1)] + [soft_values], axis=0
-    )
-    key_index = jnp.arange((REACH + 1) * row_count, dtype=jnp.int32)
-    key_block = block_index - REACH + key_index // row_count
-    causal = (key_index % row_count)[None, :] <= token_locations[:, None]
-    visible = ((key_block[None, :] < block_index) | causal) & (key_block[None, :] >= first_block)
-    logits = (
-        jnp.einsum("cphm,npm->phcn", query_rows, all_keys, preferred_element_type=jnp.float32)
-        * score_scale
-    )
-    masked = jnp.where(visible, logits, -jnp.inf)
-    top = jnp.max(masked, axis=-1)
-    exps = jnp.exp(masked - top[..., None])
-    total = jnp.sum(exps, axis=-1)
-    summed = jnp.einsum(
-        "qyjl,lqu->qyju", exps.astype(jnp.bfloat16), all_values, preferred_element_type=jnp.float32
-    )
-    carried_over_state = (top, total, summed)
-    final_output = carried_over_state[2] / carried_over_state[1][..., None]
-    soft_out = (
-        final_output.transpose(2, 0, 1, 3)
-        .reshape(row_count, heads_here, head_width)
-        .astype(jnp.bfloat16)
-    )
+    soft_out = soft_out.reshape(row_count, heads_here, head_width)
     return (lin_out, soft_out)
 
 

time: 140 us -> 133 us (0.950)
  other arithmetic: 9.32 us -> 4.92 us
  local copies, waits for them, and re-layouts: 4.97 us -> 3 us
    concatenate x1 -> x0, other arithmetic: 2.31 us -> none  [body(): jnp.concatenate([previous[back, 0] for back in range(REACH - 1, -1, -1)]...]
    dot_general x2 -> x0, matrix products: 2.17 us -> none  [the longest x1 1.38 us: body(): jnp.einsum('qyjl,lqu->qyju', exps.astype(jnp.bfloat16), all_values, prefe...]
    another operation x1 -> x0, other arithmetic: 1.72 us -> none  [body(): jnp.stack([soft_keys, soft_values])]
    dot_general x1, matrix products: 1.02 us -> 2.55 us  [body(): jnp.einsum('nwg,wgq->nwq', linear_query_rows, preceding_lower, preferred_...]
where the time goes in v9:
time: 133 us; the launch traced here: 132 us
  Pallas kernels  114 us (86%)
  matrix products  9.07 us (7%)
  other arithmetic  4.92 us (4%)
  local copies, waits for them, and re-layouts  3 us (2%)
  between operations  1.43 us (1%)
    pallas_call x1, Pallas kernels, exclusive_scan(): pl.pallas_call(functools.partial(scan_kernel, rounds, chunks, REACH), out...  108 us
    pallas_call x1, Pallas kernels, head_sum(): pl.pallas_call(functools.partial(head_sum_kernel, count), out_shape=jax.S...  6.31 us
    dot_general x1, matrix products, body(): jnp.einsum('nwg,wgq->nwq', linear_query_rows, preceding_upper, preferred_...  2.79 us

profile of v9, /device:TPU:60, one launch (start us, length us, event | category | flops | bytes accessed | tf_op | source)
XLA Modules:
  0.0 132.3 jit_solution(5899201824862861933)
XLA Ops:
  0.6 0.0 copy-start
  0.6 1.0 reduce_window_sum.11
  1.7 0.2 slice_reduce_fusion
  1.9 0.1 exponential_bitcast_fusion.1
  1.9 0.1 copy.25
  2.1 1.4 %subtract_convert_fusion.1 = (bf16[128,16,128]{2,1,0:T(8,128)(2,1)S(1)}, bf16[128,16,128]{2,1,0:T(8,128)(2,1)S(1)}) fusion(bf16[128,16,128]{2,1,0:T(8,128)(2,1)} %param.10, f32[128,16]{1,0:T(8,128)S(1)} %copy.25), kind=kLoop, calls=%fused_computation.11 | loop fusion | flops 1572864 | bytes 1581056 | tf_op jit(solution)/shard_map/convert_element_type | solution.py:418
  3.5 0.0 copy-done
  3.5 0.3 fusion.11
  3.8 1.5 %fusion.39 = (bf16[16,128,128]{2,1,0:T(8,128)(2,1)}, f32[16,128,128]{2,1,0:T(8,128)}) fusion(f32[16,128,128]{2,1,0:T(8,128)S(1)} %fusion.11, bf16[128,16,128]{2,1,0:T(8,128)(2,1)S(1)} %copy-done, bf16[128,16,128]{2,1,0:T(8,128)(2,1)S(1)} %get-tuple-element.12), kind=kOutput, calls=%fused_computation.62 | convolution fusion | flops 67633152 | bytes 3670016 | tf_op jit(solution)/shard_map/egz,egc->gzc/dot_general | solution.py:463
  6.0 0.0 copy-start.5
  6.0 0.0 copy-start.6
  6.0 0.8 fusion.29.bias_ref
  6.8 0.7 broadcast_in_dim.27.fall_ref
  7.4 0.0 copy-done.5
  7.4 0.0 copy-done.6
  7.5 0.7 maximum_bitcast_fusion.kv_ref
  8.1 107.6 %shard_map.104 = (f32[16,128,128]{2,1,0:T(8,128)}, bf16[128,2,8,128]{3,2,1,0:T(8,128)(2,1)}) custom-call(f32[16,128]{1,0:T(8,128)} %broadcast_in_dim.27.fall_ref, f32[16,128,128]{2,1,0:T(8,128)} %get-tuple-element.17.state_ref, bf16[16,128,128]{2,1,0:T(8,128)(2,1)} %get-tuple-element.16.sent0_ref, bf16[2,2,128,128]{3,2,1,0:T(8,128)(2,1)} %maximum_bitcast_fusion.kv_ref, ...), custom_call_target="tpu_custom_call" | custom-call | tf_op jit(solution)/shard_map/pallas_call | solution.py:316
  115.7 0.0 copy-done.2
  115.7 0.0 copy-start.3
  115.7 2.8 %fusion.20 = f32[16,128,128]{2,1,0:T(8,128)} fusion(bf16[128,16,128]{2,1,0:T(8,128)(2,1)S(1)} %copy-done.2, f32[16,128,128]{2,1,0:T(8,128)} %get-tuple-element.4), kind=kOutput, calls=%fused_computation.27 | convolution fusion | flops 67371008 | bytes 2621440 | tf_op jit(solution)/shard_map/nwg,wgq->nwq/dot_general | solution.py:491
  118.5 0.0 copy-done.3
  118.6 0.0 copy-start.1
  118.6 1.9 %convolution_bitcast_fusion = f32[128,16,128]{0,2,1:T(8,128)} fusion(bf16[128,16,128]{2,1,0:T(8,128)(2,1)S(1)} %copy-done.3, f32[16,128]{1,0:T(8,128)S(1)} %reduce_window_sum.11, pred[128,128]{1,0:T(8,128)(4,1)S(1)} %iota_compare_fusion.1, bf16[128,16,128]{2,1,0:T(8,128)(2,1)S(1)} %copy-done.2, bf16[128,16,128]{2,1,0:T(8,128)(2,1)S(1)} %copy-done), kind=kOutput, calls=%fused_computation.5 | convolution fusion | flops 135266304 | bytes 2646016 | tf_op jit(solution)/shard_map/hts,shd->thd/dot_general | solution.py:487
  120.5 0.0 copy-done.1
  120.5 2.5 %multiply_reduce_fusion = (f32[128]{0:T(128)}, f32[128,16,128]{0,2,1:T(8,128)S(1)}) fusion(f32[128,16,128]{0,2,1:T(8,128)} %convolution_bitcast_fusion, f32[16,128,128]{2,1,0:T(8,128)} %fusion.20, bf16[128,16,128]{2,1,0:T(8,128)(2,1)S(1)} %copy-done.2, f32[16,128,128]{2,1,0:T(8,128)S(1)} %copy-done.1, f32[128,16]{0,1:T(8,128)S(1)} %get-tuple-element.14), kind=kOutput, calls=%fused_computation.9 | convolution fusion | flops 69468032 | bytes 4727296 | tf_op jit(solution)/shard_map/nwg,wgq->nwq/dot_general | solution.py:494
  123.0 6.3 %shard_map.105 = f32[1,128]{1,0:T(1,128)} custom-call(f32[1,128]{1,0:T(1,128)} %bitcast.27), custom_call_target="tpu_custom_call" | custom-call | tf_op jit(solution)/shard_map/pallas_call | solution.py:392
  129.3 0.6 rsqrt_bitcast_fusion
  129.9 0.0 copy-done.7
  129.9 0.3 multiply_convert_fusion
  130.3 0.0 copy-start.4
  130.3 1.2 copy.36
  131.5 0.8 copy.70
  (8 shorter events, 0.1 us)
Async XLA Ops:
  0.6 2.8 %copy-start = (bf16[128,16,128]{2,1,0:T(8,128)(2,1)S(1)}, bf16[128,16,128]{2,1,0:T(8,128)(2,1)}, u32[]{:S(2)}) copy-start(bf16[128,16,128]{2,1,0:T(8,128)(2,1)} %param.11) | copy-start | bytes 1572868
  6.0 1.4 %copy-start.5 = (bf16[128,2,128]{2,1,0:T(2,128)(2,1)S(1)}, bf16[128,2,128]{2,1,0:T(2,128)(2,1)}, u32[]{:S(2)}) copy-start(bf16[128,2,128]{2,1,0:T(2,128)(2,1)} %param.16) | copy-start | bytes 196612
  6.0 1.4 %copy-start.6 = (bf16[128,2,128]{2,1,0:T(2,128)(2,1)S(1)}, bf16[128,2,128]{2,1,0:T(2,128)(2,1)}, u32[]{:S(2)}) copy-start(bf16[128,2,128]{2,1,0:T(2,128)(2,1)} %param.15) | copy-start | bytes 196612
  8.1 107.6 %copy-start.2 = (bf16[128,16,128]{2,1,0:T(8,128)(2,1)S(1)}, bf16[128,16,128]{2,1,0:T(8,128)(2,1)}, u32[]{:S(2)}) copy-start(bf16[128,16,128]{2,1,0:T(8,128)(2,1)} %param.9) | copy-start | bytes 1572868
  115.7 2.8 %copy-start.3 = (bf16[128,16,128]{2,1,0:T(8,128)(2,1)S(1)}, bf16[128,16,128]{2,1,0:T(8,128)(2,1)}, u32[]{:S(2)}) copy-start(bf16[128,16,128]{2,1,0:T(8,128)(2,1)} %param.10) | copy-start | bytes 1572868
  118.6 1.9 %copy-start.1 = (f32[16,128,128]{2,1,0:T(8,128)S(1)}, f32[16,128,128]{2,1,0:T(8,128)}, u32[]{:S(2)}) copy-start(f32[16,128,128]{2,1,0:T(8,128)} %get-tuple-element.4) | copy-start | bytes 3145732
  123.0 6.9 %copy-start.7 = (bf16[16,128]{1,0:T(8,128)(2,1)S(1)}, bf16[16,128]{1,0:T(8,128)(2,1)}, u32[]{:S(2)}) copy-start(bf16[16,128]{1,0:T(8,128)(2,1)} %param.13) | copy-start | bytes 12292
  130.3 1.2 copy-start.4

commit v10 on v9

--- a/solution.py
+++ b/solution.py
@@ -24,8 +24,13 @@
     kv_ref,
     q_ref,
     bias_ref,
+    lq_ref,
+    local_ref,
+    grow_ref,
+    gain_ref,
     out_ref,
     soft_ref,
+    lin_ref,
     whole,
     whole_fall,
     out_fall,
@@ -42,6 +47,9 @@
     kv_got,
     kv_send,
     kv_recv,
+    head_slots,
+    head_send,
+    head_recv,
 ):
     me = lax.axis_index("seq")
     head = lax.axis_index("head")
@@ -74,7 +82,14 @@
         def _():
             pl.semaphore_signal(barrier, inc=1, device_id=(me - dist, head), device_id_type=MESH)
 
-    pl.semaphore_wait(barrier, partners)
+    head_count = head_slots.shape[0]
+    for other in range(head_count):
+
+        @pl.when(other != head)
+        def _():
+            pl.semaphore_signal(barrier, inc=1, device_id=(me, other), device_id_type=MESH)
+
+    pl.semaphore_wait(barrier, partners + head_count - 1)
 
     def kv_copy(dist, device):
         return pltpu.make_async_remote_copy(
@@ -304,8 +319,49 @@
             for c in range(chunks):
                 state_copy(stage, outgoing.at[stage], c, me + dist).wait_send()
 
-
-def exclusive_scan(falling, state, kv, queries, bias, axis):
+    prior = out_ref[...]
+    upper = prior.astype(jnp.bfloat16)
+    lower = (prior - upper.astype(jnp.float32)).astype(jnp.bfloat16)
+    queries = lq_ref[...]
+    carried = jnp.einsum("hti,hij->htj", queries, upper, preferred_element_type=jnp.float32)
+    carried = carried + jnp.einsum("hti,hij->htj", queries, lower, preferred_element_type=jnp.float32)
+    mixed = local_ref[...] + grow_ref[...] * carried
+    column = jnp.sum(jnp.sum(mixed * mixed, axis=0), axis=1, keepdims=True)
+    head_slots[head] = jnp.transpose(jnp.broadcast_to(column, (column.shape[0], 128)))[0:1, :]
+
+    def head_copy(other, slot):
+        return pltpu.make_async_remote_copy(
+            src_ref=head_slots.at[head],
+            dst_ref=head_slots.at[slot],
+            send_sem=head_send.at[other],
+            recv_sem=head_recv.at[slot],
+            device_id=(me, other),
+            device_id_type=MESH,
+        )
+
+    for other in range(head_count):
+
+        @pl.when(other != head)
+        def _():
+            head_copy(other, head).start()
+
+    for other in range(head_count):
+
+        @pl.when(other != head)
+        def _():
+            head_copy(other, other).wait_recv()
+            head_copy(other, head).wait_send()
+
+    total = head_slots[0]
+    for other in range(1, head_count):
+        total = total + head_slots[other]
+    heads_all, width_all = lq_ref.shape[0] * head_count, lq_ref.shape[2]
+    scale_row = lax.rsqrt(total / (heads_all * width_all) + 1e-06)
+    scale = jnp.transpose(jnp.broadcast_to(scale_row, (128, scale_row.shape[1])))[:, 0:1]
+    lin_ref[...] = (mixed * scale[None] * gain_ref[...][:, None, :]).astype(lin_ref.dtype)
+
+
+def exclusive_scan(falling, state, kv, queries, bias, lq, local, grow, gain, axis):
     length = lax.axis_size(axis)
     rounds = length.bit_length() - 1
     stages = rounds + 3
@@ -318,9 +374,10 @@
         out_shape=(
             jax.ShapeDtypeStruct(state.shape, jnp.float32),
             jax.ShapeDtypeStruct(queries.shape, queries.dtype),
+            jax.ShapeDtypeStruct(lq.shape, jnp.bfloat16),
         ),
-        in_specs=[vmem] * 6,
-        out_specs=(vmem, vmem),
+        in_specs=[vmem] * 10,
+        out_specs=(vmem, vmem, vmem),
         scratch_shapes=[
             pltpu.VMEM(state.shape, jnp.float32),
             pltpu.VMEM((heads, columns), jnp.float32),
@@ -338,9 +395,12 @@
             pltpu.VMEM((REACH,) + kv.shape, kv.dtype),
             pltpu.SemaphoreType.DMA((REACH,)),
             pltpu.SemaphoreType.DMA((REACH,)),
+            pltpu.VMEM((lax.axis_size("head"), 1, columns), jnp.float32),
+            pltpu.SemaphoreType.DMA((lax.axis_size("head"),)),
+            pltpu.SemaphoreType.DMA((lax.axis_size("head"),)),
         ],
         compiler_params=pltpu.CompilerParams(collective_id=0, has_side_effects=True),
-    )(fall_rows, state, state.astype(jnp.bfloat16), kv, queries, bias)
+    )(fall_rows, state, state.astype(jnp.bfloat16), kv, queries, bias, lq, local, grow, gain)
 
 
 def head_sum_kernel(count, value_ref, out_ref, slots, send_sem, recv_sem):
@@ -471,36 +531,27 @@
     key_block = block_index - REACH + key_index // row_count
     causal = (key_index % row_count)[None, :] <= token_locations[:, None]
     visible = ((key_block[None, :] < block_index) | causal) & (key_block[None, :] >= window_start[0])
-    preceding_state, soft_out = exclusive_scan(
+    lin_scores = jnp.einsum(
+        "thd,shd->hts", linear_query_rows, lin_keys, preferred_element_type=jnp.float32
+    )
+    gap = jnp.where(lower_mask[None], cumulated[:, :, None] - cumulated[:, None, :], -jnp.inf)
+    lin_weights = (lin_scores * jnp.exp(gap)).astype(jnp.bfloat16)
+    local_part = jnp.einsum(
+        "hts,shd->htd", lin_weights, linear_value_rows, preferred_element_type=jnp.float32
+    )
+    normed, soft_out, lin_out = exclusive_scan(
         falling,
         recurrent_state,
         jnp.stack([soft_keys, soft_values]).transpose(0, 2, 1, 3),
         soft_queries.reshape(row_count, kv_here, group, head_width),
         jnp.where(visible, 0.0, -jnp.inf).astype(jnp.float32),
+        linear_query_rows.transpose(1, 0, 2),
+        local_part,
+        jnp.exp(cumulated)[:, :, None],
+        norm_gain.astype(jnp.float32),
         "seq",
     )
-    lin_scores = jnp.einsum(
-        "thd,shd->hts", linear_query_rows, lin_keys, preferred_element_type=jnp.float32
-    )
-    gap = jnp.where(lower_mask[None], cumulated[:, :, None] - cumulated[:, None, :], -jnp.inf)
-    lin_weights = (lin_scores * jnp.exp(gap)).astype(jnp.bfloat16)
-    local_part = jnp.einsum(
-        "hts,shd->thd", lin_weights, linear_value_rows, preferred_element_type=jnp.float32
-    )
-    preceding_upper, preceding_lower = split_parts(preceding_state)
-    carried_part = jnp.einsum(
-        "nwg,wgq->nwq", linear_query_rows, preceding_upper, preferred_element_type=jnp.float32
-    )
-    carried_part = carried_part + jnp.einsum(
-        "nwg,wgq->nwq", linear_query_rows, preceding_lower, preferred_element_type=jnp.float32
-    )
-    mixed = local_part + jnp.exp(cumulated).T[:, :, None] * carried_part
-    squares = head_sum(jnp.sum(mixed * mixed, axis=(1, 2)), "head")
-    lin_out = (
-        mixed
-        * lax.rsqrt(squares / (HEADS * DH) + 1e-06)[:, None, None]
-        * norm_gain.astype(jnp.float32)
-    ).astype(jnp.bfloat16)
+    lin_out = lin_out.transpose(1, 0, 2)
     soft_out = soft_out.reshape(row_count, heads_here, head_width)
     return (lin_out, soft_out)
 

time: 133 us -> 130 us (0.977); the launches traced: 132 us -> 128 us
  matrix products: 9.07 us -> 3.56 us
  local copies, waits for them, and re-layouts: 3 us -> 7.31 us
  Pallas kernels: 114 us -> 111 us
    pallas_call x1 -> x0, Pallas kernels: 6.31 us -> none  [head_sum(): pl.pallas_call(functools.partial(head_sum_kernel, count), out_shape=jax.S...]
    dot_general x3 -> x1, matrix products: 7.23 us -> 1.72 us  [body(): jnp.einsum('hts,shd->htd', lin_weights, linear_value_rows, preferred_elem...]
    pallas_call x1, Pallas kernels: 108 us -> 111 us  [exclusive_scan(): pl.pallas_call(functools.partial(scan_kernel, rounds, chunks, REACH), out...]
    unnamed x18 -> x11, local copies, waits for them, and re-layouts: 2.03 us -> 4.09 us
    exp x0 -> x1, local copies, waits for them, and re-layouts: none -> 1.38 us  [body(): jnp.exp(cumulated)[:, :, None]]
where the time goes in v10:
time: 130 us; the launch traced here: 128 us
  Pallas kernels  111 us (85%)
  local copies, waits for them, and re-layouts  7.31 us (6%)
  other arithmetic  4.15 us (3%)
  matrix products  3.56 us (3%)
  between operations  1.45 us (1%)
    pallas_call x1, Pallas kernels, exclusive_scan(): pl.pallas_call(functools.partial(scan_kernel, rounds, chunks, REACH), out...  111 us
    unnamed x11, local copies, waits for them, and re-layouts  4.09 us

profile of v10, /device:TPU:60, one launch (start us, length us, event | category | flops | bytes accessed | tf_op | source)
XLA Modules:
  0.0 127.8 jit_solution(5660884161613008201)
XLA Ops:
  0.6 0.0 copy-start
  0.6 0.0 copy-start.2
  1.4 1.0 reduce_window_sum.11
  2.4 0.2 slice_reduce_fusion
  2.6 0.7 broadcast_in_dim.25.fall_ref
  3.3 1.3 %convert_element_type.27.gain_ref = f32[16,128]{1,0:T(8,128)} convert(bf16[16,128]{1,0:T(8,128)(2,1)} %param.13) | non-fusion elementwise | flops 2048 | bytes 12288 | tf_op jit(solution)/shard_map/convert_element_type | solution.py:551
  4.5 0.1 exponential_bitcast_fusion
  4.6 0.1 copy.21
  4.7 0.9 copy_bitcast_fusion.1
  5.6 0.7 maximum_bitcast_fusion.kv_ref
  6.3 0.8 fusion.22.bias_ref
  7.1 0.0 copy-done.2
  7.1 0.0 copy-start.1
  7.1 0.9 copy.56
  8.0 0.1 copy-done.1
  8.1 0.3 subtract_convert_fusion
  8.5 0.0 copy-done
  8.5 1.7 %fusion.1.local_ref = f32[16,128,128]{2,1,0:T(8,128)} fusion(bf16[128,16,128]{2,1,0:T(8,128)(2,1)S(1)} %copy-done.1, f32[16,128]{1,0:T(8,128)S(1)} %reduce_window_sum.11, pred[128,128]{1,0:T(8,128)(4,1)S(1)} %iota_compare_fusion.1, bf16[128,16,128]{2,1,0:T(8,128)(2,1)S(1)} %copy-done.2, bf16[128,16,128]{2,1,0:T(8,128)(2,1)S(1)} %copy-done), kind=kOutput, calls=%fused_computation.3 | convolution fusion | flops 135266304 | bytes 2646016 | tf_op jit(solution)/shard_map/hts,shd->htd/dot_general | solution.py:539
  10.2 1.4 %copy.30.grow_ref = f32[16,128,1]{2,1,0:T(8,128)} copy(f32[16,128,1]{1,0,2:T(8,128)S(1)} %get-tuple-element.14) | data formatting | bytes 16384 | tf_op jit(solution)/shard_map/exp | solution.py:550
  11.6 0.3 fusion.9
  11.9 1.5 %fusion.32 = (bf16[16,128,128]{2,1,0:T(8,128)(2,1)}, f32[16,128,128]{2,1,0:T(8,128)}) fusion(f32[16,128,128]{2,1,0:T(8,128)S(1)} %fusion.9, bf16[128,16,128]{2,1,0:T(8,128)(2,1)S(1)} %copy-done, bf16[128,16,128]{2,1,0:T(8,128)(2,1)S(1)} %get-tuple-element.12), kind=kOutput, calls=%fused_computation.50 | convolution fusion | flops 67633152 | bytes 3670016 | tf_op jit(solution)/shard_map/egz,egc->gzc/dot_general | solution.py:523
  13.4 111.4 %shard_map.104 = (f32[16,128,128]{2,1,0:T(8,128)}, bf16[128,2,8,128]{3,2,1,0:T(8,128)(2,1)}, bf16[16,128,128]{2,1,0:T(8,128)(2,1)}) custom-call(f32[16,128]{1,0:T(8,128)} %broadcast_in_dim.25.fall_ref, f32[16,128,128]{2,1,0:T(8,128)} %get-tuple-element.17.state_ref, bf16[16,128,128]{2,1,0:T(8,128)(2,1)} %get-tuple-element.16.sent0_ref, ...), custom_call_target="tpu_custom_call" | custom-call | tf_op jit(solution)/shard_map/pallas_call | solution.py:372
  124.8 0.0 copy-start.3
  124.8 2.2 %copy.31 = bf16[128,16,128]{2,1,0:T(8,128)(2,1)} copy(bf16[128,16,128]{2,0,1:T(8,128)(2,1)} %bitcast.21) | data formatting | bytes 1048576
  127.0 0.0 copy-done.3
  127.0 0.8 copy.59
  (3 shorter events, 0.0 us)
Async XLA Ops:
  0.6 7.8 %copy-start = (bf16[128,16,128]{2,1,0:T(8,128)(2,1)S(1)}, bf16[128,16,128]{2,1,0:T(8,128)(2,1)}, u32[]{:S(2)}) copy-start(bf16[128,16,128]{2,1,0:T(8,128)(2,1)} %param.11) | copy-start | bytes 1572868
  0.6 6.4 %copy-start.2 = (bf16[128,16,128]{2,1,0:T(8,128)(2,1)S(1)}, bf16[128,16,128]{2,1,0:T(8,128)(2,1)}, u32[]{:S(2)}) copy-start(bf16[128,16,128]{2,1,0:T(8,128)(2,1)} %param.9) | copy-start | bytes 1572868
  7.1 1.0 copy-start.1
  124.8 2.2 %copy-start.3 = (bf16[128,2,8,128]{3,2,1,0:T(8,128)(2,1)S(1)}, bf16[128,2,8,128]{3,2,1,0:T(8,128)(2,1)}, u32[]{:S(2)}) copy-start(bf16[128,2,8,128]{3,2,1,0:T(8,128)(2,1)} %get-tuple-element.5) | copy-start | bytes 1572868

commit v11 on v10

--- a/solution.py
+++ b/solution.py
@@ -325,7 +325,8 @@
     queries = lq_ref[...]
     carried = jnp.einsum("hti,hij->htj", queries, upper, preferred_element_type=jnp.float32)
     carried = carried + jnp.einsum("hti,hij->htj", queries, lower, preferred_element_type=jnp.float32)
-    mixed = local_ref[...] + grow_ref[...] * carried
+    grow = jnp.transpose(grow_ref[...])
+    mixed = local_ref[...] + jnp.stack([grow[:, h : h + 1] for h in range(grow.shape[1])]) * carried
     column = jnp.sum(jnp.sum(mixed * mixed, axis=0), axis=1, keepdims=True)
     head_slots[head] = jnp.transpose(jnp.broadcast_to(column, (column.shape[0], 128)))[0:1, :]
 
@@ -358,7 +359,8 @@
     heads_all, width_all = lq_ref.shape[0] * head_count, lq_ref.shape[2]
     scale_row = lax.rsqrt(total / (heads_all * width_all) + 1e-06)
     scale = jnp.transpose(jnp.broadcast_to(scale_row, (128, scale_row.shape[1])))[:, 0:1]
-    lin_ref[...] = (mixed * scale[None] * gain_ref[...][:, None, :]).astype(lin_ref.dtype)
+    gain = gain_ref[...].astype(jnp.float32)
+    lin_ref[...] = (mixed * scale[None] * gain[:, None, :]).astype(lin_ref.dtype)
 
 
 def exclusive_scan(falling, state, kv, queries, bias, lq, local, grow, gain, axis):
@@ -547,8 +549,8 @@
         jnp.where(visible, 0.0, -jnp.inf).astype(jnp.float32),
         linear_query_rows.transpose(1, 0, 2),
         local_part,
-        jnp.exp(cumulated)[:, :, None],
-        norm_gain.astype(jnp.float32),
+        jnp.exp(cumulated),
+        norm_gain,
         "seq",
     )
     lin_out = lin_out.transpose(1, 0, 2)

time: 130 us -> 128 us (0.985)
  local copies, waits for them, and re-layouts: 7.31 us -> 5.94 us
    exp x1 -> x0, local copies, waits for them, and re-layouts: 1.38 us -> none  [body(): jnp.exp(cumulated)[:, :, None]]
where the time goes in v11:
time: 128 us; the launch traced here: 125 us
  Pallas kernels  111 us (87%)
  local copies, waits for them, and re-layouts  5.94 us (5%)
  matrix products  3.57 us (3%)
  other arithmetic  3.37 us (3%)
  between operations  1.45 us (1%)
    pallas_call x1, Pallas kernels, exclusive_scan(): pl.pallas_call(functools.partial(scan_kernel, rounds, chunks, REACH), out...  111 us
    unnamed x11, local copies, waits for them, and re-layouts  4.09 us

profile of v11, /device:TPU:60, one launch (start us, length us, event | category | flops | bytes accessed | tf_op | source)
XLA Modules:
  0.0 125.3 jit_solution(7357479994441565682)
XLA Ops:
  0.6 0.0 copy-start
  0.6 0.0 copy-start.2
  1.4 1.0 reduce_window_sum.11
  2.4 0.2 slice_reduce_fusion
  2.6 0.7 broadcast_in_dim.25.fall_ref
  3.3 0.6 fusion.32
  3.9 0.1 copy.21
  4.0 0.9 copy_bitcast_fusion.1
  4.9 0.7 maximum_bitcast_fusion.kv_ref
  5.6 0.7 fusion.22.bias_ref
  6.3 0.0 copy-done.2
  6.3 0.0 copy-start.1
  6.3 0.9 copy.55
  7.2 0.1 copy-done.1
  7.3 0.3 subtract_convert_fusion
  7.7 0.0 copy-done
  7.7 1.7 %fusion.1.local_ref = f32[16,128,128]{2,1,0:T(8,128)} fusion(bf16[128,16,128]{2,1,0:T(8,128)(2,1)S(1)} %copy-done.1, f32[16,128]{1,0:T(8,128)S(1)} %reduce_window_sum.11, pred[128,128]{1,0:T(8,128)(4,1)S(1)} %iota_compare_fusion.1, bf16[128,16,128]{2,1,0:T(8,128)(2,1)S(1)} %copy-done.2, bf16[128,16,128]{2,1,0:T(8,128)(2,1)S(1)} %copy-done), kind=kOutput, calls=%fused_computation.3 | convolution fusion | flops 135266304 | bytes 2646016 | tf_op jit(solution)/shard_map/hts,shd->htd/dot_general | solution.py:541
  9.4 0.3 fusion.9
  9.8 1.5 %fusion.33 = (bf16[16,128,128]{2,1,0:T(8,128)(2,1)}, f32[16,128,128]{2,1,0:T(8,128)}) fusion(f32[16,128,128]{2,1,0:T(8,128)S(1)} %fusion.9, bf16[128,16,128]{2,1,0:T(8,128)(2,1)S(1)} %copy-done, bf16[128,16,128]{2,1,0:T(8,128)(2,1)S(1)} %get-tuple-element.12), kind=kOutput, calls=%fused_computation.50 | convolution fusion | flops 67633152 | bytes 3670016 | tf_op jit(solution)/shard_map/egz,egc->gzc/dot_general | solution.py:525
  11.3 111.0 %shard_map.104 = (f32[16,128,128]{2,1,0:T(8,128)}, bf16[128,2,8,128]{3,2,1,0:T(8,128)(2,1)}, bf16[16,128,128]{2,1,0:T(8,128)(2,1)}) custom-call(f32[16,128]{1,0:T(8,128)} %broadcast_in_dim.25.fall_ref, f32[16,128,128]{2,1,0:T(8,128)} %get-tuple-element.17.state_ref, bf16[16,128,128]{2,1,0:T(8,128)(2,1)} %get-tuple-element.16.sent0_ref, ...), custom_call_target="tpu_custom_call" | custom-call | tf_op jit(solution)/shard_map/pallas_call | solution.py:374
  122.3 0.0 copy-start.3
  122.3 2.2 %copy.30 = bf16[128,16,128]{2,1,0:T(8,128)(2,1)} copy(bf16[128,16,128]{2,0,1:T(8,128)(2,1)} %bitcast.19) | data formatting | bytes 1048576
  124.5 0.0 copy-done.3
  124.5 0.8 copy.58
  (3 shorter events, 0.0 us)
Async XLA Ops:
  0.6 7.1 %copy-start = (bf16[128,16,128]{2,1,0:T(8,128)(2,1)S(1)}, bf16[128,16,128]{2,1,0:T(8,128)(2,1)}, u32[]{:S(2)}) copy-start(bf16[128,16,128]{2,1,0:T(8,128)(2,1)} %param.11) | copy-start | bytes 1572868
  0.6 5.7 %copy-start.2 = (bf16[128,16,128]{2,1,0:T(8,128)(2,1)S(1)}, bf16[128,16,128]{2,1,0:T(8,128)(2,1)}, u32[]{:S(2)}) copy-start(bf16[128,16,128]{2,1,0:T(8,128)(2,1)} %param.9) | copy-start | bytes 1572868
  6.3 1.0 copy-start.1
  122.3 2.2 %copy-start.3 = (bf16[128,2,8,128]{3,2,1,0:T(8,128)(2,1)S(1)}, bf16[128,2,8,128]{3,2,1,0:T(8,128)(2,1)}, u32[]{:S(2)}) copy-start(bf16[128,2,8,128]{3,2,1,0:T(8,128)(2,1)} %get-tuple-element.5) | copy-start | bytes 1572868

commit v12 on v11

--- a/solution.py
+++ b/solution.py
@@ -277,7 +277,9 @@
             total = jnp.sum(exps, axis=-1, keepdims=True)
             probs = exps.reshape(tokens * group, -1).astype(jnp.bfloat16)
             summed = jnp.dot(probs, jnp.concatenate(values, axis=0), preferred_element_type=jnp.float32)
-            soft_ref[:, g] = (summed.reshape(tokens, group, -1) / total).astype(soft_ref.dtype)
+            soft_ref[:, pl.ds(g * group, group), :] = (summed.reshape(tokens, group, -1) / total).astype(
+                soft_ref.dtype
+            )
 
     for k in range(3, rounds):
         shift, last = 2**k, k == rounds - 1
@@ -360,7 +362,9 @@
     scale_row = lax.rsqrt(total / (heads_all * width_all) + 1e-06)
     scale = jnp.transpose(jnp.broadcast_to(scale_row, (128, scale_row.shape[1])))[:, 0:1]
     gain = gain_ref[...].astype(jnp.float32)
-    lin_ref[...] = (mixed * scale[None] * gain[:, None, :]).astype(lin_ref.dtype)
+    result = (mixed * scale[None] * gain[:, None, :]).astype(lin_ref.dtype)
+    for h in range(result.shape[0]):
+        lin_ref[:, h, :] = result[h]
 
 
 def exclusive_scan(falling, state, kv, queries, bias, lq, local, grow, gain, axis):
@@ -375,8 +379,8 @@
         functools.partial(scan_kernel, rounds, chunks, REACH),
         out_shape=(
             jax.ShapeDtypeStruct(state.shape, jnp.float32),
-            jax.ShapeDtypeStruct(queries.shape, queries.dtype),
-            jax.ShapeDtypeStruct(lq.shape, jnp.bfloat16),
+            jax.ShapeDtypeStruct((rows, heads, columns), queries.dtype),
+            jax.ShapeDtypeStruct((rows, heads, columns), jnp.bfloat16),
         ),
         in_specs=[vmem] * 10,
         out_specs=(vmem, vmem, vmem),
@@ -553,7 +557,6 @@
         norm_gain,
         "seq",
     )
-    lin_out = lin_out.transpose(1, 0, 2)
     soft_out = soft_out.reshape(row_count, heads_here, head_width)
     return (lin_out, soft_out)
 

time: 128 us -> 129 us (level)
  Pallas kernels: 111 us -> 113 us
    pallas_call x1, Pallas kernels: 111 us -> 113 us  [exclusive_scan(): pl.pallas_call(functools.partial(scan_kernel, rounds, chunks, REACH), out...]
where the time goes in v12:
time: 129 us; the launch traced here: 127 us
  Pallas kernels  113 us (88%)
  local copies, waits for them, and re-layouts  5.64 us (4%)
  matrix products  3.57 us (3%)
  other arithmetic  3.37 us (3%)
  between operations  1.45 us (1%)
    pallas_call x1, Pallas kernels, exclusive_scan(): pl.pallas_call(functools.partial(scan_kernel, rounds, chunks, REACH), out...  113 us
    unnamed x11, local copies, waits for them, and re-layouts  3.78 us

profile of v12, /device:TPU:60, one launch (start us, length us, event | category | flops | bytes accessed | tf_op | source)
XLA Modules:
  0.0 126.9 jit_solution(5242762283807910090)
XLA Ops:
  0.6 0.0 copy-start
  0.6 0.0 copy-start.2
  1.4 1.0 reduce_window_sum.11
  2.4 0.2 slice_reduce_fusion
  2.6 0.7 broadcast_in_dim.25.fall_ref
  3.3 0.6 fusion.32
  3.9 0.1 copy.20
  4.0 0.9 copy_bitcast_fusion.1
  4.9 0.7 maximum_bitcast_fusion.kv_ref
  5.6 0.7 fusion.22.bias_ref
  6.3 0.0 copy-done.2
  6.3 0.0 copy-start.1
  6.3 0.9 copy.53
  7.2 0.1 copy-done.1
  7.3 0.3 subtract_convert_fusion
  7.7 0.0 copy-done
  7.7 1.7 %fusion.1.local_ref = f32[16,128,128]{2,1,0:T(8,128)} fusion(bf16[128,16,128]{2,1,0:T(8,128)(2,1)S(1)} %copy-done.1, f32[16,128]{1,0:T(8,128)S(1)} %reduce_window_sum.11, pred[128,128]{1,0:T(8,128)(4,1)S(1)} %iota_compare_fusion.1, bf16[128,16,128]{2,1,0:T(8,128)(2,1)S(1)} %copy-done.2, bf16[128,16,128]{2,1,0:T(8,128)(2,1)S(1)} %copy-done), kind=kOutput, calls=%fused_computation.3 | convolution fusion | flops 135266304 | bytes 2646016 | tf_op jit(solution)/shard_map/hts,shd->htd/dot_general | solution.py:545
  9.4 0.3 fusion.9
  9.8 1.5 %fusion.33 = (bf16[16,128,128]{2,1,0:T(8,128)(2,1)}, f32[16,128,128]{2,1,0:T(8,128)}) fusion(f32[16,128,128]{2,1,0:T(8,128)S(1)} %fusion.9, bf16[128,16,128]{2,1,0:T(8,128)(2,1)S(1)} %copy-done, bf16[128,16,128]{2,1,0:T(8,128)(2,1)S(1)} %get-tuple-element.8), kind=kOutput, calls=%fused_computation.50 | convolution fusion | flops 67633152 | bytes 3670016 | tf_op jit(solution)/shard_map/egz,egc->gzc/dot_general | solution.py:529
  11.3 112.8 %shard_map.104 = (f32[16,128,128]{2,1,0:T(8,128)}, bf16[128,16,128]{2,1,0:T(8,128)(2,1)}, bf16[128,16,128]{2,1,0:T(8,128)(2,1)}) custom-call(f32[16,128]{1,0:T(8,128)} %broadcast_in_dim.25.fall_ref, f32[16,128,128]{2,1,0:T(8,128)} %get-tuple-element.13.state_ref, bf16[16,128,128]{2,1,0:T(8,128)(2,1)} %get-tuple-element.12.sent0_ref, ...), custom_call_target="tpu_custom_call" | custom-call | tf_op jit(solution)/shard_map/pallas_call | solution.py:378
  124.1 0.0 copy-start.3
  124.1 1.9 %copy.57 = bf16[128,16,128]{2,1,0:T(8,128)(2,1)} copy(bf16[128,16,128]{2,1,0:T(8,128)(2,1)} %get-tuple-element.20) | data formatting | bytes 1048576
  126.1 0.0 copy-done.3
  126.1 0.8 copy.58
  (3 shorter events, 0.0 us)
Async XLA Ops:
  0.6 7.1 %copy-start = (bf16[128,16,128]{2,1,0:T(8,128)(2,1)S(1)}, bf16[128,16,128]{2,1,0:T(8,128)(2,1)}, u32[]{:S(2)}) copy-start(bf16[128,16,128]{2,1,0:T(8,128)(2,1)} %param.11) | copy-start | bytes 1572868
  0.6 5.7 %copy-start.2 = (bf16[128,16,128]{2,1,0:T(8,128)(2,1)S(1)}, bf16[128,16,128]{2,1,0:T(8,128)(2,1)}, u32[]{:S(2)}) copy-start(bf16[128,16,128]{2,1,0:T(8,128)(2,1)} %param.9) | copy-start | bytes 1572868
  6.3 1.0 copy-start.1
  124.1 1.9 %copy-start.3 = (bf16[128,16,128]{2,1,0:T(8,128)(2,1)S(1)}, bf16[128,16,128]{2,1,0:T(8,128)(2,1)}, u32[]{:S(2)}) copy-start(bf16[128,16,128]{2,1,0:T(8,128)(2,1)} %get-tuple-element.21) | copy-start | bytes 1572868

commit v13 on v11

--- a/solution.py
+++ b/solution.py
@@ -367,7 +367,7 @@
     length = lax.axis_size(axis)
     rounds = length.bit_length() - 1
     stages = rounds + 3
-    chunks = 8
+    chunks = 4
     heads, rows, columns = state.shape
     fall_rows = jnp.broadcast_to(falling[:, None], (heads, columns))
     vmem = pl.BlockSpec(memory_space=pltpu.VMEM)

time: 128 us -> 128 us (level)
  no operation moved by 1% of the time
where the time goes in v13:
time: 128 us; the launch traced here: 126 us
  Pallas kernels  112 us (88%)
  local copies, waits for them, and re-layouts  5.94 us (5%)
  matrix products  3.57 us (3%)
  other arithmetic  3.37 us (3%)
  between operations  1.45 us (1%)
    pallas_call x1, Pallas kernels, exclusive_scan(): pl.pallas_call(functools.partial(scan_kernel, rounds, chunks, REACH), out...  112 us
    unnamed x11, local copies, waits for them, and re-layouts  4.09 us

profile of v13, /device:TPU:60, one launch (start us, length us, event | category | flops | bytes accessed | tf_op | source)
XLA Modules:
  0.0 126.0 jit_solution(5177109757068574054)
XLA Ops:
  0.6 0.0 copy-start
  0.6 0.0 copy-start.2
  1.4 1.0 reduce_window_sum.11
  2.4 0.2 slice_reduce_fusion
  2.6 0.7 broadcast_in_dim.25.fall_ref
  3.3 0.6 fusion.32
  3.9 0.1 copy.21
  4.0 0.9 copy_bitcast_fusion.1
  4.9 0.7 maximum_bitcast_fusion.kv_ref
  5.6 0.7 fusion.22.bias_ref
  6.3 0.0 copy-done.2
  6.3 0.0 copy-start.1
  6.3 0.9 copy.55
  7.2 0.1 copy-done.1
  7.3 0.3 subtract_convert_fusion
  7.7 0.0 copy-done
  7.7 1.7 %fusion.1.local_ref = f32[16,128,128]{2,1,0:T(8,128)} fusion(bf16[128,16,128]{2,1,0:T(8,128)(2,1)S(1)} %copy-done.1, f32[16,128]{1,0:T(8,128)S(1)} %reduce_window_sum.11, pred[128,128]{1,0:T(8,128)(4,1)S(1)} %iota_compare_fusion.1, bf16[128,16,128]{2,1,0:T(8,128)(2,1)S(1)} %copy-done.2, bf16[128,16,128]{2,1,0:T(8,128)(2,1)S(1)} %copy-done), kind=kOutput, calls=%fused_computation.3 | convolution fusion | flops 135266304 | bytes 2646016 | tf_op jit(solution)/shard_map/hts,shd->htd/dot_general | solution.py:541
  9.4 0.3 fusion.9
  9.8 1.5 %fusion.33 = (bf16[16,128,128]{2,1,0:T(8,128)(2,1)}, f32[16,128,128]{2,1,0:T(8,128)}) fusion(f32[16,128,128]{2,1,0:T(8,128)S(1)} %fusion.9, bf16[128,16,128]{2,1,0:T(8,128)(2,1)S(1)} %copy-done, bf16[128,16,128]{2,1,0:T(8,128)(2,1)S(1)} %get-tuple-element.12), kind=kOutput, calls=%fused_computation.50 | convolution fusion | flops 67633152 | bytes 3670016 | tf_op jit(solution)/shard_map/egz,egc->gzc/dot_general | solution.py:525
  11.3 111.7 %shard_map.104 = (f32[16,128,128]{2,1,0:T(8,128)}, bf16[128,2,8,128]{3,2,1,0:T(8,128)(2,1)}, bf16[16,128,128]{2,1,0:T(8,128)(2,1)}) custom-call(f32[16,128]{1,0:T(8,128)} %broadcast_in_dim.25.fall_ref, f32[16,128,128]{2,1,0:T(8,128)} %get-tuple-element.17.state_ref, bf16[16,128,128]{2,1,0:T(8,128)(2,1)} %get-tuple-element.16.sent0_ref, ...), custom_call_target="tpu_custom_call" | custom-call | tf_op jit(solution)/shard_map/pallas_call | solution.py:374
  122.9 0.0 copy-start.3
  123.0 2.2 %copy.30 = bf16[128,16,128]{2,1,0:T(8,128)(2,1)} copy(bf16[128,16,128]{2,0,1:T(8,128)(2,1)} %bitcast.19) | data formatting | bytes 1048576
  125.2 0.0 copy-done.3
  125.2 0.8 copy.58
  (3 shorter events, 0.0 us)
Async XLA Ops:
  0.6 7.1 %copy-start = (bf16[128,16,128]{2,1,0:T(8,128)(2,1)S(1)}, bf16[128,16,128]{2,1,0:T(8,128)(2,1)}, u32[]{:S(2)}) copy-start(bf16[128,16,128]{2,1,0:T(8,128)(2,1)} %param.11) | copy-start | bytes 1572868
  0.6 5.7 %copy-start.2 = (bf16[128,16,128]{2,1,0:T(8,128)(2,1)S(1)}, bf16[128,16,128]{2,1,0:T(8,128)(2,1)}, u32[]{:S(2)}) copy-start(bf16[128,16,128]{2,1,0:T(8,128)(2,1)} %param.9) | copy-start | bytes 1572868
  6.3 1.0 copy-start.1
  122.9 2.2 %copy-start.3 = (bf16[128,2,8,128]{3,2,1,0:T(8,128)(2,1)S(1)}, bf16[128,2,8,128]{3,2,1,0:T(8,128)(2,1)}, u32[]{:S(2)}) copy-start(bf16[128,2,8,128]{3,2,1,0:T(8,128)(2,1)} %get-tuple-element.5) | copy-start | bytes 1572868

commit v14 on v11

--- a/solution.py
+++ b/solution.py
@@ -128,7 +128,8 @@
             device_id_type=MESH,
         )
 
-    outgoing_fall[0] = fall_ref[...]
+    fall = jnp.broadcast_to(fall_ref[...], whole_fall.shape)
+    outgoing_fall[0] = fall
 
     @pl.when(ahead(1) == 1)
     def _():
@@ -143,9 +144,9 @@
             state_copy(back0, sent0_ref, c, me - 1).start()
 
     whole[...] = state_ref[...]
-    whole_fall[...] = fall_ref[...]
+    whole_fall[...] = fall
     suffix[...] = state_ref[...]
-    suffix_fall[...] = fall_ref[...]
+    suffix_fall[...] = fall
     out_ref[...] = jnp.zeros_like(out_ref)
     out_fall[...] = jnp.ones_like(out_fall)
 
@@ -369,7 +370,7 @@
     stages = rounds + 3
     chunks = 8
     heads, rows, columns = state.shape
-    fall_rows = jnp.broadcast_to(falling[:, None], (heads, columns))
+    fall_rows = falling[:, None]
     vmem = pl.BlockSpec(memory_space=pltpu.VMEM)
     return pl.pallas_call(
         functools.partial(scan_kernel, rounds, chunks, REACH),

time: 128 us -> 127 us (level)
  no operation moved by 1% of the time
where the time goes in v14:
time: 127 us; the launch traced here: 125 us
  Pallas kernels  111 us (87%)
  local copies, waits for them, and re-layouts  5.87 us (5%)
  matrix products  3.57 us (3%)
  other arithmetic  3.37 us (3%)
  between operations  1.45 us (1%)
    pallas_call x1, Pallas kernels, exclusive_scan(): pl.pallas_call(functools.partial(scan_kernel, rounds, chunks, REACH), out...  111 us
    unnamed x11, local copies, waits for them, and re-layouts  4.09 us

profile of v14, /device:TPU:60, one launch (start us, length us, event | category | flops | bytes accessed | tf_op | source)
XLA Modules:
  0.0 125.3 jit_solution(14677766275487951391)
XLA Ops:
  0.6 0.0 copy-start
  0.6 0.0 copy-start.2
  1.4 1.0 reduce_window_sum.11
  2.4 0.8 slice_reduce_fusion
  3.2 0.6 fusion.32
  3.8 0.1 copy.21
  3.9 0.9 copy_bitcast_fusion.1
  4.8 0.7 maximum_bitcast_fusion.kv_ref
  5.5 0.8 fusion.22.bias_ref
  6.2 0.0 copy-done.2
  6.2 0.0 copy-start.1
  6.2 0.9 copy.55
  7.2 0.1 copy-done.1
  7.3 0.3 subtract_convert_fusion
  7.6 0.0 copy-done
  7.6 1.7 %fusion.1.local_ref = f32[16,128,128]{2,1,0:T(8,128)} fusion(bf16[128,16,128]{2,1,0:T(8,128)(2,1)S(1)} %copy-done.1, f32[16,128]{1,0:T(8,128)S(1)} %reduce_window_sum.11, pred[128,128]{1,0:T(8,128)(4,1)S(1)} %iota_compare_fusion.1, bf16[128,16,128]{2,1,0:T(8,128)(2,1)S(1)} %copy-done.2, bf16[128,16,128]{2,1,0:T(8,128)(2,1)S(1)} %copy-done), kind=kOutput, calls=%fused_computation.3 | convolution fusion | flops 135266304 | bytes 2646016 | tf_op jit(solution)/shard_map/hts,shd->htd/dot_general | solution.py:542
  9.4 0.3 fusion.9
  9.7 1.5 %fusion.33 = (bf16[16,128,128]{2,1,0:T(8,128)(2,1)}, f32[16,128,128]{2,1,0:T(8,128)}) fusion(f32[16,128,128]{2,1,0:T(8,128)S(1)} %fusion.9, bf16[128,16,128]{2,1,0:T(8,128)(2,1)S(1)} %copy-done, bf16[128,16,128]{2,1,0:T(8,128)(2,1)S(1)} %get-tuple-element.10), kind=kOutput, calls=%fused_computation.50 | convolution fusion | flops 67633152 | bytes 3670016 | tf_op jit(solution)/shard_map/egz,egc->gzc/dot_general | solution.py:526
  11.2 111.0 %shard_map.104 = (f32[16,128,128]{2,1,0:T(8,128)}, bf16[128,2,8,128]{3,2,1,0:T(8,128)(2,1)}, bf16[16,128,128]{2,1,0:T(8,128)(2,1)}) custom-call(f32[16,1]{1,0:T(8,128)} %get-tuple-element.15.fall_ref, f32[16,128,128]{2,1,0:T(8,128)} %get-tuple-element.17.state_ref, bf16[16,128,128]{2,1,0:T(8,128)(2,1)} %get-tuple-element.16.sent0_ref, ...), custom_call_target="tpu_custom_call" | custom-call | tf_op jit(solution)/shard_map/pallas_call | solution.py:375
  122.2 0.0 copy-start.3
  122.2 2.2 %copy.30 = bf16[128,16,128]{2,1,0:T(8,128)(2,1)} copy(bf16[128,16,128]{2,0,1:T(8,128)(2,1)} %bitcast.19) | data formatting | bytes 1048576
  124.5 0.0 copy-done.3
  124.5 0.8 copy.58
  (3 shorter events, 0.0 us)
Async XLA Ops:
  0.6 7.0 %copy-start = (bf16[128,16,128]{2,1,0:T(8,128)(2,1)S(1)}, bf16[128,16,128]{2,1,0:T(8,128)(2,1)}, u32[]{:S(2)}) copy-start(bf16[128,16,128]{2,1,0:T(8,128)(2,1)} %param.11) | copy-start | bytes 1572868
  0.6 5.6 %copy-start.2 = (bf16[128,16,128]{2,1,0:T(8,128)(2,1)S(1)}, bf16[128,16,128]{2,1,0:T(8,128)(2,1)}, u32[]{:S(2)}) copy-start(bf16[128,16,128]{2,1,0:T(8,128)(2,1)} %param.9) | copy-start | bytes 1572868
  6.2 1.0 copy-start.1
  122.2 2.2 %copy-start.3 = (bf16[128,2,8,128]{3,2,1,0:T(8,128)(2,1)S(1)}, bf16[128,2,8,128]{3,2,1,0:T(8,128)(2,1)}, u32[]{:S(2)}) copy-start(bf16[128,2,8,128]{3,2,1,0:T(8,128)(2,1)} %get-tuple-element.5) | copy-start | bytes 1572868

commit v15 on v14

--- a/solution.py
+++ b/solution.py
@@ -323,9 +323,12 @@
     prior = out_ref[...]
     upper = prior.astype(jnp.bfloat16)
     lower = (prior - upper.astype(jnp.float32)).astype(jnp.bfloat16)
-    queries = lq_ref[...]
-    carried = jnp.einsum("hti,hij->htj", queries, upper, preferred_element_type=jnp.float32)
-    carried = carried + jnp.einsum("hti,hij->htj", queries, lower, preferred_element_type=jnp.float32)
+    parts = []
+    for h in range(prior.shape[0]):
+        query = lq_ref[:, h, :]
+        part = jnp.dot(query, upper[h], preferred_element_type=jnp.float32)
+        parts.append(part + jnp.dot(query, lower[h], preferred_element_type=jnp.float32))
+    carried = jnp.stack(parts)
     grow = jnp.transpose(grow_ref[...])
     mixed = local_ref[...] + jnp.stack([grow[:, h : h + 1] for h in range(grow.shape[1])]) * carried
     column = jnp.sum(jnp.sum(mixed * mixed, axis=0), axis=1, keepdims=True)
@@ -357,7 +360,7 @@
     total = head_slots[0]
     for other in range(1, head_count):
         total = total + head_slots[other]
-    heads_all, width_all = lq_ref.shape[0] * head_count, lq_ref.shape[2]
+    heads_all, width_all = lq_ref.shape[1] * head_count, lq_ref.shape[2]
     scale_row = lax.rsqrt(total / (heads_all * width_all) + 1e-06)
     scale = jnp.transpose(jnp.broadcast_to(scale_row, (128, scale_row.shape[1])))[:, 0:1]
     gain = gain_ref[...].astype(jnp.float32)
@@ -377,7 +380,7 @@
         out_shape=(
             jax.ShapeDtypeStruct(state.shape, jnp.float32),
             jax.ShapeDtypeStruct(queries.shape, queries.dtype),
-            jax.ShapeDtypeStruct(lq.shape, jnp.bfloat16),
+            jax.ShapeDtypeStruct(state.shape, jnp.bfloat16),
         ),
         in_specs=[vmem] * 10,
         out_specs=(vmem, vmem, vmem),
@@ -548,7 +551,7 @@
         jnp.stack([soft_keys, soft_values]).transpose(0, 2, 1, 3),
         soft_queries.reshape(row_count, kv_here, group, head_width),
         jnp.where(visible, 0.0, -jnp.inf).astype(jnp.float32),
-        linear_query_rows.transpose(1, 0, 2),
+        linear_query_rows,
         local_part,
         jnp.exp(cumulated),
         norm_gain,

time: 127 us -> 128 us (level)
    unnamed x11 -> x10, local copies, waits for them, and re-layouts: 4.09 us -> 3.73 us
where the time goes in v15:
time: 128 us; the launch traced here: 125 us
  Pallas kernels  111 us (87%)
  local copies, waits for them, and re-layouts  5.51 us (4%)
  matrix products  3.57 us (3%)
  other arithmetic  3.36 us (3%)
  between operations  1.45 us (1%)
    pallas_call x1, Pallas kernels, exclusive_scan(): pl.pallas_call(functools.partial(scan_kernel, rounds, chunks, REACH), out...  111 us
    unnamed x10, local copies, waits for them, and re-layouts  3.73 us

profile of v15, /device:TPU:60, one launch (start us, length us, event | category | flops | bytes accessed | tf_op | source)
XLA Modules:
  0.0 125.3 jit_solution(2110501007695291770)
XLA Ops:
  0.6 0.0 copy-start
  0.6 0.0 copy-start.1
  1.4 1.0 reduce_window_sum.11
  2.4 0.8 slice_reduce_fusion
  3.2 0.6 fusion.32
  3.8 0.1 copy.20
  3.9 0.9 copy_bitcast_fusion
  4.8 0.6 maximum_bitcast_fusion.kv_ref
  5.5 0.8 fusion.22.bias_ref
  6.2 0.0 copy-done.1
  6.2 0.0 copy-start.2
  6.2 0.3 subtract_convert_fusion
  6.6 0.0 copy-done
  6.6 0.7 copy-done.2
  7.3 1.7 %fusion.1.local_ref = f32[16,128,128]{2,1,0:T(8,128)} fusion(bf16[128,16,128]{2,1,0:T(8,128)(2,1)S(1)} %copy-done.1, bf16[128,16,128]{2,1,0:T(8,128)(2,1)S(1)} %copy-done.2, f32[16,128]{1,0:T(8,128)S(1)} %reduce_window_sum.11, pred[128,128]{1,0:T(8,128)(4,1)S(1)} %iota_compare_fusion.1, bf16[128,16,128]{2,1,0:T(8,128)(2,1)S(1)} %copy-done), kind=kOutput, calls=%fused_computation.3 | convolution fusion | flops 135266304 | bytes 2646016 | tf_op jit(solution)/shard_map/hts,shd->htd/dot_general | solution.py:545
  9.0 0.3 fusion.11
  9.3 1.5 %fusion.33 = (bf16[16,128,128]{2,1,0:T(8,128)(2,1)}, f32[16,128,128]{2,1,0:T(8,128)}) fusion(f32[16,128,128]{2,1,0:T(8,128)S(1)} %fusion.11, bf16[128,16,128]{2,1,0:T(8,128)(2,1)S(1)} %copy-done, bf16[128,16,128]{2,1,0:T(8,128)(2,1)S(1)} %get-tuple-element.10), kind=kOutput, calls=%fused_computation.49 | convolution fusion | flops 67633152 | bytes 3670016 | tf_op jit(solution)/shard_map/egz,egc->gzc/dot_general | solution.py:529
  10.8 111.5 %shard_map.104 = (f32[16,128,128]{2,1,0:T(8,128)}, bf16[128,2,8,128]{3,2,1,0:T(8,128)(2,1)}, bf16[16,128,128]{2,1,0:T(8,128)(2,1)}) custom-call(f32[16,1]{1,0:T(8,128)} %get-tuple-element.15.fall_ref, f32[16,128,128]{2,1,0:T(8,128)} %get-tuple-element.17.state_ref, bf16[16,128,128]{2,1,0:T(8,128)(2,1)} %get-tuple-element.16.sent0_ref, ...), custom_call_target="tpu_custom_call" | custom-call | tf_op jit(solution)/shard_map/pallas_call | solution.py:378
  122.3 0.0 copy-start.3
  122.3 2.2 %copy.28 = bf16[128,16,128]{2,1,0:T(8,128)(2,1)} copy(bf16[128,16,128]{2,0,1:T(8,128)(2,1)} %bitcast.15) | data formatting | bytes 1048576
  124.6 0.0 copy-done.3
  124.6 0.8 copy.55
  (3 shorter events, 0.0 us)
Async XLA Ops:
  0.6 5.9 %copy-start = (bf16[128,16,128]{2,1,0:T(8,128)(2,1)S(1)}, bf16[128,16,128]{2,1,0:T(8,128)(2,1)}, u32[]{:S(2)}) copy-start(bf16[128,16,128]{2,1,0:T(8,128)(2,1)} %param.11) | copy-start | bytes 1572868
  0.6 5.6 %copy-start.1 = (bf16[128,16,128]{2,1,0:T(8,128)(2,1)S(1)}, bf16[128,16,128]{2,1,0:T(8,128)(2,1)}, u32[]{:S(2)}) copy-start(bf16[128,16,128]{2,1,0:T(8,128)(2,1)} %param.10) | copy-start | bytes 1572868
  6.2 1.0 copy-start.2
  122.3 2.2 %copy-start.3 = (bf16[128,2,8,128]{3,2,1,0:T(8,128)(2,1)S(1)}, bf16[128,2,8,128]{3,2,1,0:T(8,128)(2,1)}, u32[]{:S(2)}) copy-start(bf16[128,2,8,128]{3,2,1,0:T(8,128)(2,1)} %get-tuple-element.5) | copy-start | bytes 1572868

commit v16 on v15

--- a/solution.py
+++ b/solution.py
@@ -25,7 +25,9 @@
     q_ref,
     bias_ref,
     lq_ref,
-    local_ref,
+    lk_ref,
+    lv_ref,
+    cum_ref,
     grow_ref,
     gain_ref,
     out_ref,
@@ -50,6 +52,7 @@
     head_slots,
     head_send,
     head_recv,
+    local_ref,
 ):
     me = lax.axis_index("seq")
     head = lax.axis_index("head")
@@ -243,6 +246,20 @@
 
     if rounds > 3:
         send_fall(3, ahead(8), whole_fall, 8)
+
+    def local_part():
+        cum = cum_ref[...]
+        cum_col = jnp.transpose(cum)
+        tokens = cum.shape[1]
+        rows_at = lax.broadcasted_iota(jnp.int32, (tokens, tokens), 0)
+        cols_at = lax.broadcasted_iota(jnp.int32, (tokens, tokens), 1)
+        for h in range(cum.shape[0]):
+            scores = lax.dot_general(
+                lq_ref[:, h, :], lk_ref[:, h, :], (((1,), (1,)), ((), ())), preferred_element_type=jnp.float32
+            )
+            gap = jnp.where(rows_at >= cols_at, cum_col[:, h : h + 1] - cum[h : h + 1, :], -jnp.inf)
+            weights = (scores * jnp.exp(gap)).astype(jnp.bfloat16)
+            local_ref[h] = jnp.dot(weights, lv_ref[:, h, :], preferred_element_type=jnp.float32)
 
     def attention():
         for dist in range(1, reach + 1):
@@ -284,6 +301,7 @@
         shift, last = 2**k, k == rounds - 1
         if last:
             attention()
+            local_part()
         for c in range(chunks):
             forward_chunk(k, shift, c, update_whole=not last)
             if not last:
@@ -367,7 +385,7 @@
     lin_ref[...] = (mixed * scale[None] * gain[:, None, :]).astype(lin_ref.dtype)
 
 
-def exclusive_scan(falling, state, kv, queries, bias, lq, local, grow, gain, axis):
+def exclusive_scan(falling, state, kv, queries, bias, lq, lk, lv, cum, grow, gain, axis):
     length = lax.axis_size(axis)
     rounds = length.bit_length() - 1
     stages = rounds + 3
@@ -382,7 +400,7 @@
             jax.ShapeDtypeStruct(queries.shape, queries.dtype),
             jax.ShapeDtypeStruct(state.shape, jnp.bfloat16),
         ),
-        in_specs=[vmem] * 10,
+        in_specs=[vmem] * 12,
         out_specs=(vmem, vmem, vmem),
         scratch_shapes=[
             pltpu.VMEM(state.shape, jnp.float32),
@@ -404,9 +422,10 @@
             pltpu.VMEM((lax.axis_size("head"), 1, columns), jnp.float32),
             pltpu.SemaphoreType.DMA((lax.axis_size("head"),)),
             pltpu.SemaphoreType.DMA((lax.axis_size("head"),)),
+            pltpu.VMEM(state.shape, jnp.float32),
         ],
         compiler_params=pltpu.CompilerParams(collective_id=0, has_side_effects=True),
-    )(fall_rows, state, state.astype(jnp.bfloat16), kv, queries, bias, lq, local, grow, gain)
+    )(fall_rows, state, state.astype(jnp.bfloat16), kv, queries, bias, lq, lk, lv, cum, grow, gain)
 
 
 def head_sum_kernel(count, value_ref, out_ref, slots, send_sem, recv_sem):
@@ -537,14 +556,6 @@
     key_block = block_index - REACH + key_index // row_count
     causal = (key_index % row_count)[None, :] <= token_locations[:, None]
     visible = ((key_block[None, :] < block_index) | causal) & (key_block[None, :] >= window_start[0])
-    lin_scores = jnp.einsum(
-        "thd,shd->hts", linear_query_rows, lin_keys, preferred_element_type=jnp.float32
-    )
-    gap = jnp.where(lower_mask[None], cumulated[:, :, None] - cumulated[:, None, :], -jnp.inf)
-    lin_weights = (lin_scores * jnp.exp(gap)).astype(jnp.bfloat16)
-    local_part = jnp.einsum(
-        "hts,shd->htd", lin_weights, linear_value_rows, preferred_element_type=jnp.float32
-    )
     normed, soft_out, lin_out = exclusive_scan(
         falling,
         recurrent_state,
@@ -552,7 +563,9 @@
         soft_queries.reshape(row_count, kv_here, group, head_width),
         jnp.where(visible, 0.0, -jnp.inf).astype(jnp.float32),
         linear_query_rows,
-        local_part,
+        lin_keys,
+        linear_value_rows,
+        cumulated,
         jnp.exp(cumulated),
         norm_gain,
         "seq",

time: 128 us -> 126 us (0.984)
  matrix products: 3.57 us -> 1.84 us
    dot_general x1 -> x0, matrix products: 1.73 us -> none  [body(): jnp.einsum('hts,shd->htd', lin_weights, linear_value_rows, preferred_elem...]
where the time goes in v16:
time: 126 us; the launch traced here: 124 us
  Pallas kernels  112 us (89%)
  local copies, waits for them, and re-layouts  5.52 us (4%)
  other arithmetic  3.37 us (3%)
  matrix products  1.84 us (1%)
  between operations  1.4 us (1%)
    pallas_call x1, Pallas kernels, exclusive_scan(): pl.pallas_call(functools.partial(scan_kernel, rounds, chunks, REACH), out...  112 us
    unnamed x10, local copies, waits for them, and re-layouts  3.74 us

profile of v16, /device:TPU:60, one launch (start us, length us, event | category | flops | bytes accessed | tf_op | source)
XLA Modules:
  0.0 123.9 jit_solution(677917575327773132)
XLA Ops:
  0.6 0.0 copy-start.1
  1.4 1.0 reduce_window_sum.11.cum_ref
  2.4 0.0 copy-start.3
  2.4 0.8 slice_reduce_fusion
  3.1 0.0 copy-done.3
  3.1 0.6 fusion.17
  3.8 0.1 copy.19
  3.9 0.9 copy_bitcast_fusion
  4.8 0.7 maximum_bitcast_fusion.kv_ref
  5.4 0.8 fusion.8.bias_ref
  6.2 0.0 copy-done.1
  6.2 0.0 copy-start
  6.2 0.3 subtract_convert_fusion
  6.5 0.7 copy-done
  7.2 0.3 fusion.2
  7.6 1.5 %fusion.18 = (bf16[16,128,128]{2,1,0:T(8,128)(2,1)}, f32[16,128,128]{2,1,0:T(8,128)}) fusion(f32[16,128,128]{2,1,0:T(8,128)S(1)} %fusion.2, bf16[128,16,128]{2,1,0:T(8,128)(2,1)S(1)} %copy-done, bf16[128,16,128]{2,1,0:T(8,128)(2,1)S(1)} %get-tuple-element.10), kind=kOutput, calls=%fused_computation.34 | convolution fusion | flops 67633152 | bytes 3670016 | tf_op jit(solution)/shard_map/egz,egc->gzc/dot_general | solution.py:548
  9.1 111.8 %shard_map.104 = (f32[16,128,128]{2,1,0:T(8,128)}, bf16[128,2,8,128]{3,2,1,0:T(8,128)(2,1)}, bf16[16,128,128]{2,1,0:T(8,128)(2,1)}) custom-call(f32[16,1]{1,0:T(8,128)} %get-tuple-element.15.fall_ref, f32[16,128,128]{2,1,0:T(8,128)} %get-tuple-element.17.state_ref, bf16[16,128,128]{2,1,0:T(8,128)(2,1)} %get-tuple-element.16.sent0_ref, ...), custom_call_target="tpu_custom_call" | custom-call | tf_op jit(solution)/shard_map/pallas_call | solution.py:396
  120.8 0.0 copy-start.2
  120.8 2.2 %copy.26 = bf16[128,16,128]{2,1,0:T(8,128)(2,1)} copy(bf16[128,16,128]{2,0,1:T(8,128)(2,1)} %bitcast.15) | data formatting | bytes 1048576
  123.1 0.0 copy-done.2
  123.1 0.8 copy.43
  (2 shorter events, 0.0 us)
Async XLA Ops:
  0.6 5.6 %copy-start.1 = (bf16[128,16,128]{2,1,0:T(8,128)(2,1)S(1)}, bf16[128,16,128]{2,1,0:T(8,128)(2,1)}, u32[]{:S(2)}) copy-start(bf16[128,16,128]{2,1,0:T(8,128)(2,1)} %lk_ref.1) | copy-start | bytes 1572868
  2.4 0.8 copy-start.3
  6.2 1.0 copy-start
  120.8 2.2 %copy-start.2 = (bf16[128,2,8,128]{3,2,1,0:T(8,128)(2,1)S(1)}, bf16[128,2,8,128]{3,2,1,0:T(8,128)(2,1)}, u32[]{:S(2)}) copy-start(bf16[128,2,8,128]{3,2,1,0:T(8,128)(2,1)} %get-tuple-element.5) | copy-start | bytes 1572868

commit v17 on v16

--- a/solution.py
+++ b/solution.py
@@ -28,7 +28,6 @@
     lk_ref,
     lv_ref,
     cum_ref,
-    grow_ref,
     gain_ref,
     out_ref,
     soft_ref,
@@ -347,7 +346,7 @@
         part = jnp.dot(query, upper[h], preferred_element_type=jnp.float32)
         parts.append(part + jnp.dot(query, lower[h], preferred_element_type=jnp.float32))
     carried = jnp.stack(parts)
-    grow = jnp.transpose(grow_ref[...])
+    grow = jnp.transpose(jnp.exp(cum_ref[...]))
     mixed = local_ref[...] + jnp.stack([grow[:, h : h + 1] for h in range(grow.shape[1])]) * carried
     column = jnp.sum(jnp.sum(mixed * mixed, axis=0), axis=1, keepdims=True)
     head_slots[head] = jnp.transpose(jnp.broadcast_to(column, (column.shape[0], 128)))[0:1, :]
@@ -385,7 +384,7 @@
     lin_ref[...] = (mixed * scale[None] * gain[:, None, :]).astype(lin_ref.dtype)
 
 
-def exclusive_scan(falling, state, kv, queries, bias, lq, lk, lv, cum, grow, gain, axis):
+def exclusive_scan(falling, state, kv, queries, bias, lq, lk, lv, cum, gain, axis):
     length = lax.axis_size(axis)
     rounds = length.bit_length() - 1
     stages = rounds + 3
@@ -400,7 +399,7 @@
             jax.ShapeDtypeStruct(queries.shape, queries.dtype),
             jax.ShapeDtypeStruct(state.shape, jnp.bfloat16),
         ),
-        in_specs=[vmem] * 12,
+        in_specs=[vmem] * 11,
         out_specs=(vmem, vmem, vmem),
         scratch_shapes=[
             pltpu.VMEM(state.shape, jnp.float32),
@@ -425,7 +424,7 @@
             pltpu.VMEM(state.shape, jnp.float32),
         ],
         compiler_params=pltpu.CompilerParams(collective_id=0, has_side_effects=True),
-    )(fall_rows, state, state.astype(jnp.bfloat16), kv, queries, bias, lq, lk, lv, cum, grow, gain)
+    )(fall_rows, state, state.astype(jnp.bfloat16), kv, queries, bias, lq, lk, lv, cum, gain)
 
 
 def head_sum_kernel(count, value_ref, out_ref, slots, send_sem, recv_sem):
@@ -566,7 +565,6 @@
         lin_keys,
         linear_value_rows,
         cumulated,
-        jnp.exp(cumulated),
         norm_gain,
         "seq",
     )

time: 126 us -> 125 us (level)
  no operation moved by 1% of the time
where the time goes in v17:
time: 125 us; the launch traced here: 123 us
  Pallas kernels  112 us (90%)
  local copies, waits for them, and re-layouts  5.52 us (4%)
  other arithmetic  2.83 us (2%)
  matrix products  1.84 us (1%)
  between operations  1.4 us (1%)
    pallas_call x1, Pallas kernels, exclusive_scan(): pl.pallas_call(functools.partial(scan_kernel, rounds, chunks, REACH), out...  112 us
    unnamed x10, local copies, waits for them, and re-layouts  3.74 us

profile of v17, /device:TPU:60, one launch (start us, length us, event | category | flops | bytes accessed | tf_op | source)
XLA Modules:
  0.0 123.3 jit_solution(9538030501904904849)
XLA Ops:
  0.6 0.0 copy-start.1
  1.4 1.0 reduce_window_sum.11.cum_ref
  2.4 0.0 copy-start.3
  2.4 0.8 slice_reduce_fusion
  3.1 0.0 copy-done.3
  3.1 0.1 exponential_bitcast_fusion
  3.2 0.1 copy.19
  3.3 0.9 copy_bitcast_fusion
  4.2 0.7 maximum_bitcast_fusion.kv_ref
  4.9 0.8 fusion.8.bias_ref
  5.7 0.0 copy-done.1
  5.7 0.0 copy-start
  5.7 0.3 subtract_convert_fusion
  6.0 0.7 copy-done
  6.7 0.3 fusion.2
  7.1 1.5 %fusion.17 = (bf16[16,128,128]{2,1,0:T(8,128)(2,1)}, f32[16,128,128]{2,1,0:T(8,128)}) fusion(f32[16,128,128]{2,1,0:T(8,128)S(1)} %fusion.2, bf16[128,16,128]{2,1,0:T(8,128)(2,1)S(1)} %copy-done, bf16[128,16,128]{2,1,0:T(8,128)(2,1)S(1)} %get-tuple-element.10), kind=kOutput, calls=%fused_computation.33 | convolution fusion | flops 67633152 | bytes 3670016 | tf_op jit(solution)/shard_map/egz,egc->gzc/dot_general | solution.py:547
  8.5 111.7 %shard_map.104 = (f32[16,128,128]{2,1,0:T(8,128)}, bf16[128,2,8,128]{3,2,1,0:T(8,128)(2,1)}, bf16[16,128,128]{2,1,0:T(8,128)(2,1)}) custom-call(f32[16,1]{1,0:T(8,128)} %get-tuple-element.13.fall_ref, f32[16,128,128]{2,1,0:T(8,128)} %get-tuple-element.15.state_ref, bf16[16,128,128]{2,1,0:T(8,128)(2,1)} %get-tuple-element.14.sent0_ref, ...), custom_call_target="tpu_custom_call" | custom-call | tf_op jit(solution)/shard_map/pallas_call | solution.py:395
  120.3 0.0 copy-start.2
  120.3 2.2 %copy.26 = bf16[128,16,128]{2,1,0:T(8,128)(2,1)} copy(bf16[128,16,128]{2,0,1:T(8,128)(2,1)} %bitcast.15) | data formatting | bytes 1048576
  122.5 0.0 copy-done.2
  122.5 0.8 copy.43
  (2 shorter events, 0.0 us)
Async XLA Ops:
  0.6 5.0 %copy-start.1 = (bf16[128,16,128]{2,1,0:T(8,128)(2,1)S(1)}, bf16[128,16,128]{2,1,0:T(8,128)(2,1)}, u32[]{:S(2)}) copy-start(bf16[128,16,128]{2,1,0:T(8,128)(2,1)} %lk_ref.1) | copy-start | bytes 1572868
  2.4 0.8 copy-start.3
  5.7 1.0 copy-start
  120.3 2.2 %copy-start.2 = (bf16[128,2,8,128]{3,2,1,0:T(8,128)(2,1)S(1)}, bf16[128,2,8,128]{3,2,1,0:T(8,128)(2,1)}, u32[]{:S(2)}) copy-start(bf16[128,2,8,128]{3,2,1,0:T(8,128)(2,1)} %get-tuple-element.5) | copy-start | bytes 1572868

commit v18 on v17

--- a/solution.py
+++ b/solution.py
@@ -20,7 +20,6 @@
     reach,
     fall_ref,
     state_ref,
-    sent0_ref,
     kv_ref,
     q_ref,
     bias_ref,
@@ -132,18 +131,19 @@
 
     fall = jnp.broadcast_to(fall_ref[...], whole_fall.shape)
     outgoing_fall[0] = fall
+    outgoing[0] = state_ref[...].astype(jnp.bfloat16)
 
     @pl.when(ahead(1) == 1)
     def _():
         fall_copy(0, outgoing_fall.at[0], me + 1).start()
         for c in range(chunks):
-            state_copy(0, sent0_ref, c, me + 1).start()
+            state_copy(0, outgoing.at[0], c, me + 1).start()
 
     @pl.when(behind(1) == 1)
     def _():
         fall_copy(back0, outgoing_fall.at[0], me - 1).start()
         for c in range(chunks):
-            state_copy(back0, sent0_ref, c, me - 1).start()
+            state_copy(back0, outgoing.at[0], c, me - 1).start()
 
     whole[...] = state_ref[...]
     whole_fall[...] = fall
@@ -399,7 +399,7 @@
             jax.ShapeDtypeStruct(queries.shape, queries.dtype),
             jax.ShapeDtypeStruct(state.shape, jnp.bfloat16),
         ),
-        in_specs=[vmem] * 11,
+        in_specs=[vmem] * 10,
         out_specs=(vmem, vmem, vmem),
         scratch_shapes=[
             pltpu.VMEM(state.shape, jnp.float32),
@@ -424,7 +424,7 @@
             pltpu.VMEM(state.shape, jnp.float32),
         ],
         compiler_params=pltpu.CompilerParams(collective_id=0, has_side_effects=True),
-    )(fall_rows, state, state.astype(jnp.bfloat16), kv, queries, bias, lq, lk, lv, cum, gain)
+    )(fall_rows, state, kv, queries, bias, lq, lk, lv, cum, gain)
 
 
 def head_sum_kernel(count, value_ref, out_ref, slots, send_sem, recv_sem):

time: 125 us -> 125 us (level)
  no operation moved by 1% of the time
where the time goes in v18:
time: 125 us; the launch traced here: 123 us
  Pallas kernels  112 us (90%)
  local copies, waits for them, and re-layouts  5.52 us (4%)
  other arithmetic  2.83 us (2%)
  matrix products  1.67 us (1%)
  between operations  1.4 us (1%)
    pallas_call x1, Pallas kernels, exclusive_scan(): pl.pallas_call(functools.partial(scan_kernel, rounds, chunks, REACH), out...  112 us
    unnamed x10, local copies, waits for them, and re-layouts  3.74 us

profile of v18, /device:TPU:60, one launch (start us, length us, event | category | flops | bytes accessed | tf_op | source)
XLA Modules:
  0.0 123.0 jit_solution(5814149042667669473)
XLA Ops:
  0.6 0.0 copy-start.1
  1.4 1.0 reduce_window_sum.11.cum_ref
  2.4 0.0 copy-start.3
  2.4 0.8 slice_reduce_fusion
  3.1 0.0 copy-done.3
  3.1 0.1 exponential_bitcast_fusion
  3.2 0.1 copy.19
  3.3 0.9 copy_bitcast_fusion
  4.2 0.7 maximum_bitcast_fusion.kv_ref
  4.9 0.8 fusion.8.bias_ref
  5.7 0.0 copy-done.1
  5.7 0.0 copy-start
  5.7 0.3 subtract_convert_fusion
  6.0 0.7 copy-done
  6.7 0.3 fusion.2
  7.1 1.3 %convolution_add_fusion.state_ref = f32[16,128,128]{2,1,0:T(8,128)} fusion(f32[16,128,128]{2,1,0:T(8,128)S(1)} %fusion.2, bf16[128,16,128]{2,1,0:T(8,128)(2,1)S(1)} %get-tuple-element.10, bf16[128,16,128]{2,1,0:T(8,128)(2,1)S(1)} %copy-done), kind=kOutput, calls=%fused_computation | convolution fusion | flops 67371008 | bytes 3145728 | tf_op jit(solution)/shard_map/egz,egc->gzc/dot_general | solution.py:547
  8.4 111.5 %shard_map.104 = (f32[16,128,128]{2,1,0:T(8,128)}, bf16[128,2,8,128]{3,2,1,0:T(8,128)(2,1)}, bf16[16,128,128]{2,1,0:T(8,128)(2,1)}) custom-call(f32[16,1]{1,0:T(8,128)} %get-tuple-element.13.fall_ref, f32[16,128,128]{2,1,0:T(8,128)} %convolution_add_fusion.state_ref, bf16[2,2,128,128]{3,2,1,0:T(8,128)(2,1)} %maximum_bitcast_fusion.kv_ref, ...), custom_call_target="tpu_custom_call" | custom-call | tf_op jit(solution)/shard_map/pallas_call | solution.py:395
  119.9 0.0 copy-start.2
  119.9 2.2 %copy.26 = bf16[128,16,128]{2,1,0:T(8,128)(2,1)} copy(bf16[128,16,128]{2,0,1:T(8,128)(2,1)} %bitcast.14) | data formatting | bytes 1048576
  122.2 0.0 copy-done.2
  122.2 0.8 copy.39
  (2 shorter events, 0.0 us)
Async XLA Ops:
  0.6 5.0 %copy-start.1 = (bf16[128,16,128]{2,1,0:T(8,128)(2,1)S(1)}, bf16[128,16,128]{2,1,0:T(8,128)(2,1)}, u32[]{:S(2)}) copy-start(bf16[128,16,128]{2,1,0:T(8,128)(2,1)} %lk_ref.1) | copy-start | bytes 1572868
  2.4 0.8 copy-start.3
  5.7 1.0 copy-start
  119.9 2.2 %copy-start.2 = (bf16[128,2,8,128]{3,2,1,0:T(8,128)(2,1)S(1)}, bf16[128,2,8,128]{3,2,1,0:T(8,128)(2,1)}, u32[]{:S(2)}) copy-start(bf16[128,2,8,128]{3,2,1,0:T(8,128)(2,1)} %get-tuple-element.5) | copy-start | bytes 1572868
